TPU v7x, 32 devices: a whole 2x2x4 slice. The times are simulated.
32 devices in a mesh: dp: 16 (over z, x, core), ctx: 2 (over y).
Axes of the slice: x: 2, y: 2, z: 4, core: 2. Of those that a mesh axis runs over, the one named last changes fastest.
Arguments:
- tokens: bfloat16 [32768, 1024], P(('dp', 'ctx')), may hold values from -6 to 6
- cotangent: bfloat16 [32768, 1024], P(('dp', 'ctx')), may hold values from -6 to 6
- pair_order: int32 [16, 2], P('dp'), may hold values from 0 to 1, each once within a row
- qkv_weight: float32 [1024, 3072], P(('dp', 'ctx')), may hold values from -0.1875 to 0.1875
- qkv_momentum: float32 [1024, 3072], P(('dp', 'ctx')), may hold values from -0.03125 to 0.03125
- qkv_average: float32 [1024, 3072], P(('dp', 'ctx')), may hold values from -0.1875 to 0.1875
- out_weight: float32 [1024, 1024], P(('dp', 'ctx')), may hold values from -0.1875 to 0.1875
- out_momentum: float32 [1024, 1024], P(('dp', 'ctx')), may hold values from -0.03125 to 0.03125
- out_average: float32 [1024, 1024], P(('dp', 'ctx')), may hold values from -0.1875 to 0.1875
- up_weight: float32 [1024, 4096], P(('dp', 'ctx')), may hold values from -0.1875 to 0.1875
- up_momentum: float32 [1024, 4096], P(('dp', 'ctx')), may hold values from -0.03125 to 0.03125
- up_average: float32 [1024, 4096], P(('dp', 'ctx')), may hold values from -0.1875 to 0.1875
- down_weight: float32 [4096, 1024], P(('dp', 'ctx')), may hold values from -0.09375 to 0.09375
- down_momentum: float32 [4096, 1024], P(('dp', 'ctx')), may hold values from -0.03125 to 0.03125
- down_average: float32 [4096, 1024], P(('dp', 'ctx')), may hold values from -0.09375 to 0.09375
- norm_weight: float32 [8, 1024], P(None, ('dp', 'ctx')), may hold values from -1.2 to 1.45
- norm_momentum: float32 [8, 1024], P(None, ('dp', 'ctx')), may hold values from -0.03125 to 0.03125
- norm_average: float32 [8, 1024], P(None, ('dp', 'ctx')), may hold values from -1.2 to 1.45
Outputs:
- output: bfloat16 [32768, 1024], P(('dp', 'ctx'))
- input_grad: bfloat16 [32768, 1024], P(('dp', 'ctx'))
- qkv_momentum_new: float32 [1024, 3072], P(('dp', 'ctx'))
- qkv_weight_new: float32 [1024, 3072], P(('dp', 'ctx'))
- qkv_average_new: float32 [1024, 3072], P(('dp', 'ctx'))
- out_momentum_new: float32 [1024, 1024], P(('dp', 'ctx'))
- out_weight_new: float32 [1024, 1024], P(('dp', 'ctx'))
- out_average_new: float32 [1024, 1024], P(('dp', 'ctx'))
- up_momentum_new: float32 [1024, 4096], P(('dp', 'ctx'))
- up_weight_new: float32 [1024, 4096], P(('dp', 'ctx'))
- up_average_new: float32 [1024, 4096], P(('dp', 'ctx'))
- down_momentum_new: float32 [4096, 1024], P(('dp', 'ctx'))
- down_weight_new: float32 [4096, 1024], P(('dp', 'ctx'))
- down_average_new: float32 [4096, 1024], P(('dp', 'ctx'))
- norm_momentum_new: float32 [8, 1024], P(None, ('dp', 'ctx'))
- norm_weight_new: float32 [8, 1024], P(None, ('dp', 'ctx'))
- norm_average_new: float32 [8, 1024], P(None, ('dp', 'ctx'))
Inputs may be any that keep to these rules, and one draw needn't show every extreme that they name: `pair_order`: each row holds every pair number once.
All inputs are finite; a program needn't handle non-finite values.
Results may differ from a plain program's by a relative error of at most 0.01.
Values may be sent and summed in bfloat16 or wider, within the bound.
No kernel may reach another device: no remote copies, remote signals or barrier semaphores. Data moves between devices by JAX's collectives and lax.ppermute only.
A program may use at most 320 MiB of HBM per device.

v0:
```python
import math

import jax
import jax.numpy as jnp
from jax import lax
from jax.sharding import PartitionSpec as P

HEADS = 16
HEAD_DIM = 64


rate_qkv = 0.04
rate_out = 0.03
rate_up = 0.03
rate_down = 0.02
rate_norm = 0.3
group_heads = 4


def layer_norm(values, gain_row, shift_row):
    centre = values - jnp.mean(values, axis=-1, keepdims=True)
    spread = jnp.mean(centre * centre, axis=-1, keepdims=True)
    return centre * lax.rsqrt(spread + 1e-05) * gain_row + shift_row


def rotary_tables(positions):
    half_dim = HEAD_DIM // 2
    frequency = jnp.exp(jnp.arange(half_dim, dtype=jnp.float32) * (-math.log(10000.0) / half_dim))
    angles = positions.astype(jnp.float32)[:, None] * frequency[None, :]
    angles = jnp.concatenate([angles, angles], axis=1)
    return (jnp.cos(angles), jnp.sin(angles))


def rotary(values, cos_table, sin_table):
    shaped = values.reshape(values.shape[0], HEADS, HEAD_DIM)
    half_dim = HEAD_DIM // 2
    turned = jnp.concatenate([-shaped[:, :, half_dim:], shaped[:, :, :half_dim]], axis=2)
    result = shaped * cos_table[:, None, :] + turned * sin_table[:, None, :]
    return result.reshape(values.shape)


def split_heads(values):
    count = values.shape[0]
    return values.reshape(count, HEADS // group_heads, group_heads, HEAD_DIM).transpose(1, 0, 2, 3)


def join_heads(values):
    count = values.shape[1]
    return values.transpose(1, 0, 2, 3).reshape(count, HEADS, HEAD_DIM)


def masked_scores(query_block, key_heads, query_place, key_place):
    score_scale = 1.0 / math.sqrt(HEAD_DIM)
    scores = (
        jnp.einsum("qhe,khe->hqk", query_block, key_heads, preferred_element_type=jnp.float32)
        * score_scale
    )
    allowed = key_place[None, :] <= query_place[:, None]
    return jnp.where(allowed[None], scores, -jnp.inf)


def attend_forward(block_items):
    query_blocks, query_places, key_rows, value_rows, key_place = block_items
    key_groups = split_heads(key_rows.reshape(key_rows.shape[0], HEADS, HEAD_DIM))
    value_groups = split_heads(value_rows.reshape(value_rows.shape[0], HEADS, HEAD_DIM))
    mixed_list = []
    total_list = []
    for half_index in range(2):
        query_place = query_places[half_index]

        def one_group(group_items):
            query_group, key_group, value_group = group_items
            scores = masked_scores(query_group, key_group, query_place, key_place)
            row_top = jnp.max(scores, axis=2, keepdims=True)
            weights = jnp.exp(scores - row_top)
            row_total = jnp.sum(weights, axis=2, keepdims=True)
            prob_low = (weights / row_total).astype(jnp.bfloat16)
            mixed = jnp.einsum(
                "hqk,khe->qhe", prob_low, value_group, preferred_element_type=jnp.float32
            )
            return (mixed, row_top + jnp.log(row_total))

        mixed_groups, total_groups = lax.map(
            one_group, (split_heads(query_blocks[half_index]), key_groups, value_groups)
        )
        mixed_list.append(join_heads(mixed_groups))
        total_list.append(total_groups.reshape(HEADS, query_place.shape[0], 1))
    return (jnp.stack(mixed_list), jnp.stack(total_list))


def attend_backward(block_items):
    query_blocks, query_places, key_rows, value_rows, key_place, log_totals, grad_blocks = (
        block_items
    )
    score_scale = 1.0 / math.sqrt(HEAD_DIM)
    key_groups = split_heads(key_rows.reshape(key_rows.shape[0], HEADS, HEAD_DIM))
    value_groups = split_heads(value_rows.reshape(value_rows.shape[0], HEADS, HEAD_DIM))
    key_accum = jnp.zeros(key_groups.shape, jnp.float32)
    value_accum = jnp.zeros(value_groups.shape, jnp.float32)
    query_list = []
    for half_index in range(2):
        query_place = query_places[half_index]
        total_groups = log_totals[half_index].reshape(
            HEADS // group_heads, group_heads, query_place.shape[0], 1
        )

        def one_group(group_items):
            query_group, key_group, value_group, total_group, grad_group = group_items
            scores = masked_scores(query_group, key_group, query_place, key_place)
            prob_full = jnp.exp(scores - total_group)
            prob_low = prob_full.astype(jnp.bfloat16)
            grad_probs = jnp.einsum(
                "qhe,khe->hqk", grad_group, value_group, preferred_element_type=jnp.float32
            )
            inner_sum = jnp.sum(prob_full * grad_probs, axis=2, keepdims=True)
            grad_scores = (prob_full * (grad_probs - inner_sum)).astype(jnp.bfloat16)
            query_part = (
                jnp.einsum(
                    "hqk,khe->qhe", grad_scores, key_group, preferred_element_type=jnp.float32
                )
                * score_scale
            )
            key_part = (
                jnp.einsum(
                    "hqk,qhe->khe", grad_scores, query_group, preferred_element_type=jnp.float32
                )
                * score_scale
            )
            value_part = jnp.einsum(
                "hqk,qhe->khe", prob_low, grad_group, preferred_element_type=jnp.float32
            )
            return (query_part, key_part, value_part)

        query_groups, key_parts, value_parts = lax.map(
            one_group,
            (
                split_heads(query_blocks[half_index]),
                key_groups,
                value_groups,
                total_groups,
                split_heads(grad_blocks[half_index]),
            ),
        )
        query_list.append(join_heads(query_groups))
        key_accum = key_accum + key_parts
        value_accum = value_accum + value_parts
    return (jnp.stack(query_list), join_heads(key_accum), join_heads(value_accum))


def nesterov(gradient, momentum, weight, average, step_rate, token_total):
    scaled = gradient / token_total
    new_momentum = 0.5 * momentum + scaled
    new_weight = weight - step_rate * math.sqrt(token_total) * (scaled + 0.5 * new_momentum)
    new_average = 0.5 * average + 0.5 * new_weight
    return (new_momentum, new_weight, new_average)


def per_device(
    tokens,
    cotangent,
    pair_order,
    qkv_weight,
    qkv_momentum,
    qkv_average,
    out_weight,
    out_momentum,
    out_average,
    up_weight,
    up_momentum,
    up_average,
    down_weight,
    down_momentum,
    down_average,
    norm_weight,
    norm_momentum,
    norm_average,
):
    ctx_count = lax.axis_size("ctx")
    ctx_index = lax.axis_index("ctx")
    token_count = tokens.shape[0]
    model_width = tokens.shape[1]
    seq_count = pair_order.shape[0]
    local_len = token_count // seq_count
    span_len = local_len // 2
    token_total = token_count * lax.axis_size("dp") * ctx_count
    gathered = (
        lax.all_gather(qkv_weight.astype(jnp.bfloat16), ("dp", "ctx"), axis=0, tiled=True),
        lax.all_gather(out_weight.astype(jnp.bfloat16), ("dp", "ctx"), axis=0, tiled=True),
        lax.all_gather(up_weight.astype(jnp.bfloat16), ("dp", "ctx"), axis=0, tiled=True),
        lax.all_gather(down_weight.astype(jnp.bfloat16), ("dp", "ctx"), axis=0, tiled=True),
        lax.all_gather(norm_weight.astype(jnp.bfloat16), ("dp", "ctx"), axis=1, tiled=True),
    )
    w_qkv, w_out, w_up, w_down, norm_low = gathered
    norm_vals = norm_low.astype(jnp.float32)
    halves = jnp.arange(2, dtype=jnp.int32)
    span_ids = jnp.where(
        halves[None, None, :] == 0,
        pair_order[:, :, None],
        2 * ctx_count - 1 - pair_order[:, :, None],
    )
    key_place = (
        span_ids[:, :, :, None] * span_len
        + jnp.arange(span_len, dtype=jnp.int32)[None, None, None, :]
    ).reshape(seq_count, ctx_count * local_len)
    query_place = lax.dynamic_slice_in_dim(key_place, ctx_index * local_len, local_len, 1)
    cos_table, sin_table = rotary_tables(query_place.reshape(token_count))
    token_vals = tokens.astype(jnp.float32)
    normed_in, pull_one = jax.vjp(layer_norm, token_vals, norm_vals[0], norm_vals[1])
    attn_in = normed_in.astype(jnp.bfloat16)
    qkv_rows = jnp.dot(attn_in, w_qkv, preferred_element_type=jnp.float32)
    queries = rotary(qkv_rows[:, :model_width], cos_table, sin_table).astype(jnp.bfloat16)
    keys_local = rotary(qkv_rows[:, model_width : 2 * model_width], cos_table, sin_table).astype(
        jnp.bfloat16
    )
    values_local = qkv_rows[:, 2 * model_width :].astype(jnp.bfloat16)
    keys_all, values_all = (
        lax.all_gather(
            keys_local.reshape(seq_count, local_len, model_width), "ctx", axis=1, tiled=True
        ),
        lax.all_gather(
            values_local.reshape(seq_count, local_len, model_width), "ctx", axis=1, tiled=True
        ),
    )
    query_blocks = queries.reshape(seq_count, 2, span_len, HEADS, HEAD_DIM)
    query_places = query_place.reshape(seq_count, 2, span_len)
    mixed_all, log_totals = lax.map(
        attend_forward, (query_blocks, query_places, keys_all, values_all, key_place)
    )
    attn_vals = mixed_all.reshape(token_count, model_width).astype(jnp.bfloat16)
    projected = jnp.dot(attn_vals, w_out, preferred_element_type=jnp.float32)
    branch_one, pull_two = jax.vjp(layer_norm, projected, norm_vals[2], norm_vals[3])
    hidden = token_vals + branch_one
    normed_mlp, pull_three = jax.vjp(layer_norm, hidden, norm_vals[4], norm_vals[5])
    mlp_in = normed_mlp.astype(jnp.bfloat16)
    up_rows = jnp.dot(mlp_in, w_up, preferred_element_type=jnp.float32)
    active_full, pull_gelu = jax.vjp(jax.nn.gelu, up_rows)
    active = active_full.astype(jnp.bfloat16)
    down_rows = jnp.dot(active, w_down, preferred_element_type=jnp.float32)
    branch_two, pull_four = jax.vjp(layer_norm, down_rows, norm_vals[6], norm_vals[7])
    output = (hidden + branch_two).astype(jnp.bfloat16)
    grad_out = cotangent.astype(jnp.float32)
    grad_down_rows, grad_gain_four, grad_shift_four = pull_four(grad_out)
    grad_down_low = grad_down_rows.astype(jnp.bfloat16)
    down_grad = jnp.einsum("tf,td->fd", active, grad_down_low, preferred_element_type=jnp.float32)
    grad_active = jnp.einsum("td,fd->tf", grad_down_low, w_down, preferred_element_type=jnp.float32)
    grad_up_low = pull_gelu(grad_active)[0].astype(jnp.bfloat16)
    up_grad = jnp.einsum("tc,tf->cf", mlp_in, grad_up_low, preferred_element_type=jnp.float32)
    grad_mlp_in = jnp.einsum("tf,cf->tc", grad_up_low, w_up, preferred_element_type=jnp.float32)
    grad_hidden_part, grad_gain_three, grad_shift_three = pull_three(grad_mlp_in)
    grad_hidden = grad_out + grad_hidden_part
    grad_projected, grad_gain_two, grad_shift_two = pull_two(grad_hidden)
    grad_proj_low = grad_projected.astype(jnp.bfloat16)
    out_grad = jnp.einsum("tc,td->cd", attn_vals, grad_proj_low, preferred_element_type=jnp.float32)
    grad_mixed = jnp.einsum(
        "td,cd->tc", grad_proj_low, w_out, preferred_element_type=jnp.float32
    ).astype(jnp.bfloat16)
    grad_blocks = grad_mixed.reshape(seq_count, 2, span_len, HEADS, HEAD_DIM)
    grad_query_all, key_accum_all, value_accum_all = lax.map(
        attend_backward,
        (query_blocks, query_places, keys_all, values_all, key_place, log_totals, grad_blocks),
    )
    key_grads, value_grads = (
        lax.psum_scatter(
            key_accum_all.reshape(seq_count, ctx_count * local_len, model_width).astype(
                jnp.bfloat16
            ),
            "ctx",
            scatter_dimension=1,
            tiled=True,
        ).astype(jnp.float32),
        lax.psum_scatter(
            value_accum_all.reshape(seq_count, ctx_count * local_len, model_width).astype(
                jnp.bfloat16
            ),
            "ctx",
            scatter_dimension=1,
            tiled=True,
        ).astype(jnp.float32),
    )
    grad_query_pre = rotary(grad_query_all.reshape(token_count, model_width), cos_table, -sin_table)
    grad_key_pre = rotary(key_grads.reshape(token_count, model_width), cos_table, -sin_table)
    grad_qkv = jnp.concatenate(
        [grad_query_pre, grad_key_pre, value_grads.reshape(token_count, model_width)], axis=1
    ).astype(jnp.bfloat16)
    qkv_grad = jnp.einsum("tc,tf->cf", attn_in, grad_qkv, preferred_element_type=jnp.float32)
    grad_attn_in = jnp.einsum("tf,cf->tc", grad_qkv, w_qkv, preferred_element_type=jnp.float32)
    grad_token_part, grad_gain_one, grad_shift_one = pull_one(grad_attn_in)
    input_grad = (grad_hidden + grad_token_part).astype(jnp.bfloat16)
    norm_grad = jnp.stack(
        [
            grad_gain_one,
            grad_shift_one,
            grad_gain_two,
            grad_shift_two,
            grad_gain_three,
            grad_shift_three,
            grad_gain_four,
            grad_shift_four,
        ]
    )
    summed = (
        lax.psum_scatter(qkv_grad, ("dp", "ctx"), scatter_dimension=0, tiled=True),
        lax.psum_scatter(out_grad, ("dp", "ctx"), scatter_dimension=0, tiled=True),
        lax.psum_scatter(up_grad, ("dp", "ctx"), scatter_dimension=0, tiled=True),
        lax.psum_scatter(down_grad, ("dp", "ctx"), scatter_dimension=0, tiled=True),
        lax.psum_scatter(norm_grad, ("dp", "ctx"), scatter_dimension=1, tiled=True),
    )
    qkv_new = nesterov(summed[0], qkv_momentum, qkv_weight, qkv_average, rate_qkv, token_total)
    out_new = nesterov(summed[1], out_momentum, out_weight, out_average, rate_out, token_total)
    up_new = nesterov(summed[2], up_momentum, up_weight, up_average, rate_up, token_total)
    down_new = nesterov(summed[3], down_momentum, down_weight, down_average, rate_down, token_total)
    norm_new = nesterov(summed[4], norm_momentum, norm_weight, norm_average, rate_norm, token_total)
    return (
        output,
        input_grad,
        qkv_new[0],
        qkv_new[1],
        qkv_new[2],
        out_new[0],
        out_new[1],
        out_new[2],
        up_new[0],
        up_new[1],
        up_new[2],
        down_new[0],
        down_new[1],
        down_new[2],
        norm_new[0],
        norm_new[1],
        norm_new[2],
    )


def solution(mesh):
    placed = (
        P(("dp", "ctx"), None),
        P(("dp", "ctx"), None),
        P("dp", None),
        P(("dp", "ctx"), None),
        P(("dp", "ctx"), None),
        P(("dp", "ctx"), None),
        P(("dp", "ctx"), None),
        P(("dp", "ctx"), None),
        P(("dp", "ctx"), None),
        P(("dp", "ctx"), None),
        P(("dp", "ctx"), None),
        P(("dp", "ctx"), None),
        P(("dp", "ctx"), None),
        P(("dp", "ctx"), None),
        P(("dp", "ctx"), None),
        P(None, ("dp", "ctx")),
        P(None, ("dp", "ctx")),
        P(None, ("dp", "ctx")),
    )
    return jax.shard_map(
        per_device,
        mesh=mesh,
        in_specs=placed,
        out_specs=(
            P(("dp", "ctx"), None),
            P(("dp", "ctx"), None),
            P(("dp", "ctx"), None),
            P(("dp", "ctx"), None),
            P(("dp", "ctx"), None),
            P(("dp", "ctx"), None),
            P(("dp", "ctx"), None),
            P(("dp", "ctx"), None),
            P(("dp", "ctx"), None),
            P(("dp", "ctx"), None),
            P(("dp", "ctx"), None),
            P(("dp", "ctx"), None),
            P(("dp", "ctx"), None),
            P(("dp", "ctx"), None),
            P(None, ("dp", "ctx")),
            P(None, ("dp", "ctx")),
            P(None, ("dp", "ctx")),
        ),
        check_vma=False,
    )
```

profile of v0, /device:TPU:1, one launch (start us, length us, event | category | flops | bytes accessed | tf_op | source)
XLA Modules:
  0.0 2225.0 jit_solution(5330858355117442927)
XLA Ops:
  9.7 67.8 %all-gather.2 = bf16[32,32,8]{1,2,0:T(8,128)(2,1)S(1)} all-gather(bf16[1,32,8]{1,2,0:T(8,128)(2,1)S(1)} %convert_bitcast_fusion), channel_id=1, replica_groups=mesh['dp'=16,'ctx'=2] {'dp','ctx'}, dimensions={0}, use_global_device_ids=true | all-gather | bytes 16896 | tf_op jit(solution)/shard_map/all_gather | solution.py:191
  180.1 35.5 %all-gather.20.cloned.1.call-done = bf16[2048,1024]{1,0:T(8,128)(2,1)} async-done(((bf16[1024,1024]{1,0:T(8,128)(2,1)}), bf16[2048,1024]{1,0:T(8,128)(2,1)}) %all-gather.20.cloned.1.call-update) | async-done | bytes 4194320 | tf_op jit(solution)/shard_map/all_gather | solution.py:217
  222.2 63.3 %while.85 = (s32[]{:T(128)}, bf16[4,512,4,64]{1,3,2,0:T(8,128)(2,1)S(1)}, f32[4,4,512,1]{2,1,3,0:T(4,128)S(1)}, bf16[4,2048,4,64]{1,3,2,0:T(8,128)(2,1)}, s32[1,...) while((s32[]{:T(128)}, ...), condition=%wide.region_5.6_spmd.clone, body=%wide.region_2.5_spmd.clone.sunk | while | flops 1125122048 | bytes 57512056 | solution.py:83
  288.8 63.7 %while.86 = (s32[]{:T(128)}, bf16[4,512,4,64]{1,3,2,0:T(8,128)(2,1)S(1)}, f32[4,4,512,1]{2,1,3,0:T(4,128)S(1)}, bf16[4,2048,4,64]{1,3,2,0:T(8,128)(2,1)}, s32[1,...) while((s32[]{:T(128)}, ...), condition=%wide.region_9.10_spmd.clone, body=%wide.region_6.9_spmd.clone.sunk | while | flops 1125122048 | bytes 57512056 | solution.py:83
  371.5 16.9 fusion.158
  388.4 47.4 %all-gather.16.cloned.1.call-done = bf16[4096,1024]{1,0:T(8,128)(2,1)} async-done(((bf16[128,1024]{1,0:T(8,128)(2,1)}), bf16[4096,1024]{1,0:T(8,128)(2,1)}) %all-gather.16.cloned.1.call-update) | async-done | bytes 8388624 | tf_op jit(solution)/shard_map/all_gather | solution.py:190
  435.8 16.8 fusion.169
  463.2 28.1 %fusion.120 = bf16[1024,4096]{1,0:T(8,128)(2,1)} fusion(f32[1024,4096]{1,0:T(8,128)} %fusion.158, bf16[4096,1024]{1,0:T(8,128)(2,1)} %all-gather.16.cloned.1.call-done, f32[1024]{0:T(1024)S(1)} %negate_multiply_fusion.3, bf16[1024,1024]{0,1:T(8,128)(2,1)S(1)} %copy-done.13, f32[1024,1024]{0,1:T(8,128)S(1)} %copy-done.16, f32[1024]{0:T(1024)S(1)} %get-tuple-element.579, ...), kind=kOutput, calls=%fused_computation.136 | convolution fusion | flops 8683257856 | bytes 39866368 | tf_op jit(solution)/shard_map/td,fd->tf/dot_general | solution.py:245
  491.3 15.9 fusion.171
  541.5 195.0 %while.87 = (s32[]{:T(128)}, f32[4,512,4,64]{1,3,2,0:T(8,128)S(1)}, f32[4,2048,4,64]{1,3,2,0:T(8,128)}, f32[4,2048,4,64]{1,3,2,0:T(8,128)}, bf16[4,2048,4,64]{1,...) while((s32[]{:T(128)}, f32[4,512,4,64]{1,3,2,0:T(8,128)S(1)}, ...), condition=%wide.region_24.25_spmd.clone, body=%wide.region_22.24_spmd.clone.sunk | while | flops 2748973056 | bytes 210336976 | solution.py:134
  558.8 12.8 multiply_reduce_fusion.11
  607.5 12.8 multiply_reduce_fusion.11
  704.8 12.8 multiply_reduce_fusion.11
  746.8 195.1 %while.88 = (s32[]{:T(128)}, f32[4,512,4,64]{1,3,2,0:T(8,128)S(1)}, f32[4,2048,4,64]{1,3,2,0:T(8,128)}, f32[4,2048,4,64]{1,3,2,0:T(8,128)}, bf16[4,2048,4,64]{1,...) while((s32[]{:T(128)}, f32[4,512,4,64]{1,3,2,0:T(8,128)S(1)}, ...), condition=%wide.region_27.28_spmd.clone, body=%wide.region_25.27_spmd.clone.sunk | while | flops 2748973056 | bytes 210336976 | solution.py:134
  812.5 12.8 multiply_reduce_fusion.12
  1020.2 40.4 %reduce-scatter.12.cloned.1.call-done = bf16[1,1024,1024]{1,2,0:T(8,128)(2,1)} async-done(((bf16[1,2048,1024]{1,2,0:T(8,128)(2,1)}), bf16[1,1024,1024]{1,2,0:T(8,128)(2,1)}) %reduce-scatter.12.cloned.1.call-update) | async-done | bytes 2097168 | tf_op jit(solution)/shard_map/reduce_scatter | solution.py:271
  1085.3 14.3 fusion.138
  1100.3 21.3 fusion.140
  1122.3 17.0 fusion.157
  1153.6 49.1 %reduce-scatter.16.cloned.1.call-done = f32[32,1024]{1,0:T(8,128)} async-done(((f32[1024,1024]{1,0:T(8,128)}), f32[32,1024]{1,0:T(8,128)}) %reduce-scatter.16.cloned.1.call-update) | async-done | bytes 131088 | tf_op jit(solution)/shard_map/reduce_scatter | solution.py:303
  1204.5 131.2 %reduce-scatter.22.cloned.1.call-done = f32[32,8]{1,0:T(8,128)} async-done(((f32[1024,8]{1,0:T(8,128)}), f32[32,8]{1,0:T(8,128)}) %reduce-scatter.22.cloned.1.call-update) | async-done | bytes 1040
  1337.1 158.8 %reduce-scatter.14.cloned.1.call-done = f32[32,3072]{1,0:T(8,128)} async-done(((f32[1024,3072]{1,0:T(8,128)}), f32[32,3072]{1,0:T(8,128)}) %reduce-scatter.14.cloned.1.call-update) | async-done | bytes 393232 | tf_op jit(solution)/shard_map/reduce_scatter | solution.py:302
  1498.2 356.9 %reduce-scatter.20.cloned.1.call-done = f32[128,1024]{1,0:T(8,128)} async-done(((f32[4096,1024]{1,0:T(8,128)}), f32[128,1024]{1,0:T(8,128)}) %reduce-scatter.20.cloned.1.call-update) | async-done | bytes 524304 | tf_op jit(solution)/shard_map/reduce_scatter | solution.py:305
  1857.4 358.4 %reduce-scatter.18.cloned.1.call-done = f32[32,4096]{1,0:T(8,128)} async-done(((f32[1024,4096]{1,0:T(8,128)}), f32[32,4096]{1,0:T(8,128)}) %reduce-scatter.18.cloned.1.call-update) | async-done | bytes 524304 | tf_op jit(solution)/shard_map/reduce_scatter | solution.py:304
  (484 shorter events, 781.3 us)
Async XLA Ops:
  7.2 76.4 %all-gather.10.cloned.1.call-start = ((), (), s32[]{:S(2)}) async-start(), calls=%async_computation.7 | async-start | bytes 6488064 | tf_op jit(solution)/shard_map/all_gather | solution.py:187
  9.0 164.6 %all-gather.18.cloned.1.call-start = ((), (), s32[]{:S(2)}) async-start(), calls=%async_computation.17 | async-start | bytes 6291456 | tf_op jit(solution)/shard_map/all_gather | solution.py:220
  99.4 116.2 %all-gather.20.cloned.1.call-start = ((), (), s32[]{:S(2)}) async-start(), calls=%async_computation.18 | async-start | bytes 6291456 | tf_op jit(solution)/shard_map/all_gather | solution.py:217
  160.1 199.7 %all-gather.12.cloned.1.call-start = ((), (), s32[]{:S(2)}) async-start(), calls=%async_computation.8 | async-start | bytes 2162688 | tf_op jit(solution)/shard_map/all_gather | solution.py:188
  160.8 210.7 %all-gather.14.cloned.1.call-start = ((), (), s32[]{:S(2)}) async-start(), calls=%async_computation.9 | async-start | bytes 8650752 | tf_op jit(solution)/shard_map/all_gather | solution.py:189
  161.6 274.2 %all-gather.16.cloned.1.call-start = ((), (), s32[]{:S(2)}) async-start(), calls=%async_computation.10 | async-start | bytes 8650752 | tf_op jit(solution)/shard_map/all_gather | solution.py:190
  162.4 841.5 %reduce-scatter.10.cloned.1.call-start = ((), (), s32[]{:S(2)}) async-start(), calls=%async_computation.11 | async-start | bytes 6291456 | tf_op jit(solution)/shard_map/reduce_scatter | solution.py:263
  369.0 152.1 %copy-start.50 = (f32[1024]{0:T(1024)}, f32[1024]{0:T(1024)S(1)}, u32[]{:S(2)}) copy-start(f32[1024]{0:T(1024)S(1)} %broadcast_multiply_fusion.2) | copy-start | bytes 12292
  951.3 109.4 %reduce-scatter.12.cloned.1.call-start = ((), (), s32[]{:S(2)}) async-start(), calls=%async_computation.12 | async-start | bytes 6291456 | tf_op jit(solution)/shard_map/reduce_scatter | solution.py:271
  961.3 241.4 %reduce-scatter.16.cloned.1.call-start = ((), (), s32[]{:S(2)}) async-start(), calls=%async_computation.14 | async-start | bytes 4325376 | tf_op jit(solution)/shard_map/reduce_scatter | solution.py:303
  969.1 366.6 %reduce-scatter.22.cloned.1.call-start = ((), (), s32[]{:S(2)}) async-start(), calls=%async_computation.19 | async-start | bytes 540672
  1085.2 410.6 %reduce-scatter.14.cloned.1.call-start = ((), (), s32[]{:S(2)}) async-start(), calls=%async_computation.13 | async-start | bytes 12976128 | tf_op jit(solution)/shard_map/reduce_scatter | solution.py:302
  1099.6 755.4 %reduce-scatter.20.cloned.1.call-start = ((), (), s32[]{:S(2)}) async-start(), calls=%async_computation.16 | async-start | bytes 17301504 | tf_op jit(solution)/shard_map/reduce_scatter | solution.py:305
  1121.6 1094.2 %reduce-scatter.18.cloned.1.call-start = ((), (), s32[]{:S(2)}) async-start(), calls=%async_computation.15 | async-start | bytes 17301504 | tf_op jit(solution)/shard_map/reduce_scatter | solution.py:304
  1149.4 187.0 %copy-start.79 = (f32[8,32]{1,0:T(8,128)S(1)}, f32[8,32]{1,0:T(8,128)}, u32[]{:S(2)}) copy-start(f32[8,32]{1,0:T(8,128)} %param.41) | copy-start | bytes 3076
  1149.4 187.0 %copy-start.81 = (f32[8,32]{1,0:T(8,128)S(1)}, f32[8,32]{1,0:T(8,128)}, u32[]{:S(2)}) copy-start(f32[8,32]{1,0:T(8,128)} %param.43) | copy-start | bytes 3076
  1149.4 187.0 %copy-start.82 = (f32[8,32]{1,0:T(8,128)S(1)}, f32[8,32]{1,0:T(8,128)}, u32[]{:S(2)}) copy-start(f32[8,32]{1,0:T(8,128)} %param.42) | copy-start | bytes 3076
  1149.4 346.4 %copy-start.37 = (f32[32,3072]{1,0:T(8,128)S(1)}, f32[32,3072]{1,0:T(8,128)}, u32[]{:S(2)}) copy-start(f32[32,3072]{1,0:T(8,128)} %param.29) | copy-start | bytes 1179652
  1149.4 705.6 %copy-start.33 = (f32[128,1024]{1,0:T(8,128)S(1)}, f32[128,1024]{1,0:T(8,128)}, u32[]{:S(2)}) copy-start(f32[128,1024]{1,0:T(8,128)} %param.38) | copy-start | bytes 1572868
  1149.5 705.6 %copy-start.39 = (f32[128,1024]{1,0:T(8,128)S(1)}, f32[128,1024]{1,0:T(8,128)}, u32[]{:S(2)}) copy-start(f32[128,1024]{1,0:T(8,128)} %param.40) | copy-start | bytes 1572868
  1149.5 705.6 %copy-start.40 = (f32[128,1024]{1,0:T(8,128)S(1)}, f32[128,1024]{1,0:T(8,128)}, u32[]{:S(2)}) copy-start(f32[128,1024]{1,0:T(8,128)} %param.39) | copy-start | bytes 1572868
  1153.6 1062.3 %copy-start.35 = (f32[32,4096]{1,0:T(8,128)S(1)}, f32[32,4096]{1,0:T(8,128)}, u32[]{:S(2)}) copy-start(f32[32,4096]{1,0:T(8,128)} %param.35) | copy-start | bytes 1572868
  1153.6 1062.3 %copy-start.41 = (f32[32,4096]{1,0:T(8,128)S(1)}, f32[32,4096]{1,0:T(8,128)}, u32[]{:S(2)}) copy-start(f32[32,4096]{1,0:T(8,128)} %param.37) | copy-start | bytes 1572868
  1153.6 1062.3 %copy-start.42 = (f32[32,4096]{1,0:T(8,128)S(1)}, f32[32,4096]{1,0:T(8,128)}, u32[]{:S(2)}) copy-start(f32[32,4096]{1,0:T(8,128)} %param.36) | copy-start | bytes 1572868
  (95 other events, 911.2 us)
Sparse Core Ops, SparseCore 0:
  11.5 72.0 all-gather.9
  99.5 54.9 all-gather.17
  160.2 55.3 all-gather.19
  219.1 57.0 all-gather.11
  279.7 76.3 all-gather.13
  359.6 76.0 all-gather.15
  951.4 52.4 reduce-scatter.9
  1006.3 54.2 reduce-scatter.11
  1062.9 139.7 reduce-scatter.15
  1205.3 130.3 reduce-scatter.21
  1342.7 153.0 reduce-scatter.13
  1498.0 357.0 reduce-scatter.19
  1857.4 358.4 reduce-scatter.17
where the time goes:
time: 2230 us; the launch traced here: 2220 us
  waiting for transfers between devices  1190 us (53%)
  matrix products  486 us (22%)
  other arithmetic  262 us (12%)
  local copies, waits for them, and re-layouts  203 us (9%)
  blocking collectives  67.8 us (3%)
    reduce_scatter x1, waiting for transfers between devices, per_device(): lax.psum_scatter(up_grad, ('dp', 'ctx'), scatter_dimension=0, tiled=True)  358 us
    reduce_scatter x1, waiting for transfers between devices, per_device(): lax.psum_scatter(down_grad, ('dp', 'ctx'), scatter_dimension=0, tiled=True)  357 us
    reduce_scatter x1, waiting for transfers between devices, per_device(): lax.psum_scatter(qkv_grad, ('dp', 'ctx'), scatter_dimension=0, tiled=True)  159 us
    unnamed x14, waiting for transfers between devices  131 us
    dot_general x8, matrix products, one_group(): jnp.einsum('qhe,khe->hqk', grad_group, value_group, preferred_element_typ...  102 us
    convert_element_type x8, other arithmetic, one_group(): grad_scores = (prob_full * (grad_probs - inner_sum)).astype(jnp.bfloat16)  96.6 us
    all_gather x1, blocking collectives, per_device(): lax.all_gather(norm_weight.astype(jnp.bfloat16), ('dp', 'ctx'), axis=1, t...  67.8 us
    dot_general x16, matrix products, masked_scores(): jnp.einsum('qhe,khe->hqk', query_block, key_heads, preferred_element_type...  64.8 us
  transfers between devices with their start and end apart: 13, of which 10 were waited for; matrix products, arithmetic and copies ran while one was open for 18% of the time, Pallas kernels for 0%

commit v1 on v0

v1 whole, which is shorter than its diff:
```python
import functools
import math

import jax
import jax.numpy as jnp
from jax import lax
from jax.experimental import pallas as pl
from jax.experimental.pallas import tpu as pltpu
from jax.sharding import Mesh, PartitionSpec as P

HEADS = 16
HEAD_DIM = 64
BF = jnp.bfloat16
F32 = jnp.float32
EPS = 1e-05
VMEM_LIMIT = 56 << 20

rate_qkv = 0.04
rate_out = 0.03
rate_up = 0.03
rate_down = 0.02
rate_norm = 0.3

LOG2E = math.log2(math.e)
SCALE = 1.0 / math.sqrt(HEAD_DIM)
NT = (((1,), (1,)), ((), ()))
TN = (((0,), (0,)), ((), ()))


def dot(x, y, dims=None):
    if dims is None:
        return jnp.dot(x, y, preferred_element_type=F32)
    return lax.dot_general(x, y, dims, preferred_element_type=F32)


def call(body, grid, ins, outs, out_shape, args, scratch=(), scalars=0):
    return pl.pallas_call(
        body,
        grid_spec=pltpu.PrefetchScalarGridSpec(
            num_scalar_prefetch=scalars,
            grid=grid,
            in_specs=ins,
            out_specs=outs,
            scratch_shapes=scratch,
        ),
        out_shape=out_shape,
        compiler_params=pltpu.CompilerParams(
            dimension_semantics=("arbitrary",) * len(grid), vmem_limit_bytes=VMEM_LIMIT
        ),
    )(*args)


def shape(rows, cols, dtype):
    return jax.ShapeDtypeStruct((rows, cols), dtype)


def whole(x):
    zeros = (0,) * x.ndim
    return pl.BlockSpec(x.shape, lambda *_: zeros)


def ln_parts(v):
    centre = v - jnp.mean(v, axis=-1, keepdims=True)
    inv = lax.rsqrt(jnp.mean(centre * centre, axis=-1, keepdims=True) + EPS)
    return centre * inv, inv


def ln_grad(xhat, inv, gain, z):
    e = z * gain
    return (
        e - jnp.mean(e, axis=-1, keepdims=True) - xhat * jnp.mean(e * xhat, axis=-1, keepdims=True)
    ) * inv


def column_sums(z, xhat):
    return jnp.concatenate(
        [jnp.sum(z * xhat, axis=0, keepdims=True), jnp.sum(z, axis=0, keepdims=True)], axis=0
    )


def add_to(ref, value):
    @pl.when(pl.program_id(0) == 0)
    def _():
        ref[...] = value

    @pl.when(pl.program_id(0) > 0)
    def _():
        ref[...] += value


def swapped_halves(u):
    lane = lax.broadcasted_iota(jnp.int32, u.shape, 1) % HEAD_DIM
    return jnp.where(lane < HEAD_DIM // 2, pltpu.roll(u, 96, 1), pltpu.roll(u, 32, 1))


def qkv_body(place, x_ref, norm_ref, w_ref, cos_ref, sin_ref, a_ref, q_ref, k_ref, v_ref):
    width = q_ref.shape[1]
    xhat, _ = ln_parts(x_ref[...].astype(F32))
    a = (xhat * norm_ref[0:1, :] + norm_ref[1:2, :]).astype(BF)
    a_ref[...] = a
    cos, sin = cos_ref[...], sin_ref[...]
    for part, ref in enumerate((q_ref, k_ref)):
        rows = dot(a, w_ref[:, part * width : (part + 1) * width])
        for group in range(width // 128):
            u = rows[:, group * 128 : (group + 1) * 128]
            ref[:, group * 128 : (group + 1) * 128] = (u * cos + swapped_halves(u) * sin).astype(BF)
    v_ref[...] = dot(a, w_ref[:, 2 * width :]).astype(BF)


def qkv_forward(place, x_two, norm, w_qkv, cos, sin, span):
    tokens, model = x_two.shape
    width = w_qkv.shape[1] // 3
    row = lambda cols: pl.BlockSpec((span, cols), lambda i, p: (i, 0))
    return call(
        qkv_body,
        (tokens // span,),
        [
            pl.BlockSpec((span, model), lambda i, p: (p[i], 0)),
            whole(norm),
            whole(w_qkv),
            row(128),
            row(128),
        ],
        [row(model), row(width), row(width), row(width)],
        [shape(tokens, model, BF)] + [shape(tokens, width, BF)] * 3,
        (place, x_two, norm, w_qkv, cos, sin),
        scalars=1,
    )


def head_mask(shape_):
    return lax.broadcasted_iota(jnp.int32, shape_, 1) < HEAD_DIM


def forward_body(place, q_ref, k_ref, v_ref, o_ref, lse_ref):
    span = q_ref.shape[0]
    block = pl.program_id(1)
    first = head_mask((span, 128))
    q = q_ref[...]
    zero = jnp.zeros_like(q)
    heads = (jnp.where(first, q, zero), jnp.where(first, zero, q))
    causal = lax.broadcasted_iota(jnp.int32, (span, span), 1) <= lax.broadcasted_iota(
        jnp.int32, (span, span), 0
    )

    def step(start, carry, diagonal):
        k = k_ref[pl.ds(start, span), :]
        v = v_ref[pl.ds(start, span), :]
        result = []
        for head in range(2):
            top, total, acc = carry[head]
            s = dot(heads[head], k, NT) * (SCALE * LOG2E)
            if diagonal:
                s = jnp.where(causal, s, -jnp.inf)
            new_top = jnp.maximum(top, jnp.max(s, axis=1, keepdims=True))
            p = jnp.exp2(s - new_top)
            shrink = jnp.exp2(top - new_top)
            total = total * shrink + jnp.sum(p, axis=1, keepdims=True)
            acc = acc * shrink + dot(p.astype(BF), v)
            result.append((new_top, total, acc))
        return tuple(result)

    empty = (
        jnp.full((span, 1), -1e30, F32),
        jnp.zeros((span, 1), F32),
        jnp.zeros((span, 128), F32),
    )
    carry = step(pl.multiple_of(block * span, span), (empty, empty), True)
    carry = lax.fori_loop(
        0, block, lambda i, c: step(pl.multiple_of(i * span, span), c, False), carry
    )
    (top0, total0, acc0), (top1, total1, acc1) = carry
    o_ref[...] = jnp.where(first, acc0 / total0, acc1 / total1).astype(BF)
    lse = jnp.where(first, top0 + jnp.log2(total0), top1 + jnp.log2(total1))
    turned = lse.T
    lse_ref[...] = jnp.concatenate([turned[0:8], turned[HEAD_DIM : HEAD_DIM + 8]], axis=0)


def attend_forward(place, q, k, v, span):
    tokens, width = q.shape
    pairs, blocks = width // 128, tokens // span
    full = pl.BlockSpec((tokens, 128), lambda h, i, p: (0, h))
    return call(
        forward_body,
        (pairs, blocks),
        [pl.BlockSpec((span, 128), lambda h, i, p: (i, h)), full, full],
        [
            pl.BlockSpec((span, 128), lambda h, i, p: (p[i], h)),
            pl.BlockSpec((16, span), lambda h, i, p: (h, i)),
        ],
        [shape(tokens, width, BF), shape(16 * pairs, tokens, F32)],
        (place, q, k, v),
        scalars=1,
    )


def backward_body(
    place,
    q_ref,
    k_ref,
    v_ref,
    o_ref,
    g_ref,
    lse_ref,
    cos_ref,
    sin_ref,
    dq_ref,
    dk_ref,
    dv_ref,
    dq_acc,
    inner,
    dk_acc,
    dv_acc,
):
    span = dk_ref.shape[0]
    blocks = q_ref.shape[0] // span
    key_block = pl.program_id(1)
    first = head_mask((span, 128))

    @pl.when(key_block == 0)
    def _():
        dq_acc[...] = jnp.zeros_like(dq_acc)
        for i in range(blocks):
            rows = pl.ds(pl.multiple_of(place[i] * span, span), span)
            prod = (o_ref[rows, :].astype(F32) * g_ref[rows, :].astype(F32)).T
            for head in range(2):
                inner[head * 8 : head * 8 + 1, i * span : (i + 1) * span] = jnp.sum(
                    prod[head * HEAD_DIM : (head + 1) * HEAD_DIM], axis=0, keepdims=True
                )

    dk_acc[...] = jnp.zeros_like(dk_acc)
    dv_acc[...] = jnp.zeros_like(dv_acc)
    k = k_ref[...]
    v = v_ref[...]
    zero = jnp.zeros_like(k)
    keys = (jnp.where(first, k, zero), jnp.where(first, zero, k))
    values = (jnp.where(first, v, zero), jnp.where(first, zero, v))
    causal = lax.broadcasted_iota(jnp.int32, (span, span), 0) <= lax.broadcasted_iota(
        jnp.int32, (span, span), 1
    )

    def step(block, diagonal):
        start = pl.multiple_of(block * span, span)
        q = q_ref[pl.ds(start, span), :]
        g = g_ref[pl.ds(pl.multiple_of(place[block] * span, span), span), :]
        for head in range(2):
            mine = first if head == 0 else jnp.logical_not(first)
            lse = lse_ref[head * 8 : head * 8 + 1, pl.ds(start, span)]
            mean = inner[head * 8 : head * 8 + 1, pl.ds(start, span)]
            s = dot(keys[head], q, NT) * (SCALE * LOG2E)
            p = jnp.exp2(s - lse)
            if diagonal:
                p = jnp.where(causal, p, 0.0)
            dp = dot(values[head], g, NT)
            ds = (p * (dp - mean)).astype(BF)
            dv_acc[...] += dot(p.astype(BF), jnp.where(mine, g, zero))
            dk_acc[...] += dot(ds, jnp.where(mine, q, zero))
            dq_acc[pl.ds(start, span), :] += dot(ds, keys[head], TN)

    step(key_block, True)

    @pl.loop(key_block + 1, blocks)
    def _(block):
        step(block, False)

    start = pl.multiple_of(key_block * span, span)
    cos, sin = cos_ref[pl.ds(start, span), :], sin_ref[pl.ds(start, span), :]
    dk = dk_acc[...] * SCALE
    dk_ref[...] = (dk * cos - swapped_halves(dk) * sin).astype(BF)
    dv_ref[...] = dv_acc[...].astype(BF)
    dq = dq_acc[pl.ds(start, span), :] * SCALE
    dq_ref[...] = (dq * cos - swapped_halves(dq) * sin).astype(BF)


def attend_backward(place, q, k, v, o, g, lse, cos, sin, span):
    tokens, width = q.shape
    pairs, blocks = width // 128, tokens // span
    full = pl.BlockSpec((tokens, 128), lambda h, i, p: (0, h))
    part = pl.BlockSpec((span, 128), lambda h, i, p: (i, h))
    return call(
        backward_body,
        (pairs, blocks),
        [
            full,
            part,
            part,
            full,
            full,
            pl.BlockSpec((16, tokens), lambda h, i, p: (h, 0)),
            whole(cos),
            whole(sin),
        ],
        [part, part, part],
        [shape(tokens, width, BF)] * 3,
        (place, q, k, v, o, g, lse, cos, sin),
        scratch=[
            pltpu.VMEM((tokens, 128), F32),
            pltpu.VMEM((16, tokens), F32),
            pltpu.VMEM((span, 128), F32),
            pltpu.VMEM((span, 128), F32),
        ],
        scalars=1,
    )


def project_body(om_ref, oo_ref, wm_ref, wo_ref, x_ref, norm_ref, a_ref, h_ref, c_ref):
    a = dot(om_ref[...], wm_ref[...]) + dot(oo_ref[...], wo_ref[...])
    a_ref[...] = a
    xhat, _ = ln_parts(a)
    h = x_ref[...].astype(F32) + (xhat * norm_ref[2:3, :] + norm_ref[3:4, :])
    h_ref[...] = h
    hhat, _ = ln_parts(h)
    c_ref[...] = (hhat * norm_ref[4:5, :] + norm_ref[5:6, :]).astype(BF)


def project(o_mine, o_other, w_mine, w_other, x, norm, rows=256):
    tokens, model = x.shape
    row = lambda cols: pl.BlockSpec((rows, cols), lambda i: (i, 0))
    half = o_mine.shape[1]
    return call(
        project_body,
        (tokens // rows,),
        [row(half), row(half), whole(w_mine), whole(w_other), row(model), whole(norm)],
        [row(model)] * 3,
        [shape(tokens, model, F32), shape(tokens, model, F32), shape(tokens, model, BF)],
        (o_mine, o_other, w_mine, w_other, x, norm),
    )


def turn_body(m_ref, r_ref, h_ref, y_ref, norm_ref, out_ref, dm_ref, sums_ref):
    xhat, inv = ln_parts(m_ref[...] + r_ref[...].astype(F32))
    gain = norm_ref[6:7, :]
    out_ref[...] = (h_ref[...] + (xhat * gain + norm_ref[7:8, :])).astype(BF)
    z = y_ref[...].astype(F32)
    dm_ref[...] = ln_grad(xhat, inv, gain, z).astype(BF)
    add_to(sums_ref, column_sums(z, xhat))


def turn(m_part, m_other, h, y, norm, rows=256):
    tokens, model = y.shape
    row = pl.BlockSpec((rows, model), lambda i: (i, 0))
    return call(
        turn_body,
        (tokens // rows,),
        [row, row, row, row, whole(norm)],
        [row, row, pl.BlockSpec((2, model), lambda i: (0, 0))],
        [shape(tokens, model, BF), shape(tokens, model, BF), shape(2, model, F32)],
        (m_part, m_other, h, y, norm),
    )


def descend_body(
    dc_ref, r_ref, h_ref, a_ref, y_ref, norm_ref, dh_ref, da_ref, sums3_ref, sums2_ref
):
    dc = dc_ref[...] + r_ref[...].astype(F32)
    hhat, inv = ln_parts(h_ref[...])
    dh = y_ref[...].astype(F32) + ln_grad(hhat, inv, norm_ref[4:5, :], dc)
    dh_ref[...] = dh
    add_to(sums3_ref, column_sums(dc, hhat))
    ahat, inv = ln_parts(a_ref[...])
    da_ref[...] = ln_grad(ahat, inv, norm_ref[2:3, :], dh).astype(BF)
    add_to(sums2_ref, column_sums(dh, ahat))


def descend(dc_part, dc_other, h, a, y, norm, rows=256):
    tokens, model = y.shape
    row = pl.BlockSpec((rows, model), lambda i: (i, 0))
    sums = pl.BlockSpec((2, model), lambda i: (0, 0))
    return call(
        descend_body,
        (tokens // rows,),
        [row] * 5 + [whole(norm)],
        [row, row, sums, sums],
        [
            shape(tokens, model, F32),
            shape(tokens, model, BF),
            shape(2, model, F32),
            shape(2, model, F32),
        ],
        (dc_part, dc_other, h, a, y, norm),
    )


def up_down_body(c_ref, wu_ref, wd_ref, g_ref, s_ref, m_ref, acc):
    u = dot(c_ref[...], wu_ref[...])
    k = math.sqrt(2.0 / math.pi)
    square = u * u
    t = jnp.tanh(u * (k + (k * 0.044715) * square))
    half = 0.5 + 0.5 * t
    g = (u * half).astype(BF)
    g_ref[...] = g
    s_ref[...] = (
        half + (0.5 * u) * (1.0 - t * t) * (k + (3.0 * k * 0.044715) * square)
    ).astype(BF)
    add_to(acc, dot(g, wd_ref[...]))

    @pl.when(pl.program_id(0) == pl.num_programs(0) - 1)
    def _():
        m_ref[...] = acc[...].astype(m_ref.dtype)


def up_down(c, w_up, w_down, dtype, cols=512):
    tokens, model = c.shape
    units = w_up.shape[1]
    wide = pl.BlockSpec((tokens, cols), lambda i: (0, i))
    return call(
        up_down_body,
        (units // cols,),
        [
            whole(c),
            pl.BlockSpec((model, cols), lambda i: (0, i)),
            pl.BlockSpec((cols, model), lambda i: (i, 0)),
        ],
        [wide, wide, pl.BlockSpec((tokens, model), lambda i: (0, 0))],
        [shape(tokens, units, BF), shape(tokens, units, BF), shape(tokens, model, dtype)],
        (c, w_up, w_down),
        scratch=[pltpu.VMEM((tokens, model), F32)],
    )


def down_up_body(dm_ref, s_ref, wu_ref, wd_ref, du_ref, dc_ref, acc):
    du = (dot(dm_ref[...], wd_ref[...], NT) * s_ref[...].astype(F32)).astype(BF)
    du_ref[...] = du
    add_to(acc, dot(du, wu_ref[...], NT))

    @pl.when(pl.program_id(0) == pl.num_programs(0) - 1)
    def _():
        dc_ref[...] = acc[...].astype(dc_ref.dtype)


def down_up(dm, slope, w_up, w_down, dtype, cols=512):
    tokens, model = dm.shape
    units = w_up.shape[1]
    wide = pl.BlockSpec((tokens, cols), lambda i: (0, i))
    return call(
        down_up_body,
        (units // cols,),
        [
            whole(dm),
            wide,
            pl.BlockSpec((model, cols), lambda i: (0, i)),
            pl.BlockSpec((cols, model), lambda i: (i, 0)),
        ],
        [wide, pl.BlockSpec((tokens, model), lambda i: (0, 0))],
        [shape(tokens, units, BF), shape(tokens, model, dtype)],
        (dm, slope, w_up, w_down),
        scratch=[pltpu.VMEM((tokens, model), F32)],
    )


def input_part(q_ref, k_ref, v_ref, w_ref):
    width = q_ref.shape[1]
    return (
        dot(q_ref[...], w_ref[:, :width], NT)
        + dot(k_ref[...], w_ref[:, width : 2 * width], NT)
        + dot(v_ref[...], w_ref[:, 2 * width :], NT)
    )


def other_body(inverse, q_ref, k_ref, v_ref, w_ref, out_ref):
    out_ref[...] = input_part(q_ref, k_ref, v_ref, w_ref).astype(BF)


def own_body(
    inverse, q_ref, k_ref, v_ref, w_ref, r_ref, x_ref, dh_ref, norm_ref, out_ref, sums_ref
):
    z = input_part(q_ref, k_ref, v_ref, w_ref) + r_ref[...].astype(F32)
    xhat, inv = ln_parts(x_ref[...].astype(F32))
    out_ref[...] = (dh_ref[...] + ln_grad(xhat, inv, norm_ref[0:1, :], z)).astype(BF)
    add_to(sums_ref, column_sums(z, xhat))


def input_other(inverse, dq, dk, dv, w_qkv, span):
    width, model = dq.shape[1], w_qkv.shape[0]
    part = pl.BlockSpec((span, width), lambda i, p: (p[i + 2], 0))
    return call(
        other_body,
        (2,),
        [part, part, part, whole(w_qkv)],
        pl.BlockSpec((span, model), lambda i, p: (i, 0)),
        shape(2 * span, model, BF),
        (inverse, dq, dk, dv, w_qkv),
        scalars=1,
    )


def input_own(inverse, dq, dk, dv, w_qkv, recv, x, dh, norm, span):
    width, model = dq.shape[1], w_qkv.shape[0]
    part = pl.BlockSpec((span, width), lambda i, p: (p[i], 0))
    row = pl.BlockSpec((span, model), lambda i, p: (i, 0))
    return call(
        own_body,
        (2,),
        [part, part, part, whole(w_qkv), row, row, row, whole(norm)],
        [row, pl.BlockSpec((2, model), lambda i, p: (0, 0))],
        [shape(2 * span, model, BF), shape(2, model, F32)],
        (inverse, dq, dk, dv, w_qkv, recv, x, dh, norm),
        scalars=1,
    )


def nesterov(gradient, momentum, weight, average, step_rate, token_total):
    scaled = gradient / token_total
    new_momentum = 0.5 * momentum + scaled
    new_weight = weight - step_rate * math.sqrt(token_total) * (scaled + 0.5 * new_momentum)
    new_average = 0.5 * average + 0.5 * new_weight
    return (new_momentum, new_weight, new_average)


def per_device(
    tokens,
    cotangent,
    pair_order,
    qkv_weight,
    qkv_momentum,
    qkv_average,
    out_weight,
    out_momentum,
    out_average,
    up_weight,
    up_momentum,
    up_average,
    down_weight,
    down_momentum,
    down_average,
    norm_weight,
    norm_momentum,
    norm_average,
):
    chips = lax.axis_size("chip")
    ctx_count = lax.axis_size("ctx")
    assert ctx_count == 2 and pair_order.shape[0] == 1 and chips & (chips - 1) == 0
    levels = chips.bit_length() - 1
    chip, core, side = lax.axis_index("chip"), lax.axis_index("core"), lax.axis_index("ctx")
    count, model = tokens.shape
    span = count // 2
    token_total = count * chips * 4
    half = model // 2
    everyone = ("chip", "ctx")
    flip = [(0, 1), (1, 0)]

    def to_core(x):
        return lax.ppermute(x, "core", flip)

    def regroup(x):
        return lax.ppermute(x, ("core", "ctx"), [(0, 0), (1, 2), (2, 1), (3, 3)])

    def exchange(x, level):
        if level == "ctx":
            return lax.ppermute(x, "ctx", flip)
        return lax.ppermute(x, "chip", [(i, i ^ (1 << level)) for i in range(chips)])

    def pick(x, index, dim):
        return lax.dynamic_index_in_dim(x, index, dim, keepdims=False)

    def by_core(mine, other):
        return jnp.where(core == 0, jnp.stack([mine, other]), jnp.stack([other, mine]))

    def reduce_rows(g, order):
        rest = g.shape[levels:]
        names = [levels - 1 - i for i in range(levels)] + ["ctx"]
        if len(rest) == 4:
            names = names[:-1] + ["core", "ctx"]
        for index, level in enumerate(order):
            dim = names.index(level)
            bit = side if level == "ctx" else (chip >> level) & 1
            sent = exchange(pick(g, 1 - bit, dim), level)
            g = pick(g, bit, dim).astype(F32) + sent.astype(F32)
            if index < len(order) - 1:
                g = g.astype(BF)
            names.pop(dim)
        return g

    cube = (2,) * levels
    order_a = [0, "ctx"] + list(range(1, levels))
    order_b = ["ctx", 0] + list(range(1, levels))

    w = qkv_weight.astype(BF).reshape(-1, 3, HEADS // 2, 2, HEAD_DIM)
    mine, other = pick(w, core, 3), to_core(pick(w, 1 - core, 3))
    rows = w.shape[0]
    local = by_core(mine.reshape(rows, -1), other.reshape(rows, -1)).reshape(2 * rows, -1)
    w_qkv = lax.all_gather(local, everyone, axis=0, tiled=True)
    w_qkv = (
        w_qkv.reshape(chips, 2, 2, rows, 3 * half).transpose(0, 2, 1, 3, 4).reshape(model, 3 * half)
    )
    w_out = lax.all_gather(out_weight.astype(BF), everyone, axis=0, tiled=True)
    w_out_other = to_core(w_out)
    units = down_weight.shape[0]
    w = up_weight.astype(BF).reshape(rows, chips, 2, 2 * units)
    mine, other = pick(w, core, 2), to_core(pick(w, 1 - core, 2))
    local = by_core(mine.reshape(rows, -1), other.reshape(rows, -1)).reshape(2 * rows, -1)
    w_up = lax.all_gather(local, everyone, axis=0, tiled=True)
    w_up = w_up.reshape(chips, 2, 2, rows, -1).transpose(0, 2, 1, 3, 4).reshape(model, -1)
    w_down = lax.all_gather(down_weight.astype(BF), everyone, axis=0, tiled=True)
    norm = lax.all_gather(norm_weight.astype(BF), ("chip", "core", "ctx"), axis=1, tiled=True).astype(F32)

    x = regroup(tokens)
    y = regroup(cotangent)
    x_two = jnp.concatenate([x, to_core(x)], axis=0)
    order_row = jnp.where(core == side, pair_order, to_core(pair_order))[0]
    mine_first = pick(order_row, core, 0) == 0
    place = jnp.where(
        mine_first, jnp.array([0, 2, 3, 1], jnp.int32), jnp.array([2, 0, 1, 3], jnp.int32)
    )
    inverse = jnp.where(
        mine_first, jnp.array([0, 3, 1, 2], jnp.int32), jnp.array([1, 2, 0, 3], jnp.int32)
    )
    steps = jnp.arange(HEAD_DIM // 2, dtype=F32)
    frequency = jnp.exp(steps * (-math.log(10000.0) / (HEAD_DIM // 2)))
    angles = jnp.arange(2 * count, dtype=jnp.int32).astype(F32)[:, None] * frequency[None, :]
    cos, sin = jnp.cos(angles), jnp.sin(angles)
    cos_table = jnp.concatenate([cos] * 4, axis=1)
    sin_table = jnp.concatenate([-sin, sin] * 2, axis=1)

    a, q, k, v = qkv_forward(place, x_two, norm, w_qkv, cos_table, sin_table, span)
    o, lse = attend_forward(place, q, k, v, span)
    o_mine, o_sent = o[:count], o[count:]
    o_other = to_core(o_sent)
    projected, hidden, c = project(o_mine, o_other, w_out, w_out_other, x, norm)
    c_other = to_core(c)
    g_other, slope_other, m_sent = up_down(c_other, w_up, w_down, BF)
    m_recv = to_core(m_sent)
    g_mine, slope_mine, m_part = up_down(c, w_up, w_down, F32)
    output, dm, sums4 = turn(m_part, m_recv, hidden, y, norm)

    dm_other = to_core(dm)
    du_mine, dc_part = down_up(dm, slope_mine, w_up, w_down, F32)
    du_other, dc_sent = down_up(dm_other, slope_other, w_up, w_down, BF)
    dc_recv = to_core(dc_sent)
    g_two = jnp.concatenate([g_mine, g_other], axis=0)
    dm_two = jnp.concatenate([dm, dm_other], axis=0)
    grad_down = dot(g_two, dm_two, TN).astype(BF)
    c_two = jnp.concatenate([c, c_other], axis=0)
    du_two = jnp.concatenate([du_mine, du_other], axis=0)
    grad_up = dot(c_two, du_two, TN).astype(BF)
    dh, da, sums3, sums2 = descend(dc_part, dc_recv, hidden, projected, y, norm)
    da_two = jnp.concatenate([da, to_core(da)], axis=0)
    do = dot(da_two, w_out, NT).astype(BF)
    grad_out = dot(o, da_two, TN).astype(BF)
    dq, dk, dv = attend_backward(place, q, k, v, o, do, lse, cos_table, sin_table, span)
    dx_recv = to_core(input_other(inverse, dq, dk, dv, w_qkv, span))
    grad_q, grad_k, grad_v = (dot(a, d, TN).astype(BF) for d in (dq, dk, dv))
    input_grad, sums1 = input_own(inverse, dq, dk, dv, w_qkv, dx_recv, x, dh, norm, span)

    down_sum = jnp.concatenate(
        [
            reduce_rows(grad_down[:, s].reshape(*cube, 2, units, half), o_)
            for s, o_ in ((slice(0, half), order_a), (slice(half, model), order_b))
        ],
        axis=-1,
    ).reshape(units, model)
    out_sum = jnp.concatenate(
        [
            reduce_rows(grad_out[:, s].reshape(*cube, 2, rows, half), o_)
            for s, o_ in ((slice(0, half), order_a), (slice(half, model), order_b))
        ],
        axis=-1,
    ).reshape(rows, model)

    def from_cores(part):
        return by_core(pick(part, core, 0), to_core(pick(part, 1 - core, 0)))

    ff_half = grad_up.shape[1] // 2
    up_part = jnp.concatenate(
        [
            reduce_rows(grad_up[:, s].reshape(*cube, 2, 2, rows, ff_half), o_)
            for s, o_ in ((slice(0, ff_half), order_a), (slice(ff_half, 2 * ff_half), order_b))
        ],
        axis=-1,
    )
    up_sum = (
        from_cores(up_part)
        .reshape(2, rows, chips, 2 * units)
        .transpose(1, 2, 0, 3)
        .reshape(rows, 4 * chips * units)
    )
    qkv_part = jnp.stack(
        [
            reduce_rows(g.reshape(*cube, 2, 2, rows, half), o_)
            for g, o_ in ((grad_q, order_a), (grad_k, order_b), (grad_v, order_a))
        ],
        axis=2,
    )
    qkv_sum = (
        from_cores(qkv_part)
        .reshape(2, rows, 3, HEADS // 2, HEAD_DIM)
        .transpose(1, 2, 3, 0, 4)
        .reshape(rows, 3 * model)
    )
    norm_grad = jnp.concatenate([sums1, sums2, sums3, sums4], axis=0)
    norm_grad = norm_grad + to_core(norm_grad)
    tiles = norm_grad.reshape(8, *cube, 2, 2, rows)
    tiles = jnp.moveaxis(tiles, 0, levels + 2)
    tiles = pick(tiles, core, levels)
    norm_sum = reduce_rows_f32(tiles, order_a, levels, chip, side, exchange, pick)

    qkv_new = nesterov(qkv_sum, qkv_momentum, qkv_weight, qkv_average, rate_qkv, token_total)
    out_new = nesterov(out_sum, out_momentum, out_weight, out_average, rate_out, token_total)
    up_new = nesterov(up_sum, up_momentum, up_weight, up_average, rate_up, token_total)
    down_new = nesterov(down_sum, down_momentum, down_weight, down_average, rate_down, token_total)
    norm_new = nesterov(norm_sum, norm_momentum, norm_weight, norm_average, rate_norm, token_total)
    return (
        regroup(output),
        regroup(input_grad),
        *qkv_new,
        *out_new,
        *up_new,
        *down_new,
        *norm_new,
    )


def reduce_rows_f32(g, order, levels, chip, side, exchange, pick):
    names = [levels - 1 - i for i in range(levels)] + ["ctx"]
    for level in order:
        dim = names.index(level)
        bit = side if level == "ctx" else (chip >> level) & 1
        g = pick(g, bit, dim) + exchange(pick(g, 1 - bit, dim), level)
        names.pop(dim)
    return g


def solution(mesh):
    dp, ctx = mesh.shape["dp"], mesh.shape["ctx"]
    inner = Mesh(mesh.devices.reshape(dp // 2, 2, ctx), ("chip", "core", "ctx"))
    rows = P(("chip", "core", "ctx"), None)
    cols = P(None, ("chip", "core", "ctx"))
    return jax.shard_map(
        per_device,
        mesh=inner,
        in_specs=(rows, rows, P(("chip", "core"), None)) + (rows,) * 12 + (cols,) * 3,
        out_specs=(rows,) * 14 + (cols,) * 3,
        check_vma=False,
    )
```

time: 2230 us -> 755 us (0.34)
  waiting for transfers between devices: 1190 us -> 185 us
  matrix products: 486 us -> 42.3 us
  Pallas kernels: 0 us -> 261 us
  other arithmetic: 262 us -> 34.2 us
  local copies, waits for them, and re-layouts: 203 us -> 42.8 us
  starting transfers between devices: 1.46 us -> 93.1 us
    reduce_scatter x6 -> x0, waiting for transfers between devices: 972 us -> none  [the longest x1 358 us: per_device(): lax.psum_scatter(up_grad, ('dp', 'ctx'), scatter_dimension=0, tiled=True)]
    dot_general x68 -> x7, matrix products: 486 us -> 42.3 us  [dot(): return lax.dot_general(x, y, dims, preferred_element_type=F32)]
    pallas_call x0 -> x12, Pallas kernels: none -> 261 us  [call(): pl.pallas_call(body, grid_spec=pltpu.PrefetchScalarGridSpec(num_scalar_pr...]
    unnamed x14 -> x4, waiting for transfers between devices: 131 us -> 0.07 us
    convert_element_type x17 -> x32, other arithmetic: 136 us -> 8.1 us  [the longest x27 4.67 us: reduce_rows(): g = g.astype(BF)]
    ppermute x0 -> x59, waiting for transfers between devices: none -> 119 us  [the longest x30 49.8 us: exchange(): return lax.ppermute(x, 'chip', [(i, i ^ 1 << level) for i in range(chips)])]
    ppermute x0 -> x59, starting transfers between devices: none -> 92.9 us  [the longest x30 30.9 us: exchange(): return lax.ppermute(x, 'chip', [(i, i ^ 1 << level) for i in range(chips)])]
    reduce_sum x21 -> x0, other arithmetic: 66.2 us -> none  [the longest x8 34.8 us: one_group(): row_total = jnp.sum(weights, axis=2, keepdims=True)]
  transfers between devices with their start and end apart: 13 -> 63, of which waited for: 10 -> 25; matrix products, arithmetic and copies ran while one was open for 18% -> 13% of each run, Pallas kernels for 0% -> 33%
where the time goes in v1:
time: 755 us; the launch traced here: 741 us
  Pallas kernels  261 us (35%)
  waiting for transfers between devices  185 us (25%)
  starting transfers between devices  93.1 us (12%)
  blocking collectives  66.2 us (9%)
  local copies, waits for them, and re-layouts  42.8 us (6%)
  matrix products  42.3 us (6%)
  other arithmetic  34.2 us (5%)
  between operations  15.4 us (2%)
    pallas_call x12, Pallas kernels, call(): pl.pallas_call(body, grid_spec=pltpu.PrefetchScalarGridSpec(num_scalar_pr...  261 us
    all_gather x1, blocking collectives, per_device(): lax.all_gather(norm_weight.astype(BF), ('chip', 'core', 'ctx'), axis=1, t...  66.2 us
    all_gather x1, waiting for transfers between devices, per_device(): lax.all_gather(down_weight.astype(BF), everyone, axis=0, tiled=True)  59.2 us
    ppermute x30, waiting for transfers between devices, exchange(): return lax.ppermute(x, 'chip', [(i, i ^ 1 << level) for i in range(chips)])  49.8 us
    dot_general x7, matrix products, dot(): return lax.dot_general(x, y, dims, preferred_element_type=F32)  42.3 us
    ppermute x10, waiting for transfers between devices, exchange(): return lax.ppermute(x, 'ctx', flip)  39 us
    ppermute x30, starting transfers between devices, exchange(): return lax.ppermute(x, 'chip', [(i, i ^ 1 << level) for i in range(chips)])  30.9 us
    ppermute x4, waiting for transfers between devices, regroup(): return lax.ppermute(x, ('core', 'ctx'), [(0, 0), (1, 2), (2, 1), (3, 3)])  24.6 us
  transfers between devices with their start and end apart: 63, of which 25 were waited for; matrix products, arithmetic and copies ran while one was open for 13% of the time, Pallas kernels for 33%

profile of v1, /device:TPU:1, one launch (start us, length us, event | category | flops | bytes accessed | tf_op | source)
XLA Modules:
  0.0 740.8 jit_solution(14265937196273802677)
XLA Ops:
  23.3 24.6 %collective-permute-done.1.x_ref = bf16[1024,1024]{1,0:T(8,128)(2,1)S(1)} collective-permute-done((bf16[1024,1024]{1,0:T(8,128)(2,1)}, bf16[1024,1024]{1,0:T(8,128)(2,1)S(1)}, u32[]{:S(2)}, u32[]{:S(2)}) %collective-permute-start.1) | collective-permute-done | bytes 2097184 | tf_op jit(solution)/shard_map/ppermute | solution.py:546
  48.4 66.2 %all-gather = bf16[32,32,8]{1,2,0:T(8,128)(2,1)S(1)} all-gather(bf16[1,32,8]{1,2,0:T(8,128)(2,1)S(1)} %convert_bitcast_fusion), channel_id=1, replica_groups=mesh['chip'=8,'core'=2,'ctx'=2] {'chip','core','ctx'}, dimensions={0}, use_global_device_ids=true | all-gather | bytes 16896 | tf_op jit(solution)/shard_map/all_gather | solution.py:595
  142.0 13.8 %shard_map.341 = (bf16[2048,1024]{1,0:T(8,128)(2,1)}, bf16[2048,512]{1,0:T(8,128)(2,1)}, bf16[2048,512]{1,0:T(8,128)(2,1)}, bf16[2048,512]{1,0:T(8,128)(2,1)}) custom-call(s32[4]{0:T(128)} %broadcast_select_fusion.1.place, bf16[2048,1024]{1,0:T(8,128)(2,1)} %pad_maximum_fusion.x_ref, f32[8,1024]{1,0:T(8,128)} %bitcast.318, bf16[1024,1536]{1,0:T(8,128)(2,1)} %bitcast.306, ...), custom_call_target="tpu_custom_call" | custom-call | tf_op jit(solution)/shard_map/pallas_call | solution.py:37
  155.9 54.8 %shard_map.342 = (bf16[2048,512]{1,0:T(8,128)(2,1)}, f32[64,2048]{1,0:T(8,128)}) custom-call(s32[4]{0:T(128)} %broadcast_select_fusion.1.place, bf16[2048,512]{1,0:T(8,128)(2,1)} %get-tuple-element.48.q_ref, bf16[2048,512]{1,0:T(8,128)(2,1)} %get-tuple-element.49.k_ref, bf16[2048,512]{1,0:T(8,128)(2,1)} %get-tuple-element.50.v_ref), custom_call_target="tpu_custom_call" | custom-call | tf_op jit(solution)/shard_map/pallas_call | solution.py:37
  218.4 8.4 %shard_map.343 = (f32[1024,1024]{1,0:T(8,128)}, f32[1024,1024]{1,0:T(8,128)}, bf16[1024,1024]{1,0:T(8,128)(2,1)}) custom-call(bf16[1024,512]{1,0:T(8,128)(2,1)} %get-tuple-element.105.om_ref, bf16[1024,512]{1,0:T(8,128)(2,1)} %copy-done.20, bf16[512,1024]{1,0:T(8,128)(2,1)} %all-gather.8.cloned.1.call-done.wm_ref, ...), custom_call_target="tpu_custom_call" | custom-call | tf_op jit(solution)/shard_map/pallas_call | solution.py:37
  235.0 59.2 %all-gather.12.cloned.1.call-done.wd_ref = bf16[2048,1024]{1,0:T(8,128)(2,1)} async-done(((bf16[128,1024]{1,0:T(8,128)(2,1)}), bf16[2048,1024]{1,0:T(8,128)(2,1)}) %all-gather.12.cloned.1.call-update) | async-done | bytes 4194320 | tf_op jit(solution)/shard_map/all_gather | solution.py:594
  294.2 18.3 %shard_map.345 = (bf16[1024,2048]{1,0:T(8,128)(2,1)}, bf16[1024,2048]{1,0:T(8,128)(2,1)}, bf16[1024,1024]{1,0:T(8,128)(2,1)}) custom-call(bf16[1024,1024]{1,0:T(8,128)(2,1)} %collective-permute-done.7.c_ref, bf16[1024,2048]{1,0:T(8,128)(2,1)} %bitcast.302, bf16[2048,1024]{1,0:T(8,128)(2,1)} %all-gather.12.cloned.1.call-done.wd_ref), custom_call_target="tpu_custom_call" | custom-call | tf_op jit(solution)/shard_map/pallas_call | solution.py:37
  314.4 18.6 %shard_map.344 = (bf16[1024,2048]{1,0:T(8,128)(2,1)}, bf16[1024,2048]{1,0:T(8,128)(2,1)}, f32[1024,1024]{1,0:T(8,128)}) custom-call(bf16[1024,1024]{1,0:T(8,128)(2,1)} %get-tuple-element.52.c_ref, bf16[1024,2048]{1,0:T(8,128)(2,1)} %bitcast.303, bf16[2048,1024]{1,0:T(8,128)(2,1)} %all-gather.12.cloned.1.call-done.wd_ref), custom_call_target="tpu_custom_call" | custom-call | tf_op jit(solution)/shard_map/pallas_call | solution.py:37
  335.1 8.6 %shard_map.346 = (bf16[1024,1024]{1,0:T(8,128)(2,1)}, bf16[1024,1024]{1,0:T(8,128)(2,1)}, f32[2,1024]{1,0:T(2,128)}) custom-call(f32[1024,1024]{1,0:T(8,128)} %get-tuple-element.53.m_ref, bf16[1024,1024]{1,0:T(8,128)(2,1)} %copy-done.15, f32[1024,1024]{1,0:T(8,128)} %get-tuple-element.55.h_ref, bf16[1024,1024]{1,0:T(8,128)(2,1)} %copy-done.4, ...), custom_call_target="tpu_custom_call" | custom-call | tf_op jit(solution)/shard_map/pallas_call | solution.py:37
  347.2 16.9 %shard_map.347 = (bf16[1024,2048]{1,0:T(8,128)(2,1)}, f32[1024,1024]{1,0:T(8,128)}) custom-call(bf16[1024,1024]{1,0:T(8,128)(2,1)} %get-tuple-element.57.dm_ref, bf16[1024,2048]{1,0:T(8,128)(2,1)} %get-tuple-element.58.s_ref, bf16[1024,2048]{1,0:T(8,128)(2,1)} %bitcast.304, bf16[2048,1024]{1,0:T(8,128)(2,1)} %all-gather.12.cloned.1.call-done.wd_ref), custom_call_target="tpu_custom_call" | custom-call | tf_op jit(solution)/shard_map/pallas_call | solution.py:37
  365.5 16.0 %shard_map.348 = (bf16[1024,2048]{1,0:T(8,128)(2,1)}, bf16[1024,1024]{1,0:T(8,128)(2,1)}) custom-call(bf16[1024,1024]{1,0:T(8,128)(2,1)} %copy-done.8, bf16[1024,2048]{1,0:T(8,128)(2,1)} %get-tuple-element.60.s_ref, bf16[1024,2048]{1,0:T(8,128)(2,1)} %bitcast.305, bf16[2048,1024]{1,0:T(8,128)(2,1)} %all-gather.12.cloned.1.call-done.wd_ref), custom_call_target="tpu_custom_call" | custom-call | tf_op jit(solution)/shard_map/pallas_call | solution.py:37
  381.5 12.1 %fusion.19 = bf16[1024,2048]{1,0:T(8,128)(2,1)S(1)} fusion(bf16[1024,2048]{1,0:T(8,128)(2,1)} %get-tuple-element.72, bf16[1024,2048]{1,0:T(8,128)(2,1)} %get-tuple-element.71, bf16[1024,1024]{1,0:T(8,128)(2,1)} %collective-permute-done.7.c_ref, bf16[1024,1024]{1,0:T(8,128)(2,1)S(1)} %copy-done.6), kind=kOutput, calls=%fused_computation.16 | convolution fusion | flops 8617197568 | bytes 16777216 | tf_op jit(solution)/shard_map/dot_general | solution.py:33
  397.1 11.8 %fusion.14 = bf16[2048,1024]{1,0:T(8,128)(2,1)S(1)} fusion(bf16[1024,1024]{1,0:T(8,128)(2,1)S(1)} %copy-done.9, bf16[1024,1024]{1,0:T(8,128)(2,1)S(1)} %copy-done.7, bf16[1024,2048]{1,0:T(8,128)(2,1)} %get-tuple-element.74, bf16[1024,2048]{1,0:T(8,128)(2,1)} %get-tuple-element.73), kind=kOutput, calls=%fused_computation.15 | convolution fusion | flops 8617197568 | bytes 16777216 | tf_op jit(solution)/shard_map/dot_general | solution.py:33
  413.7 8.1 %collective-permute-done.41 = bf16[2,2,2,2,32,1024]{5,4,3,2,1,0:T(8,128)(2,1)} collective-permute-done((bf16[2,2,2,2,32,1024]{5,4,3,2,1,0:T(8,128)(2,1)}, bf16[2,2,2,2,32,1024]{5,4,3,2,1,0:T(8,128)(2,1)}, u32[]{:S(2)}, u32[]{:S(2)}) %collective-permute-start.41) | collective-permute-done | bytes 1048608 | tf_op jit(solution)/shard_map/ppermute | solution.py:550
  424.2 20.1 %collective-permute-done.50 = bf16[2,2,2,128,512]{4,3,0,1,2:T(8,128)(2,1)S(1)} collective-permute-done((bf16[2,2,2,128,512]{4,3,0,1,2:T(8,128)(2,1)S(1)}, bf16[2,2,2,128,512]{4,3,0,1,2:T(8,128)(2,1)S(1)}, u32[]{:S(2)}, u32[]{:S(2)}) %collective-permute-start.50) | collective-permute-done | bytes 1048608 | tf_op jit(solution)/shard_map/ppermute | solution.py:550
  446.2 8.3 %collective-permute-done.42 = bf16[2,2,2,32,1024]{4,3,2,1,0:T(8,128)(2,1)S(1)} collective-permute-done((bf16[2,2,2,32,1024]{4,3,2,1,0:T(8,128)(2,1)S(1)}, bf16[2,2,2,32,1024]{4,3,2,1,0:T(8,128)(2,1)S(1)}, u32[]{:S(2)}, u32[]{:S(2)}) %collective-permute-start.42) | collective-permute-done | bytes 524320 | tf_op jit(solution)/shard_map/ppermute | solution.py:551
  457.0 8.7 %collective-permute-done.51 = bf16[2,2,128,512]{3,2,0,1:T(8,128)(2,1)S(1)} collective-permute-done((bf16[2,2,128,512]{3,2,0,1:T(8,128)(2,1)S(1)}, bf16[2,2,128,512]{3,2,0,1:T(8,128)(2,1)S(1)}, u32[]{:S(2)}, u32[]{:S(2)}) %collective-permute-start.51) | collective-permute-done | bytes 524320 | tf_op jit(solution)/shard_map/ppermute | solution.py:551
  486.1 12.1 %shard_map.349 = (f32[1024,1024]{1,0:T(8,128)}, bf16[1024,1024]{1,0:T(8,128)(2,1)}, f32[2,1024]{1,0:T(2,128)}, f32[2,1024]{1,0:T(2,128)}) custom-call(f32[1024,1024]{1,0:T(8,128)} %get-tuple-element.59.dc_ref, bf16[1024,1024]{1,0:T(8,128)(2,1)} %copy-done.16, f32[1024,1024]{1,0:T(8,128)} %get-tuple-element.55.h_ref, f32[1024,1024]{1,0:T(8,128)} %get-tuple-element.62.a_ref, ...), custom_call_target="tpu_custom_call" | custom-call | tf_op jit(solution)/shard_map/pallas_call | solution.py:37
  524.2 74.0 %shard_map.350 = (bf16[2048,512]{1,0:T(8,128)(2,1)}, bf16[2048,512]{1,0:T(8,128)(2,1)}, bf16[2048,512]{1,0:T(8,128)(2,1)}) custom-call(s32[4]{0:T(128)} %broadcast_select_fusion.1.place, bf16[2048,512]{1,0:T(8,128)(2,1)} %get-tuple-element.48.q_ref, bf16[2048,512]{1,0:T(8,128)(2,1)} %get-tuple-element.49.k_ref, bf16[2048,512]{1,0:T(8,128)(2,1)} %get-tuple-element.50.v_ref, ...), custom_call_target="tpu_custom_call" | custom-call | tf_op jit(solution)/shard_map/pallas_call | solution.py:37
  612.3 7.9 %shard_map.351 = bf16[1024,1024]{1,0:T(8,128)(2,1)} custom-call(s32[4]{0:T(128)} %broadcast_select_fusion.inverse, bf16[2048,512]{1,0:T(8,128)(2,1)} %get-tuple-element.65.q_ref, bf16[2048,512]{1,0:T(8,128)(2,1)} %get-tuple-element.66.k_ref, bf16[2048,512]{1,0:T(8,128)(2,1)} %get-tuple-element.67.v_ref, bf16[1024,1536]{1,0:T(8,128)(2,1)} %bitcast.307), custom_call_target="tpu_custom_call" | custom-call | tf_op jit(solution)/shard_map/pallas_call | solution.py:37
  621.7 9.2 %collective-permute-done.34 = bf16[2,2,32,512]{3,2,0,1:T(8,128)(2,1)S(1)} collective-permute-done((bf16[2,2,32,512]{3,2,0,1:T(8,128)(2,1)S(1)}, bf16[2,2,32,512]{3,2,0,1:T(8,128)(2,1)S(1)}, u32[]{:S(2)}, u32[]{:S(2)}) %collective-permute-start.34) | collective-permute-done | bytes 131104 | tf_op jit(solution)/shard_map/ppermute | solution.py:551
  669.8 11.9 %shard_map.352 = (bf16[1024,1024]{1,0:T(8,128)(2,1)}, f32[2,1024]{1,0:T(2,128)}) custom-call(s32[4]{0:T(128)} %broadcast_select_fusion.inverse, bf16[2048,512]{1,0:T(8,128)(2,1)} %get-tuple-element.65.q_ref, bf16[2048,512]{1,0:T(8,128)(2,1)} %get-tuple-element.66.k_ref, bf16[2048,512]{1,0:T(8,128)(2,1)} %get-tuple-element.67.v_ref, ...), custom_call_target="tpu_custom_call" | custom-call | tf_op jit(solution)/shard_map/pallas_call | solution.py:37
  682.5 10.6 %collective-permute-start.54 = (f32[8,1024]{1,0:T(8,128)S(1)}, f32[8,1024]{1,0:T(8,128)S(1)}, u32[]{:S(2)}, u32[]{:S(2)}) collective-permute-start(f32[8,1024]{1,0:T(8,128)S(1)} %pad_maximum_fusion.4), channel_id=1, source_target_pairs={{0,2},{2,0},{1,3},{3,1},{4,6},{6,4},{5,7},{7,5},{8,10},{10,8},{9,1... | collective-permute-start | bytes 98312 | tf_op jit(solution)/shard_map/ppermute | solution.py:543
  699.0 15.4 %collective-permute-start.56 = (f32[2,2,8,32]{3,1,0,2:T(2,128)S(1)}, f32[2,2,8,32]{3,1,0,2:T(2,128)S(1)}, u32[]{:S(2)}, u32[]{:S(2)}) collective-permute-start(f32[2,2,8,32]{3,1,0,2:T(2,128)S(1)} %bitcast.338), channel_id=1, source_target_pairs={{0,1},{1,0},{2,3},{3,2},{4,5},{5,4},{6,7},{7,6},{8,9},{9,8},{10,11... | collective-permute-start | bytes 12296 | tf_op jit(solution)/shard_map/ppermute | solution.py:550
  (350 shorter events, 209.7 us)
Async XLA Ops:
  7.2 116.7 %all-gather.8.cloned.1.call-start = ((), (), s32[]{:S(2)}) async-start(), calls=%async_computation.1 | async-start | bytes 1114112 | tf_op jit(solution)/shard_map/all_gather | solution.py:586
  8.9 129.3 %all-gather.6.cloned.1.call-start = ((), (), s32[]{:S(2)}) async-start(), calls=%async_computation | async-start | bytes 3342336 | tf_op jit(solution)/shard_map/all_gather | solution.py:582
  14.4 215.9 %all-gather.10.cloned.1.call-start = ((), (), s32[]{:S(2)}) async-start(), calls=%async_computation.2 | async-start | bytes 4456448 | tf_op jit(solution)/shard_map/all_gather | solution.py:592
  18.0 276.2 %all-gather.12.cloned.1.call-start = ((), (), s32[]{:S(2)}) async-start(), calls=%async_computation.3 | async-start | bytes 4456448 | tf_op jit(solution)/shard_map/all_gather | solution.py:594
  18.0 29.9 %collective-permute-start.1 = (bf16[1024,1024]{1,0:T(8,128)(2,1)}, bf16[1024,1024]{1,0:T(8,128)(2,1)S(1)}, u32[]{:S(2)}, u32[]{:S(2)}) collective-permute-start(bf16[1024,1024]{1,0:T(8,128)(2,1)} %param.22), channel_id=1, source_target_pairs={{0,0},{1,2},{2,1},{3,3},{4,4},{5,6},{6,5},{7,7},{8,8},{9,10},{10,9... | collective-permute-start | bytes 6291464 | tf_op jit(solution)/shard_map/ppermute | solution.py:546
  47.9 79.4 %collective-permute-start.2 = (bf16[1024,1024]{1,0:T(8,128)(2,1)S(1)}, bf16[1024,1024]{1,0:T(8,128)(2,1)}, u32[]{:S(2)}, u32[]{:S(2)}) collective-permute-start(bf16[1024,1024]{1,0:T(8,128)(2,1)S(1)} %collective-permute-done.1.x_ref), channel_id=1, source_target_pairs={{0,2},{2,0},{1,3},{3,1},{4,6},{6,4},{5,7},{7,5},{8,10},{10,8},{9,1... | collective-permute-start | bytes 6291464 | tf_op jit(solution)/shard_map/ppermute | solution.py:543
  47.9 74.3 %collective-permute-start = (s32[1,2]{1,0:T(1,128)S(1)}, s32[1,2]{1,0:T(1,128)S(1)}, u32[]{:S(2)}, u32[]{:S(2)}) collective-permute-start(s32[1,2]{1,0:T(1,128)S(1)} %copy-done.32), channel_id=1, source_target_pairs={{0,2},{2,0},{1,3},{3,1},{4,6},{6,4},{5,7},{7,5},{8,10},{10,8},{9,1... | collective-permute-start | bytes 32 | tf_op jit(solution)/shard_map/ppermute | solution.py:543
  123.9 91.2 %collective-permute-start.5 = (bf16[512,1024]{1,0:T(8,128)(2,1)}, bf16[512,1024]{1,0:T(8,128)(2,1)}, u32[]{:S(2)}, u32[]{:S(2)}) collective-permute-start(bf16[512,1024]{1,0:T(8,128)(2,1)} %all-gather.8.cloned.1.call-done.wm_ref), channel_id=1, source_target_pairs={{0,2},{2,0},{1,3},{3,1},{4,6},{6,4},{5,7},{7,5},{8,10},{10,8},{9,1... | collective-permute-start | bytes 3145736 | tf_op jit(solution)/shard_map/ppermute | solution.py:543
  226.8 67.4 %collective-permute-start.7 = (bf16[1024,1024]{1,0:T(8,128)(2,1)}, bf16[1024,1024]{1,0:T(8,128)(2,1)}, u32[]{:S(2)}, u32[]{:S(2)}) collective-permute-start(bf16[1024,1024]{1,0:T(8,128)(2,1)} %get-tuple-element.52.c_ref), channel_id=1, source_target_pairs={{0,2},{2,0},{1,3},{3,1},{4,6},{6,4},{5,7},{7,5},{8,10},{10,8},{9,1... | collective-permute-start | bytes 6291464 | tf_op jit(solution)/shard_map/ppermute | solution.py:543
  227.1 105.9 %collective-permute-start.9 = (bf16[1024,1024]{1,0:T(8,128)(2,1)}, bf16[1024,1024]{1,0:T(8,128)(2,1)S(1)}, u32[]{:S(2)}, u32[]{:S(2)}) collective-permute-start(bf16[1024,1024]{1,0:T(8,128)(2,1)} %param.23), channel_id=1, source_target_pairs={{0,0},{1,2},{2,1},{3,3},{4,4},{5,6},{6,5},{7,7},{8,8},{9,10},{10,9... | collective-permute-start | bytes 6291464 | tf_op jit(solution)/shard_map/ppermute | solution.py:546
  343.8 69.5 %collective-permute-start.10 = (bf16[1024,1024]{1,0:T(8,128)(2,1)}, bf16[1024,1024]{1,0:T(8,128)(2,1)S(1)}, u32[]{:S(2)}, u32[]{:S(2)}) collective-permute-start(bf16[1024,1024]{1,0:T(8,128)(2,1)} %get-tuple-element.56), channel_id=1, source_target_pairs={{0,0},{1,2},{2,1},{3,3},{4,4},{5,6},{6,5},{7,7},{8,8},{9,10},{10,9... | collective-permute-start | bytes 6291464 | tf_op jit(solution)/shard_map/ppermute | solution.py:546
  396.4 27.2 %collective-permute-start.37 = (bf16[2,2,2,2,32,1024]{5,4,2,0,1,3:T(8,128)(2,1)}, bf16[2,2,2,2,32,1024]{5,4,2,0,1,3:T(8,128)(2,1)S(1)}, u32[]{:S(2)}, u32[]{:S(2)}) collective-permute-start(bf16[2,2,2,2,32,1024]{5,4,2,0,1,3:T(8,128)(2,1)} %bitcast.293), channel_id=1, source_target_pairs={{0,4},{4,0},{8,12},{12,8},{16,20},{20,16},{24,28},{28,24},{1,5},{5... | collective-permute-start | bytes 3145736 | tf_op jit(solution)/shard_map/ppermute | solution.py:551
  409.4 34.9 %collective-permute-start.50 = (bf16[2,2,2,128,512]{4,3,0,1,2:T(8,128)(2,1)S(1)}, bf16[2,2,2,128,512]{4,3,0,1,2:T(8,128)(2,1)S(1)}, u32[]{:S(2)}, u32[]{:S(2)}) collective-permute-start(bf16[2,2,2,128,512]{4,3,0,1,2:T(8,128)(2,1)S(1)} %bitcast.324), channel_id=1, source_target_pairs={{0,1},{1,0},{2,3},{3,2},{4,5},{5,4},{6,7},{7,6},{8,9},{9,8},{10,11... | collective-permute-start | bytes 3145736 | tf_op jit(solution)/shard_map/ppermute | solution.py:550
  412.0 32.7 %collective-permute-start.46 = (bf16[2,2,2,128,512]{4,3,0,1,2:T(8,128)(2,1)S(1)}, bf16[2,2,2,128,512]{4,3,0,1,2:T(8,128)(2,1)S(1)}, u32[]{:S(2)}, u32[]{:S(2)}) collective-permute-start(bf16[2,2,2,128,512]{4,3,0,1,2:T(8,128)(2,1)S(1)} %bitcast.325), channel_id=1, source_target_pairs={{0,4},{4,0},{8,12},{12,8},{16,20},{20,16},{24,28},{28,24},{1,5},{5... | collective-permute-start | bytes 3145736 | tf_op jit(solution)/shard_map/ppermute | solution.py:551
  413.3 71.5 %collective-permute-start.12 = (bf16[1024,1024]{1,0:T(8,128)(2,1)S(1)}, bf16[1024,1024]{1,0:T(8,128)(2,1)S(1)}, u32[]{:S(2)}, u32[]{:S(2)}) collective-permute-start(bf16[1024,1024]{1,0:T(8,128)(2,1)S(1)} %copy-done.38), channel_id=1, source_target_pairs={{0,2},{2,0},{1,3},{3,1},{4,6},{6,4},{5,7},{7,5},{8,10},{10,8},{9,1... | collective-permute-start | bytes 6291464 | tf_op jit(solution)/shard_map/ppermute | solution.py:543
  423.5 31.0 %collective-permute-start.42 = (bf16[2,2,2,32,1024]{4,3,2,1,0:T(8,128)(2,1)S(1)}, bf16[2,2,2,32,1024]{4,3,2,1,0:T(8,128)(2,1)S(1)}, u32[]{:S(2)}, u32[]{:S(2)}) collective-permute-start(bf16[2,2,2,32,1024]{4,3,2,1,0:T(8,128)(2,1)S(1)} %dynamic-slice_bitcast_fusion.3), channel_id=1, source_target_pairs={{0,4},{4,0},{8,12},{12,8},{16,20},{20,16},{24,28},{28,24},{1,5},{5... | collective-permute-start | bytes 1572872 | tf_op jit(solution)/shard_map/ppermute | solution.py:551
  424.1 31.9 %collective-permute-start.38 = (bf16[2,2,2,32,1024]{4,3,2,0,1:T(8,128)(2,1)S(1)}, bf16[2,2,2,32,1024]{4,3,2,0,1:T(8,128)(2,1)S(1)}, u32[]{:S(2)}, u32[]{:S(2)}) collective-permute-start(bf16[2,2,2,32,1024]{4,3,2,0,1:T(8,128)(2,1)S(1)} %dynamic-slice_bitcast_fusion.4), channel_id=1, source_target_pairs={{0,1},{1,0},{2,3},{3,2},{4,5},{5,4},{6,7},{7,6},{8,9},{9,8},{10,11... | collective-permute-start | bytes 1572872 | tf_op jit(solution)/shard_map/ppermute | solution.py:550
  518.2 102.0 %collective-permute-start.33 = (bf16[2,2,2,32,512]{4,3,0,1,2:T(8,128)(2,1)S(1)}, bf16[2,2,2,32,512]{4,3,0,1,2:T(8,128)(2,1)S(1)}, u32[]{:S(2)}, u32[]{:S(2)}) collective-permute-start(bf16[2,2,2,32,512]{4,3,0,1,2:T(8,128)(2,1)S(1)} %bitcast.334), channel_id=1, source_target_pairs={{0,1},{1,0},{2,3},{3,2},{4,5},{5,4},{6,7},{7,6},{8,9},{9,8},{10,11... | collective-permute-start | bytes 786440 | tf_op jit(solution)/shard_map/ppermute | solution.py:550
  520.1 101.4 %collective-permute-start.29 = (bf16[2,2,2,32,512]{4,3,0,1,2:T(8,128)(2,1)S(1)}, bf16[2,2,2,32,512]{4,3,0,1,2:T(8,128)(2,1)S(1)}, u32[]{:S(2)}, u32[]{:S(2)}) collective-permute-start(bf16[2,2,2,32,512]{4,3,0,1,2:T(8,128)(2,1)S(1)} %bitcast.333), channel_id=1, source_target_pairs={{0,4},{4,0},{8,12},{12,8},{16,20},{20,16},{24,28},{28,24},{1,5},{5... | collective-permute-start | bytes 786440 | tf_op jit(solution)/shard_map/ppermute | solution.py:551
  603.8 45.9 %collective-permute-start.16 = (bf16[2,2,2,2,32,512]{5,4,2,0,1,3:T(8,128)(2,1)S(1)}, bf16[2,2,2,2,32,512]{5,4,2,0,1,3:T(8,128)(2,1)S(1)}, u32[]{:S(2)}, u32[]{:S(2)}) collective-permute-start(bf16[2,2,2,2,32,512]{5,4,2,0,1,3:T(8,128)(2,1)S(1)} %bitcast.331), channel_id=1, source_target_pairs={{0,4},{4,0},{8,12},{12,8},{16,20},{20,16},{24,28},{28,24},{1,5},{5... | collective-permute-start | bytes 1572872 | tf_op jit(solution)/shard_map/ppermute | solution.py:551
  610.1 41.4 %collective-permute-start.20 = (bf16[2,2,2,2,32,512]{5,4,3,0,1,2:T(8,128)(2,1)S(1)}, bf16[2,2,2,2,32,512]{5,4,3,0,1,2:T(8,128)(2,1)S(1)}, u32[]{:S(2)}, u32[]{:S(2)}) collective-permute-start(bf16[2,2,2,2,32,512]{5,4,3,0,1,2:T(8,128)(2,1)S(1)} %bitcast.332), channel_id=1, source_target_pairs={{0,1},{1,0},{2,3},{3,2},{4,5},{5,4},{6,7},{7,6},{8,9},{9,8},{10,11... | collective-permute-start | bytes 1572872 | tf_op jit(solution)/shard_map/ppermute | solution.py:550
  610.9 41.3 %collective-permute-start.24 = (bf16[2,2,2,2,32,512]{5,4,2,0,1,3:T(8,128)(2,1)S(1)}, bf16[2,2,2,2,32,512]{5,4,2,0,1,3:T(8,128)(2,1)S(1)}, u32[]{:S(2)}, u32[]{:S(2)}) collective-permute-start(bf16[2,2,2,2,32,512]{5,4,2,0,1,3:T(8,128)(2,1)S(1)} %bitcast.330), channel_id=1, source_target_pairs={{0,4},{4,0},{8,12},{12,8},{16,20},{20,16},{24,28},{28,24},{1,5},{5... | collective-permute-start | bytes 1572872 | tf_op jit(solution)/shard_map/ppermute | solution.py:551
  620.2 48.3 %collective-permute-start.14 = (bf16[1024,1024]{1,0:T(8,128)(2,1)}, bf16[1024,1024]{1,0:T(8,128)(2,1)S(1)}, u32[]{:S(2)}, u32[]{:S(2)}) collective-permute-start(bf16[1024,1024]{1,0:T(8,128)(2,1)} %shard_map.351), channel_id=1, source_target_pairs={{0,2},{2,0},{1,3},{3,1},{4,6},{6,4},{5,7},{7,5},{8,10},{10,8},{9,1... | collective-permute-start | bytes 6291464 | tf_op jit(solution)/shard_map/ppermute | solution.py:543
  696.2 33.5 %collective-permute-start.15 = (bf16[1024,1024]{1,0:T(8,128)(2,1)}, bf16[1024,1024]{1,0:T(8,128)(2,1)}, u32[]{:S(2)}, u32[]{:S(2)}) collective-permute-start(bf16[1024,1024]{1,0:T(8,128)(2,1)} %get-tuple-element.69), channel_id=1, source_target_pairs={{0,0},{1,2},{2,1},{3,3},{4,4},{5,6},{6,5},{7,7},{8,8},{9,10},{10,9... | collective-permute-start | bytes 6291464 | tf_op jit(solution)/shard_map/ppermute | solution.py:546
  (78 other events, 955.9 us)
Sparse Core Ops, SparseCore 0:
  11.4 56.0 all-gather.7
  70.9 67.2 all-gather.5
  141.5 74.3 all-gather.9
  219.1 75.0 all-gather.11

commit v2 on v1

v2 whole, which is shorter than its diff:
```python
import functools
import math

import jax
import jax.numpy as jnp
from jax import lax
from jax.experimental import pallas as pl
from jax.experimental.pallas import tpu as pltpu
from jax.sharding import Mesh, PartitionSpec as P

HEADS = 16
HEAD_DIM = 64
BF = jnp.bfloat16
F32 = jnp.float32
EPS = 1e-05
VMEM_LIMIT = 56 << 20

rate_qkv = 0.04
rate_out = 0.03
rate_up = 0.03
rate_down = 0.02
rate_norm = 0.3

LOG2E = math.log2(math.e)
SCALE = 1.0 / math.sqrt(HEAD_DIM)
NT = (((1,), (1,)), ((), ()))
TN = (((0,), (0,)), ((), ()))


def dot(x, y, dims=None):
    if dims is None:
        return jnp.dot(x, y, preferred_element_type=F32)
    return lax.dot_general(x, y, dims, preferred_element_type=F32)


def call(body, grid, ins, outs, out_shape, args, scratch=(), scalars=0):
    return pl.pallas_call(
        body,
        grid_spec=pltpu.PrefetchScalarGridSpec(
            num_scalar_prefetch=scalars,
            grid=grid,
            in_specs=ins,
            out_specs=outs,
            scratch_shapes=scratch,
        ),
        out_shape=out_shape,
        compiler_params=pltpu.CompilerParams(
            dimension_semantics=("arbitrary",) * len(grid), vmem_limit_bytes=VMEM_LIMIT
        ),
    )(*args)


def shape(rows, cols, dtype):
    return jax.ShapeDtypeStruct((rows, cols), dtype)


def whole(x):
    zeros = (0,) * x.ndim
    return pl.BlockSpec(x.shape, lambda *_: zeros)


def ln_parts(v):
    centre = v - jnp.mean(v, axis=-1, keepdims=True)
    inv = lax.rsqrt(jnp.mean(centre * centre, axis=-1, keepdims=True) + EPS)
    return centre * inv, inv


def ln_grad(xhat, inv, gain, z):
    e = z * gain
    return (
        e - jnp.mean(e, axis=-1, keepdims=True) - xhat * jnp.mean(e * xhat, axis=-1, keepdims=True)
    ) * inv


def column_sums(z, xhat):
    return jnp.concatenate(
        [jnp.sum(z * xhat, axis=0, keepdims=True), jnp.sum(z, axis=0, keepdims=True)], axis=0
    )


def add_to(ref, value):
    @pl.when(pl.program_id(0) == 0)
    def _():
        ref[...] = value

    @pl.when(pl.program_id(0) > 0)
    def _():
        ref[...] += value


def regroup_lanes(u, size):
    lane = lax.broadcasted_iota(jnp.int32, (u.shape[0], 128), 1) % (4 * size)
    groups = []
    for start in range(0, u.shape[1], 128):
        w = u[:, start : start + 128]
        w = jnp.where(
            (lane >= size) & (lane < 2 * size),
            pltpu.roll(w, 128 - size, 1),
            jnp.where((lane >= 2 * size) & (lane < 3 * size), pltpu.roll(w, size, 1), w),
        )
        groups.append(w)
    return jnp.concatenate(groups, axis=1)


def swapped_halves(u):
    lane = lax.broadcasted_iota(jnp.int32, u.shape, 1) % HEAD_DIM
    return jnp.where(lane < HEAD_DIM // 2, pltpu.roll(u, 96, 1), pltpu.roll(u, 32, 1))


def qkv_rows(a, w, cos, sin, q_ref, k_ref, v_ref):
    width = q_ref.shape[1]
    for part, ref in enumerate((q_ref, k_ref)):
        rows = dot(a, w[:, part * width : (part + 1) * width])
        for group in range(width // 128):
            u = rows[:, group * 128 : (group + 1) * 128]
            ref[:, group * 128 : (group + 1) * 128] = (u * cos + swapped_halves(u) * sin).astype(BF)
    v_ref[...] = dot(a, w[:, 2 * width :]).astype(BF)


def first_qkv_body(
    size,
    inverse,
    own_ref,
    other_ref,
    w_ref,
    cos_ref,
    sin_ref,
    a_ref,
    q_ref,
    k_ref,
    v_ref,
):
    owners = w_ref.shape[0]
    x = jnp.where(pl.program_id(0) < 2, own_ref[...], other_ref[...])
    xhat, _ = ln_parts(x.astype(F32))
    norm = jnp.concatenate(
        [w_ref[n, 2 * size : 2 * size + 8, : 2 * size] for n in range(owners)], axis=1
    ).astype(F32)
    a = (regroup_lanes(xhat, size) * norm[0:1, :] + norm[1:2, :]).astype(BF)
    a_ref[...] = a
    w = w_ref[:, : 2 * size, :].reshape(2 * size * owners, w_ref.shape[2])
    qkv_rows(a, w, cos_ref[...], sin_ref[...], q_ref, k_ref, v_ref)


def next_qkv_body(a_ref, w_ref, cos_ref, sin_ref, q_ref, k_ref, v_ref):
    qkv_rows(a_ref[...], w_ref[...], cos_ref[...], sin_ref[...], q_ref, k_ref, v_ref)


def first_qkv(size, inverse, own, other, w_qkv, cos, sin, span):
    tokens, model = 2 * own.shape[0], own.shape[1]
    width = w_qkv.shape[2] // 3
    row = lambda cols: pl.BlockSpec((span, cols), lambda i, p: (p[i], 0))
    return call(
        functools.partial(first_qkv_body, size),
        (tokens // span,),
        [
            pl.BlockSpec((span, model), lambda i, p: (jnp.minimum(i, 1), 0)),
            pl.BlockSpec((span, model), lambda i, p: (jnp.maximum(i - 2, 0), 0)),
            whole(w_qkv),
            row(128),
            row(128),
        ],
        [row(model), row(width), row(width), row(width)],
        [shape(tokens, model, BF)] + [shape(tokens, width, BF)] * 3,
        (inverse, own, other, w_qkv, cos, sin),
        scalars=1,
    )


def next_qkv(a, w_qkv, cos, sin, span):
    tokens, model = a.shape
    width = w_qkv.shape[1] // 3
    row = lambda cols: pl.BlockSpec((span, cols), lambda i: (i, 0))
    return call(
        next_qkv_body,
        (tokens // span,),
        [row(model), whole(w_qkv), row(128), row(128)],
        [row(width)] * 3,
        [shape(tokens, width, BF)] * 3,
        (a, w_qkv, cos, sin),
    )


def head_mask(shape_):
    return lax.broadcasted_iota(jnp.int32, shape_, 1) < HEAD_DIM


def forward_body(inverse, q_ref, k_ref, v_ref, own_ref, sent_ref, lse_ref):
    span = q_ref.shape[0]
    turn_index = pl.program_id(1)
    block = inverse[turn_index]
    first = head_mask((span, 128))
    q = q_ref[...]
    zero = jnp.zeros_like(q)
    heads = (jnp.where(first, q, zero), jnp.where(first, zero, q))
    causal = lax.broadcasted_iota(jnp.int32, (span, span), 1) <= lax.broadcasted_iota(
        jnp.int32, (span, span), 0
    )

    def step(start, carry, diagonal):
        k = k_ref[pl.ds(start, span), :]
        v = v_ref[pl.ds(start, span), :]
        result = []
        for head in range(2):
            top, total, acc = carry[head]
            s = dot(heads[head], k, NT) * (SCALE * LOG2E)
            if diagonal:
                s = jnp.where(causal, s, -jnp.inf)
            new_top = jnp.maximum(top, jnp.max(s, axis=1, keepdims=True))
            p = jnp.exp2(s - new_top)
            shrink = jnp.exp2(top - new_top)
            total = total * shrink + jnp.sum(p, axis=1, keepdims=True)
            acc = acc * shrink + dot(p.astype(BF), v)
            result.append((new_top, total, acc))
        return tuple(result)

    empty = (
        jnp.full((span, 1), -1e30, F32),
        jnp.zeros((span, 1), F32),
        jnp.zeros((span, 128), F32),
    )
    carry = step(pl.multiple_of(block * span, span), (empty, empty), True)
    carry = lax.fori_loop(
        0, block, lambda i, c: step(pl.multiple_of(i * span, span), c, False), carry
    )
    (top0, total0, acc0), (top1, total1, acc1) = carry
    o = jnp.where(first, acc0 / total0, acc1 / total1).astype(BF)

    @pl.when(turn_index < 2)
    def _():
        own_ref[...] = o

    @pl.when(turn_index >= 2)
    def _():
        sent_ref[...] = o

    lse = jnp.where(first, top0 + jnp.log2(total0), top1 + jnp.log2(total1))
    turned = lse.T
    lse_ref[...] = jnp.concatenate([turned[0:8], turned[HEAD_DIM : HEAD_DIM + 8]], axis=0)


def attend_forward(inverse, q, k, v, span):
    tokens, width = q.shape
    pairs, blocks = width // 128, tokens // span
    full = pl.BlockSpec((tokens, 128), lambda h, i, p: (0, h))
    return call(
        forward_body,
        (pairs, blocks),
        [pl.BlockSpec((span, 128), lambda h, i, p: (p[i], h)), full, full],
        [
            pl.BlockSpec((span, 128), lambda h, i, p: (jnp.minimum(i, 1), h)),
            pl.BlockSpec((span, 128), lambda h, i, p: (jnp.maximum(i - 2, 0), h)),
            pl.BlockSpec((16, span), lambda h, i, p: (h, p[i])),
        ],
        [
            shape(tokens // 2, width, BF),
            shape(tokens // 2, width, BF),
            shape(16 * pairs, tokens, F32),
        ],
        (inverse, q, k, v),
        scalars=1,
    )


def backward_body(
    inverse,
    q_ref,
    k_ref,
    v_ref,
    own_ref,
    sent_ref,
    g_ref,
    lse_ref,
    cos_ref,
    sin_ref,
    dq_ref,
    dk_ref,
    dv_ref,
    dq_acc,
    inner,
    dk_acc,
    dv_acc,
):
    span = dk_ref.shape[0]
    blocks = q_ref.shape[0] // span
    key_block = pl.program_id(0)
    first = head_mask((span, 128))

    @pl.when(key_block == 0)
    def _():
        dq_acc[...] = jnp.zeros_like(dq_acc)
        for i in range(blocks):
            o_ref = own_ref if i < 2 else sent_ref
            start = pl.multiple_of(inverse[i] * span, span)
            o = o_ref[(i % 2) * span : (i % 2 + 1) * span, :].astype(F32)
            prod = (o * g_ref[pl.ds(start, span), :].astype(F32)).T
            for head in range(2):
                inner[head * 8 : head * 8 + 1, pl.ds(start, span)] = jnp.sum(
                    prod[head * HEAD_DIM : (head + 1) * HEAD_DIM], axis=0, keepdims=True
                )

    dk_acc[...] = jnp.zeros_like(dk_acc)
    dv_acc[...] = jnp.zeros_like(dv_acc)
    k = k_ref[...]
    v = v_ref[...]
    zero = jnp.zeros_like(k)
    keys = (jnp.where(first, k, zero), jnp.where(first, zero, k))
    values = (jnp.where(first, v, zero), jnp.where(first, zero, v))
    causal = lax.broadcasted_iota(jnp.int32, (span, span), 0) <= lax.broadcasted_iota(
        jnp.int32, (span, span), 1
    )

    def step(block, diagonal):
        start = pl.multiple_of(block * span, span)
        q = q_ref[pl.ds(start, span), :]
        g = g_ref[pl.ds(start, span), :]
        for head in range(2):
            mine = first if head == 0 else jnp.logical_not(first)
            lse = lse_ref[head * 8 : head * 8 + 1, pl.ds(start, span)]
            mean = inner[head * 8 : head * 8 + 1, pl.ds(start, span)]
            s = dot(keys[head], q, NT) * (SCALE * LOG2E)
            p = jnp.exp2(s - lse)
            if diagonal:
                p = jnp.where(causal, p, 0.0)
            dp = dot(values[head], g, NT)
            ds = (p * (dp - mean)).astype(BF)
            dv_acc[...] += dot(p.astype(BF), jnp.where(mine, g, zero))
            dk_acc[...] += dot(ds, jnp.where(mine, q, zero))
            dq_acc[pl.ds(start, span), :] += dot(ds, keys[head], TN)

    step(key_block, True)

    @pl.loop(key_block + 1, blocks)
    def _(block):
        step(block, False)

    start = pl.multiple_of(key_block * span, span)
    cos, sin = cos_ref[pl.ds(start, span), :], sin_ref[pl.ds(start, span), :]
    dk = dk_acc[...] * SCALE
    dk_ref[...] = (dk * cos - swapped_halves(dk) * sin).astype(BF)
    dv_ref[...] = dv_acc[...].astype(BF)
    dq = dq_acc[pl.ds(start, span), :] * SCALE
    dq_ref[...] = (dq * cos - swapped_halves(dq) * sin).astype(BF)


def attend_backward(inverse, q, k, v, own, sent, g, lse, cos, sin, span, pair, g_pair):
    tokens = q.shape[0]
    blocks = tokens // span
    full = pl.BlockSpec((tokens, 128), lambda i, p: (0, pair))
    part = pl.BlockSpec((span, 128), lambda i, p: (i, pair))
    side = pl.BlockSpec((tokens // 2, 128), lambda i, p: (0, pair))
    out = pl.BlockSpec((span, 128), lambda i, p: (i, 0))
    return call(
        backward_body,
        (blocks,),
        [
            full,
            part,
            part,
            side,
            side,
            pl.BlockSpec((tokens, 128), lambda i, p: (0, g_pair)),
            pl.BlockSpec((16, tokens), lambda i, p: (pair, 0)),
            whole(cos),
            whole(sin),
        ],
        [out, out, out],
        [shape(tokens, 128, BF)] * 3,
        (inverse, q, k, v, own, sent, g, lse, cos, sin),
        scratch=[
            pltpu.VMEM((tokens, 128), F32),
            pltpu.VMEM((16, tokens), F32),
            pltpu.VMEM((span, 128), F32),
            pltpu.VMEM((span, 128), F32),
        ],
        scalars=1,
    )


def mix_body(inverse, own_ref, other_ref, w_ref, out_ref):
    index = pl.program_id(0)

    @pl.when(index < 2)
    def _():
        out_ref[...] = dot(own_ref[...], w_ref[...], NT).astype(BF)

    @pl.when(index >= 2)
    def _():
        out_ref[...] = dot(other_ref[...], w_ref[...], NT).astype(BF)


def mix_gradient(inverse, own, other, w_out, span):
    model = own.shape[1]
    width = w_out.shape[0]
    return call(
        mix_body,
        (4,),
        [
            pl.BlockSpec((span, model), lambda i, p: (jnp.minimum(i, 1), 0)),
            pl.BlockSpec((span, model), lambda i, p: (jnp.maximum(i - 2, 0), 0)),
            whole(w_out),
        ],
        pl.BlockSpec((span, width), lambda i, p: (p[i], 0)),
        shape(4 * span, width, BF),
        (inverse, own, other, w_out),
        scalars=1,
    )


def project_body(
    size, m0_ref, m1_ref, o0_ref, o1_ref, wm_ref, wo_ref, x_ref, norm_ref, a_ref, h_ref, c_ref
):
    half = m0_ref.shape[1]
    a = (
        dot(m0_ref[...], wm_ref[:half, :])
        + dot(m1_ref[...], wm_ref[half:, :])
        + dot(o0_ref[...], wo_ref[:half, :])
        + dot(o1_ref[...], wo_ref[half:, :])
    )
    a_ref[...] = a
    xhat, _ = ln_parts(a)
    h = x_ref[...].astype(F32) + (xhat * norm_ref[2:3, :] + norm_ref[3:4, :])
    h_ref[...] = h
    hhat, _ = ln_parts(h)
    c_ref[...] = regroup_lanes(hhat * norm_ref[4:5, :] + norm_ref[5:6, :], size).astype(BF)


def project(size, mine, other, w_mine, w_other, x, norm, rows=256):
    tokens, model = x.shape
    row = lambda cols: pl.BlockSpec((rows, cols), lambda i: (i, 0))
    half = row(mine[0].shape[1])
    return call(
        functools.partial(project_body, size),
        (tokens // rows,),
        [half] * 4 + [whole(w_mine), whole(w_other), row(model), whole(norm)],
        [row(model)] * 3,
        [shape(tokens, model, F32), shape(tokens, model, F32), shape(tokens, model, BF)],
        (*mine, *other, w_mine, w_other, x, norm),
    )


def turn_body(m_ref, r_ref, h_ref, y_ref, norm_ref, out_ref, dm_ref, sums_ref):
    xhat, inv = ln_parts(m_ref[...] + r_ref[...].astype(F32))
    gain = norm_ref[6:7, :]
    out_ref[...] = (h_ref[...] + (xhat * gain + norm_ref[7:8, :])).astype(BF)
    z = y_ref[...].astype(F32)
    dm_ref[...] = ln_grad(xhat, inv, gain, z).astype(BF)
    add_to(sums_ref, column_sums(z, xhat))


def turn(m_part, m_other, h, y, norm, rows=256):
    tokens, model = y.shape
    row = pl.BlockSpec((rows, model), lambda i: (i, 0))
    return call(
        turn_body,
        (tokens // rows,),
        [row, row, row, row, whole(norm)],
        [row, row, pl.BlockSpec((2, model), lambda i: (0, 0))],
        [shape(tokens, model, BF), shape(tokens, model, BF), shape(2, model, F32)],
        (m_part, m_other, h, y, norm),
    )


def descend_body(
    size, dc_ref, r_ref, h_ref, a_ref, y_ref, norm_ref, dh_ref, da_ref, sums3_ref, sums2_ref
):
    dc = regroup_lanes(dc_ref[...] + r_ref[...].astype(F32), size)
    hhat, inv = ln_parts(h_ref[...])
    dh = y_ref[...].astype(F32) + ln_grad(hhat, inv, norm_ref[4:5, :], dc)
    dh_ref[...] = dh
    add_to(sums3_ref, column_sums(dc, hhat))
    ahat, inv = ln_parts(a_ref[...])
    da_ref[...] = ln_grad(ahat, inv, norm_ref[2:3, :], dh).astype(BF)
    add_to(sums2_ref, column_sums(dh, ahat))


def descend(size, dc_part, dc_other, h, a, y, norm, rows=256):
    tokens, model = y.shape
    row = pl.BlockSpec((rows, model), lambda i: (i, 0))
    sums = pl.BlockSpec((2, model), lambda i: (0, 0))
    return call(
        functools.partial(descend_body, size),
        (tokens // rows,),
        [row] * 5 + [whole(norm)],
        [row, row, sums, sums],
        [
            shape(tokens, model, F32),
            shape(tokens, model, BF),
            shape(2, model, F32),
            shape(2, model, F32),
        ],
        (dc_part, dc_other, h, a, y, norm),
    )


def up_down_body(c_ref, wu_ref, wd_ref, g_ref, s_ref, m_ref, acc):
    u = dot(c_ref[...], wu_ref[...])
    k = math.sqrt(2.0 / math.pi)
    square = u * u
    t = jnp.tanh(u * (k + (k * 0.044715) * square))
    half = 0.5 + 0.5 * t
    g = (u * half).astype(BF)
    g_ref[...] = g
    s_ref[...] = (
        half + (0.5 * u) * (1.0 - t * t) * (k + (3.0 * k * 0.044715) * square)
    ).astype(BF)
    add_to(acc, dot(g, wd_ref[...]))

    @pl.when(pl.program_id(0) == pl.num_programs(0) - 1)
    def _():
        m_ref[...] = acc[...].astype(m_ref.dtype)


def up_down(c, w_up, w_down, dtype, cols=512):
    tokens, model = c.shape
    units = 2 * model
    wide = pl.BlockSpec((tokens, cols), lambda i: (0, i))
    specs = [
        pl.BlockSpec((model, cols), lambda i: (0, i)),
        pl.BlockSpec((cols, model), lambda i: (i, 0)),
    ]
    return call(
        up_down_body,
        (units // cols,),
        [whole(c)] + specs,
        [wide, wide, pl.BlockSpec((tokens, model), lambda i: (0, 0))],
        [shape(tokens, units, BF), shape(tokens, units, BF), shape(tokens, model, dtype)],
        (c, w_up, w_down),
        scratch=[pltpu.VMEM((tokens, model), F32)],
    )


def down_up_body(dm_ref, s_ref, wu_ref, wd_ref, du_ref, dc_ref, acc):
    du = (dot(dm_ref[...], wd_ref[...], NT) * s_ref[...].astype(F32)).astype(BF)
    du_ref[...] = du
    add_to(acc, dot(du, wu_ref[...], NT))

    @pl.when(pl.program_id(0) == pl.num_programs(0) - 1)
    def _():
        dc_ref[...] = acc[...].astype(dc_ref.dtype)


def down_up(dm, slope, w_up, w_down, dtype, cols=512):
    tokens, model = dm.shape
    units = 2 * model
    wide = pl.BlockSpec((tokens, cols), lambda i: (0, i))
    specs = [
        pl.BlockSpec((model, cols), lambda i: (0, i)),
        pl.BlockSpec((cols, model), lambda i: (i, 0)),
    ]
    return call(
        down_up_body,
        (units // cols,),
        [whole(dm), wide] + specs,
        [wide, pl.BlockSpec((tokens, model), lambda i: (0, 0))],
        [shape(tokens, units, BF), shape(tokens, model, dtype)],
        (dm, slope, w_up, w_down),
        scratch=[pltpu.VMEM((tokens, model), F32)],
    )


def other_body(inverse, d0_ref, d1_ref, w0_ref, w1_ref, out_ref):
    out_ref[...] = (dot(d0_ref[...], w0_ref[...], NT) + dot(d1_ref[...], w1_ref[...], NT)).astype(BF)


def own_body(
    size, inverse, d0_ref, d1_ref, w0_ref, w1_ref, r_ref, x_ref, dh_ref, norm_ref, out_ref, sums_ref
):
    z = dot(d0_ref[...], w0_ref[...], NT) + dot(d1_ref[...], w1_ref[...], NT)
    z = regroup_lanes(z + r_ref[...].astype(F32), size)
    xhat, inv = ln_parts(x_ref[...].astype(F32))
    out_ref[...] = (dh_ref[...] + ln_grad(xhat, inv, norm_ref[0:1, :], z)).astype(BF)
    add_to(sums_ref, column_sums(z, xhat))


def input_other(inverse, d, w, span):
    width, model = d[0].shape[1], w[0].shape[0]
    part = pl.BlockSpec((span, width), lambda i, p: (p[i + 2], 0))
    return call(
        other_body,
        (2,),
        [part, part, whole(w[0]), whole(w[1])],
        pl.BlockSpec((span, model), lambda i, p: (i, 0)),
        shape(2 * span, model, BF),
        (inverse, *d, *w),
        scalars=1,
    )


def input_own(size, inverse, d, w, recv, x, dh, norm, span):
    width, model = d[0].shape[1], w[0].shape[0]
    part = pl.BlockSpec((span, width), lambda i, p: (p[i], 0))
    row = pl.BlockSpec((span, model), lambda i, p: (i, 0))
    return call(
        functools.partial(own_body, size),
        (2,),
        [part, part, whole(w[0]), whole(w[1]), row, row, row, whole(norm)],
        [row, pl.BlockSpec((2, model), lambda i, p: (0, 0))],
        [shape(2 * span, model, BF), shape(2, model, F32)],
        (inverse, *d, *w, recv, x, dh, norm),
        scalars=1,
    )


def nesterov(gradient, momentum, weight, average, step_rate, token_total):
    scaled = gradient / token_total
    new_momentum = 0.5 * momentum + scaled
    new_weight = weight - step_rate * math.sqrt(token_total) * (scaled + 0.5 * new_momentum)
    new_average = 0.5 * average + 0.5 * new_weight
    return (new_momentum, new_weight, new_average)


def tie(*values):
    return lax.optimization_barrier(values)


def per_device(
    tokens,
    cotangent,
    pair_order,
    qkv_weight,
    qkv_momentum,
    qkv_average,
    out_weight,
    out_momentum,
    out_average,
    up_weight,
    up_momentum,
    up_average,
    down_weight,
    down_momentum,
    down_average,
    norm_weight,
    norm_momentum,
    norm_average,
):
    chips = lax.axis_size("chip")
    ctx_count = lax.axis_size("ctx")
    assert ctx_count == 2 and pair_order.shape[0] == 1 and chips & (chips - 1) == 0
    levels = chips.bit_length() - 1
    chip, core, side = lax.axis_index("chip"), lax.axis_index("core"), lax.axis_index("ctx")
    count, model = tokens.shape
    span = count // 2
    token_total = count * chips * 4
    half = model // 2
    part_heads = HEADS // 4
    rows = qkv_weight.shape[0]
    units = down_weight.shape[0]
    flip = [(0, 1), (1, 0)]

    everyone = ("chip", "core", "ctx")
    full_order = list(range(levels - 1, -1, -1)) + ["core", "ctx"]
    mask_of = {"ctx": 1, "core": 2, **{n: 4 << n for n in range(levels)}}

    def exchange(x, mask):
        return lax.ppermute(x, everyone, [(i, i ^ mask) for i in range(4 * chips)])

    def to_core(x):
        return exchange(x, mask_of["core"])

    def swap_begin(x):
        return lax.ppermute(x, ("core", "ctx"), [(1, 2), (2, 1)])

    def swap_end(x, moved):
        return jnp.where(core == side, x, moved)

    def bit_of(level):
        if level == "ctx":
            return side
        if level == "core":
            return core
        return (chip >> level) & 1

    def pick(x, index, dim):
        return lax.dynamic_index_in_dim(x, index, dim, keepdims=False)

    def by_bit(bit, mine, other, axis=0):
        return jnp.stack(
            [jnp.where(bit == 0, mine, other), jnp.where(bit == 0, other, mine)], axis=axis
        )

    def masks(step):
        result = [0]
        for level in step:
            result = [m for old in result for m in (old, old | mask_of[level])]
        return result

    class Gather:
        def __init__(self, value, steps):
            self.value, self.names, self.steps = value, [], list(steps)

        def send(self):
            self.moved = [exchange(self.value, m) for m in masks(self.steps[0])[1:]]

        def join(self):
            parts = [self.value] + self.moved
            for level in reversed(self.steps.pop(0)):
                dim = sum(full_order.index(n) < full_order.index(level) for n in self.names)
                self.names.insert(dim, level)
                parts = [
                    by_bit(bit_of(level), parts[n], parts[n + 1], dim)
                    for n in range(0, len(parts), 2)
                ]
            (self.value,) = parts

    def tied(gathers, attribute, *rest):
        values, rest = tie([getattr(g, attribute) for g in gathers], rest)
        for g, v in zip(gathers, values):
            setattr(g, attribute, v)
        return rest

    high = list(range(1, levels))
    chain = high[::-1]
    far_steps = [tuple(chain[n : n + 2]) for n in range(0, len(chain), 2)]
    reduce_orders = (
        [(n,) for n in [0, "ctx"] + high],
        [(n,) for n in ["ctx", 0] + high],
    )
    chain = [0, "ctx"] + high
    short_order = [tuple(chain[n : n + 2]) for n in range(0, len(chain), 2)]
    chain = ["core", "ctx", 0] + high
    small_order = [tuple(chain[n : n + 2]) for n in range(0, len(chain), 2)]

    w = qkv_weight.astype(BF).reshape(rows, 3, 2, part_heads, 2, HEAD_DIM)
    norm_low = norm_weight.astype(BF)
    qkv_moved, norm_moved = to_core(pick(w, 1 - core, 4)), to_core(norm_low)
    local = by_bit(core, pick(w, core, 4), qkv_moved).transpose(3, 0, 1, 2, 4, 5)
    local = local.reshape(2, 2 * rows, -1)
    norm_local = jnp.pad(
        by_bit(core, norm_low, norm_moved, 1).reshape(8, -1), ((0, 0), (0, local.shape[2] - 2 * rows))
    )
    w_local = out_weight.astype(BF).reshape(rows, 2, half).transpose(1, 0, 2).reshape(2 * rows, half)
    first = Gather(
        jnp.concatenate([local[0], norm_local], axis=0), far_steps + [("ctx",), (0,)]
    )
    second = Gather(
        jnp.concatenate([local[1], w_local], axis=1), far_steps + [("ctx",), (0,)]
    )

    def join_all(gathers, *rest):
        rest = tied(gathers, "moved", *rest)
        for gather in gathers:
            gather.join()
        return tied(gathers, "value", *rest)

    def send_all(gathers):
        for gather in gathers:
            gather.send()

    first.send()
    positions = jnp.arange(2 * count, dtype=jnp.int32)
    positions, w, tokens_out, order_row = join_all(
        [first], positions, up_weight, tokens, pair_order
    )
    tied([first, second], "value")
    for _ in far_steps[1:]:
        send_all([first, second])
        join_all([first, second])
    send_all([first] + [second] * (len(far_steps) == 1))
    x_moved = swap_begin(tokens_out)
    w = w.astype(BF).reshape(rows, chips, 2, 2 * units)
    up_moved = to_core(pick(w, 1 - core, 2))
    order_row = jnp.where(core == side, order_row, to_core(order_row))[0]
    mine_first = pick(order_row, core, 0) == 0
    inverse = jnp.where(
        mine_first, jnp.array([0, 3, 1, 2], jnp.int32), jnp.array([1, 2, 0, 3], jnp.int32)
    )
    steps = jnp.arange(HEAD_DIM // 2, dtype=F32)
    frequency = jnp.exp(steps * (-math.log(10000.0) / (HEAD_DIM // 2)))
    angles = positions.astype(F32)[:, None] * frequency[None, :]
    cos, sin = jnp.cos(angles), jnp.sin(angles)
    cos_table = jnp.concatenate([cos] * 4, axis=1)
    sin_table = jnp.concatenate([-sin, sin] * 2, axis=1)
    local = by_bit(core, pick(w, core, 2).reshape(rows, 2, -1), up_moved.reshape(rows, 2, -1))
    wide = Gather(local.reshape(2 * rows, -1), far_steps)
    down_low = down_weight.astype(BF)
    cos_table, sin_table, inverse, down_low, wide.value, x_moved = join_all(
        [first] + [second] * (len(far_steps) == 1),
        cos_table,
        sin_table,
        inverse,
        down_low,
        wide.value,
        x_moved,
    )
    send_all([first, second, wide])
    w_down = lax.all_gather(down_low, ("chip", "ctx"), axis=0, tiled=True)
    x = swap_end(tokens, x_moved)
    x_other = to_core(x)
    for _ in far_steps[1:]:
        join_all([wide])
        wide.send()
    (x_other,) = join_all([first, second, wide], x_other)

    cut = wide.value.shape[-1] // 2
    ups = []
    for n in range(2):
        gather = Gather(wide.value[..., n * cut : (n + 1) * cut], [("ctx",), (0,)][:: 1 - 2 * n])
        gather.names = list(wide.names)
        ups.append(gather)
    x_other, y_out = tied([second] + ups, "value", x_other, cotangent)
    send_all([second] + ups)

    a, q0, k0, v0 = first_qkv(
        rows,
        inverse,
        x,
        x_other,
        first.value.reshape(2 * chips, 2 * rows + 8, -1),
        cos_table,
        sin_table,
        span,
    )
    gathered = first.value.reshape(2 * chips, 2 * rows + 8, -1)
    w_first = gathered[:, : 2 * rows].reshape(model, -1)
    norm = gathered[:, 2 * rows :, : 2 * rows].reshape(chips, 2, 8, 2, rows)
    norm = norm.transpose(2, 0, 3, 1, 4).reshape(8, model).astype(F32)
    q0, y_out = tie(q0, y_out)
    y_moved = swap_begin(y_out)
    own0, sent0, lse0 = attend_forward(inverse, q0, k0, v0, span)
    own0, sent0, a = join_all([second] + ups, own0, sent0, a)
    send_all(ups)
    while second.steps:
        second.send()
        own0, sent0, a = join_all([second], own0, sent0, a)
    w_rest = second.value.reshape(chips * 2, 2 * rows, -1)
    w_second = w_rest[..., :-half].reshape(model, -1)
    w_out = (
        w_rest[..., -half:]
        .reshape(chips * 2, 2, rows, half)
        .transpose(0, 2, 1, 3)
        .reshape(half, model)
    )
    w_qkv = (w_first, w_second)
    w_out_other = to_core(w_out)
    recv0 = to_core(sent0)
    q1, k1, v1 = next_qkv(a, w_second, cos_table, sin_table, span)
    own1, sent1, lse1 = attend_forward(inverse, q1, k1, v1, span)
    own1, sent1, y_moved = join_all(ups, own1, sent1, y_moved)
    w_up = jnp.concatenate([gather.value for gather in ups], axis=-1).reshape(model, -1)
    y = swap_end(cotangent, y_moved)
    recv1 = to_core(sent1)
    projected, hidden, c = project(
        rows, (own0, own1), (recv0, recv1), w_out, w_out_other, x, norm
    )
    c_other = to_core(c)
    g_other, slope_other, m_sent = up_down(c_other, w_up, w_down, BF)
    m_recv = to_core(m_sent)
    g_mine, slope_mine, m_part = up_down(c, w_up, w_down, F32)
    output, dm, sums4 = turn(m_part, m_recv, hidden, y, norm)
    output_moved = swap_begin(output)

    class Reduction:
        def __init__(self, value, names, order, wire):
            self.value, self.names, self.order, self.wire = value, names, list(order), wire
            self.flying = False

        def split(self):
            parts = [self.value]
            names = list(self.names)
            for level in self.order[0]:
                dim, bit = names.index(level), bit_of(level)
                names.pop(dim)
                parts = [pick(p, b, dim) for p in parts for b in (bit, 1 - bit)]
            self.names = names
            self.kept, self.moved = parts[0], parts[1:]

        def send(self):
            step = self.order.pop(0)
            self.moved = [exchange(p, m) for p, m in zip(self.moved, masks(step)[1:])]
            self.flying = True

        def add(self):
            v = sum([p.astype(F32) for p in self.moved], self.kept.astype(F32))
            self.value = v.astype(self.wire) if self.order else v
            self.flying = False

    def collect(flying, main):
        flying = [r for r in flying if r.flying]
        moved, main = tie([r.moved for r in flying], main)
        for r, m in zip(flying, moved):
            r.moved = m
            r.add()
        return main

    def launch(started, main):
        started = [r for r in started if r.order and not r.flying]
        for r in started:
            r.split()
        moved, main = tie([r.moved for r in started], main)
        for r, m in zip(started, moved):
            r.moved = m
            r.send()
        return main

    def slot(flying, started, main):
        return launch(flying + started, collect(flying, main))

    row_names = [n for n in full_order if n != "core"]

    def by_rows(g):
        return g.reshape((2,) * (levels + 1) + (-1, g.shape[1]))

    def halves(g):
        cut = g.shape[1] // 2
        g = by_rows(g)
        return [
            Reduction(g[..., n * cut : (n + 1) * cut], row_names, reduce_orders[n], BF)
            for n in range(2)
        ]

    def joined(pair):
        return jnp.concatenate([r.value for r in pair], axis=-1)

    dm_other = to_core(dm)
    du_mine, dc_part = down_up(dm, slope_mine, w_up, w_down, F32)
    du_other, dc_sent = down_up(dm_other, slope_other, w_up, w_down, BF)
    du_other, dc_sent, dc_part, output_moved = tie(du_other, dc_sent, dc_part, output_moved)
    output = swap_end(output, output_moved)
    dc_recv = to_core(dc_sent)
    g_two = jnp.concatenate([g_mine, g_other], axis=0)
    dm_two = jnp.concatenate([dm, dm_other], axis=0)
    down_grad = dot(g_two, dm_two, TN).astype(BF)
    down = halves(down_grad)
    du_mine, du_other = launch(down, (du_mine, du_other))
    c_two = jnp.concatenate([c, c_other], axis=0)
    du_two = jnp.concatenate([du_mine, du_other], axis=0)
    up_grad, dc_part = tie(dot(c_two, du_two, TN).astype(BF), dc_part)
    up = halves(up_grad)
    dh, da, sums3, sums2 = descend(rows, dc_part, dc_recv, hidden, projected, y, norm)
    da = slot(down, up, da)
    da_other = to_core(da)
    do = mix_gradient(inverse, da, da_other, w_out, span)
    da_two = jnp.concatenate([da, da_other], axis=0)
    o_two = jnp.concatenate(
        [jnp.concatenate([own0, own1], axis=1), jnp.concatenate([sent0, sent1], axis=1)], axis=0
    )
    out_grad, do = tie(dot(o_two, da_two, TN).astype(BF), do)
    out = [Reduction(by_rows(out_grad), row_names, reduce_orders[1], BF)]

    def attention_gradient(pair, do):
        q, k, v, own, sent, lse = (
            (q0, k0, v0, own0, sent0, lse0) if pair < 2 else (q1, k1, v1, own1, sent1, lse1)
        )
        return attend_backward(
            inverse, q, k, v, own, sent, do, lse, cos_table, sin_table, span, pair % 2, pair
        )

    def weave(first, second):
        return jnp.concatenate([t for pair in zip(first, second) for t in pair], axis=1)

    d0 = attention_gradient(0, do)
    do, d0 = slot(down, [], (do, d0))
    d1 = attention_gradient(1, do)
    do, d1 = slot(down + up, out, (do, d1))
    d_first = weave(d0, d1)
    qkv_first = [
        Reduction(by_rows(dot(a, d_first, TN).astype(BF)), row_names, reduce_orders[0], BF)
    ]
    do = launch(qkv_first, do)
    d2 = attention_gradient(2, do)
    do, d2 = slot(down + up, [], (do, d2))
    d3 = attention_gradient(3, do)
    d_second = weave(d2, d3)
    qkv_second = [Reduction(by_rows(dot(a, d_second, TN).astype(BF)), row_names, short_order, BF)]
    d_second = launch(qkv_second, d_second)
    d = (d_first, d_second)
    dx_sent = slot(down + up + out + qkv_first, [], input_other(inverse, d, w_qkv, span))
    dx_recv = to_core(dx_sent)
    dx_recv = slot(down + up + out + qkv_first, [], dx_recv)
    input_grad, sums1 = input_own(rows, inverse, d, w_qkv, dx_recv, x, dh, norm, span)
    norm_grad = jnp.concatenate([sums1, sums2, sums3, sums4], axis=0)
    share = norm_grad.reshape((8,) + (2,) * (levels + 2) + (rows,))
    share = Reduction(
        jnp.moveaxis(share, 0, levels + 2), full_order, small_order, F32
    )
    everything = down + up + out + qkv_first + qkv_second + [share]
    input_moved = swap_begin(input_grad)
    sums1 = slot(everything[:-1], [share], sums1)
    while any(r.flying for r in everything):
        sums1 = slot(everything, [], sums1)
        sums1, input_moved = tie(sums1, input_moved)
    input_grad = swap_end(input_grad, input_moved)

    def from_cores(part):
        return by_bit(core, pick(part, core, 0), to_core(pick(part, 1 - core, 0)))

    down_sum = joined(down).reshape(units, model)
    out_sum = out[0].value.reshape(rows, model)
    up_part = joined(up).reshape(2, rows, chips, 2 * units)
    up_sum = from_cores(up_part).transpose(1, 2, 0, 3).reshape(rows, -1)
    qkv_part = jnp.stack(
        [p[0].value.reshape(2, rows, 3, part_heads, HEAD_DIM) for p in (qkv_first, qkv_second)],
        axis=3,
    )
    qkv_sum = from_cores(qkv_part).transpose(1, 2, 3, 4, 0, 5).reshape(rows, -1)
    qkv_new = nesterov(qkv_sum, qkv_momentum, qkv_weight, qkv_average, rate_qkv, token_total)
    out_new = nesterov(out_sum, out_momentum, out_weight, out_average, rate_out, token_total)
    up_new = nesterov(up_sum, up_momentum, up_weight, up_average, rate_up, token_total)
    down_new = nesterov(down_sum, down_momentum, down_weight, down_average, rate_down, token_total)
    norm_new = nesterov(share.value, norm_momentum, norm_weight, norm_average, rate_norm, token_total)
    return (output, input_grad, *qkv_new, *out_new, *up_new, *down_new, *norm_new)


def solution(mesh):
    dp, ctx = mesh.shape["dp"], mesh.shape["ctx"]
    inner = Mesh(mesh.devices.reshape(dp // 2, 2, ctx), ("chip", "core", "ctx"))
    rows = P(("chip", "core", "ctx"), None)
    cols = P(None, ("chip", "core", "ctx"))
    return jax.shard_map(
        per_device,
        mesh=inner,
        in_specs=(rows, rows, P(("chip", "core"), None)) + (rows,) * 12 + (cols,) * 3,
        out_specs=(rows,) * 14 + (cols,) * 3,
        check_vma=False,
    )
```

time: 755 us -> 629 us (0.83); the launches traced: 741 us -> 626 us
  waiting for transfers between devices: 185 us -> 68.8 us
  blocking collectives: 66.2 us -> 0 us
  Pallas kernels: 261 us -> 295 us
  other arithmetic: 34.2 us -> 66 us
    all_gather x1 -> x0, blocking collectives: 66.2 us -> none  [per_device(): lax.all_gather(norm_weight.astype(BF), ('chip', 'core', 'ctx'), axis=1, t...]
    all_gather x4 -> x1, waiting for transfers between devices: 65.9 us -> 0.01 us  [per_device(): w_down = lax.all_gather(down_low, ('chip', 'ctx'), axis=0, tiled=True)]
    ppermute x59 -> x74, waiting for transfers between devices: 119 us -> 68.8 us  [the longest x70 60.7 us: exchange(): return lax.ppermute(x, everyone, [(i, i ^ mask) for i in range(4 * chips)])]
    pallas_call x12 -> x18, Pallas kernels: 261 us -> 295 us  [call(): pl.pallas_call(body, grid_spec=pltpu.PrefetchScalarGridSpec(num_scalar_pr...]
    another operation x4 -> x30, other arithmetic: 0.08 us -> 14.8 us  [by_bit(): jnp.stack([jnp.where(bit == 0, mine, other), jnp.where(bit == 0, other, m...]
    squeeze x30 -> x26, local copies, waits for them, and re-layouts: 1.69 us -> 11.5 us  [pick(): return lax.dynamic_index_in_dim(x, index, dim, keepdims=False)]
    select_n x4 -> x9, other arithmetic: 2.59 us -> 11.6 us  [the longest x4 11.4 us: swap_end(): return jnp.where(core == side, x, moved)]
    transpose x2 -> x1, local copies, waits for them, and re-layouts: 8.59 us -> 0.01 us  [per_device(): out_weight.astype(BF).reshape(rows, 2, half).transpose(1, 0, 2)]
  transfers between devices with their start and end apart: 63 -> 75, of which waited for: 25 -> 15; matrix products, arithmetic and copies ran while one was open for 13% -> 18% of each run, Pallas kernels for 33% -> 43%
where the time goes in v2:
time: 629 us; the launch traced here: 626 us
  Pallas kernels  295 us (47%)
  starting transfers between devices  94.7 us (15%)
  waiting for transfers between devices  68.8 us (11%)
  other arithmetic  66 us (10%)
  local copies, waits for them, and re-layouts  47.2 us (8%)
  matrix products  37.4 us (6%)
  between operations  16.3 us (3%)
    pallas_call x18, Pallas kernels, call(): pl.pallas_call(body, grid_spec=pltpu.PrefetchScalarGridSpec(num_scalar_pr...  295 us
    ppermute x70, starting transfers between devices, exchange(): return lax.ppermute(x, everyone, [(i, i ^ mask) for i in range(4 * chips)])  76.3 us
    ppermute x70, waiting for transfers between devices, exchange(): return lax.ppermute(x, everyone, [(i, i ^ mask) for i in range(4 * chips)])  60.7 us
    dot_general x5, matrix products, dot(): return lax.dot_general(x, y, dims, preferred_element_type=F32)  37.4 us
    ppermute x4, starting transfers between devices, swap_begin(): return lax.ppermute(x, ('core', 'ctx'), [(1, 2), (2, 1)])  18.3 us
    unnamed x199, local copies, waits for them, and re-layouts  16.1 us
    another operation x30, other arithmetic, by_bit(): jnp.stack([jnp.where(bit == 0, mine, other), jnp.where(bit == 0, other, m...  14.8 us
  transfers between devices with their start and end apart: 75, of which 15 were waited for; matrix products, arithmetic and copies ran while one was open for 18% of the time, Pallas kernels for 43%

profile of v2, /device:TPU:1, one launch (start us, length us, event | category | flops | bytes accessed | tf_op | source)
XLA Modules:
  0.0 625.6 jit_solution(11764129789664173311)
XLA Ops:
  53.8 10.7 %collective-permute-done.5 = bf16[2,2,72,768]{3,2,1,0:T(8,128)(2,1)} collective-permute-done((bf16[2,2,72,768]{3,2,1,0:T(8,128)(2,1)S(1)}, bf16[2,2,72,768]{3,2,1,0:T(8,128)(2,1)}, u32[]{:S(2)}, u32[]{:S(2)}) %collective-permute-start.5) | collective-permute-done | bytes 442400 | tf_op jit(solution)/shard_map/ppermute | solution.py:656
  75.1 10.4 %collective-permute-done.14 = bf16[64,2048]{1,0:T(8,128)(2,1)S(1)} collective-permute-done((bf16[64,2048]{1,0:T(8,128)(2,1)S(1)}, bf16[64,2048]{1,0:T(8,128)(2,1)S(1)}, u32[]{:S(2)}, u32[]{:S(2)}) %collective-permute-start.14) | collective-permute-done | bytes 262176 | tf_op jit(solution)/shard_map/ppermute | solution.py:656
  103.3 14.4 %shard_map.323 = (bf16[2048,1024]{1,0:T(8,128)(2,1)}, bf16[2048,256]{1,0:T(8,128)(2,1)}, bf16[2048,256]{1,0:T(8,128)(2,1)}, bf16[2048,256]{1,0:T(8,128)(2,1)}) custom-call(s32[4]{0:T(128)} %broadcast_select_fusion.12.inverse, bf16[1024,1024]{1,0:T(8,128)(2,1)} %copy-done, bf16[1024,1024]{1,0:T(8,128)(2,1)} %collective-permute-done.17.other_ref, ...), custom_call_target="tpu_custom_call" | custom-call | tf_op jit(solution)/shard_map/pallas_call | solution.py:37
  123.6 29.4 %shard_map.324 = (bf16[1024,256]{1,0:T(8,128)(2,1)}, bf16[1024,256]{1,0:T(8,128)(2,1)}, f32[32,2048]{1,0:T(8,128)}) custom-call(s32[4]{0:T(128)} %broadcast_select_fusion.12.inverse, bf16[2048,256]{1,0:T(8,128)(2,1)} %get-tuple-element.296.q_ref, bf16[2048,256]{1,0:T(8,128)(2,1)} %get-tuple-element.297.k_ref, bf16[2048,256]{1,0:T(8,128)(2,1)} %get-tuple-element.298.v_ref), custom_call_target="tpu_custom_call" | custom-call | tf_op jit(solution)/shard_map/pallas_call | solution.py:37
  163.0 8.0 %shard_map.325 = (bf16[2048,256]{1,0:T(8,128)(2,1)}, bf16[2048,256]{1,0:T(8,128)(2,1)}, bf16[2048,256]{1,0:T(8,128)(2,1)}) custom-call(bf16[2048,1024]{1,0:T(8,128)(2,1)} %get-tuple-element.311.a_ref, bf16[1024,768]{1,0:T(8,128)(2,1)} %bitcast.354, f32[2048,128]{1,0:T(8,128)} %pad_maximum_fusion.6.cos_ref, f32[2048,128]{1,0:T(8,128)} %pad_maximum_fusion.7.sin_ref), custom_call_target="tpu_custom_call" | custom-call | tf_op jit(solution)/shard_map/pallas_call | solution.py:37
  171.0 29.4 %shard_map.326 = (bf16[1024,256]{1,0:T(8,128)(2,1)}, bf16[1024,256]{1,0:T(8,128)(2,1)}, f32[32,2048]{1,0:T(8,128)}) custom-call(s32[4]{0:T(128)} %broadcast_select_fusion.12.inverse, bf16[2048,256]{1,0:T(8,128)(2,1)} %get-tuple-element.313.q_ref, bf16[2048,256]{1,0:T(8,128)(2,1)} %get-tuple-element.314.k_ref, bf16[2048,256]{1,0:T(8,128)(2,1)} %get-tuple-element.315.v_ref), custom_call_target="tpu_custom_call" | custom-call | tf_op jit(solution)/shard_map/pallas_call | solution.py:37
  207.3 9.4 %shard_map.327 = (f32[1024,1024]{1,0:T(8,128)}, f32[1024,1024]{1,0:T(8,128)}, bf16[1024,1024]{1,0:T(8,128)(2,1)}) custom-call(bf16[1024,256]{1,0:T(8,128)(2,1)} %get-tuple-element.308.m0_ref.own_ref, bf16[1024,256]{1,0:T(8,128)(2,1)} %get-tuple-element.324.m1_ref.own_ref, bf16[1024,256]{1,0:T(8,128)(2,1)} %collective-permute-done.24.o0_ref, ...), custom_call_target="tpu_custom_call" | custom-call | tf_op jit(solution)/shard_map/pallas_call | solution.py:37
  221.2 17.9 %shard_map.329 = (bf16[1024,2048]{1,0:T(8,128)(2,1)}, bf16[1024,2048]{1,0:T(8,128)(2,1)}, bf16[1024,1024]{1,0:T(8,128)(2,1)}) custom-call(bf16[1024,1024]{1,0:T(8,128)(2,1)} %collective-permute-done.27.c_ref, bf16[1024,2048]{1,0:T(8,128)(2,1)} %bitcast.350, bf16[2048,1024]{1,0:T(8,128)(2,1)} %all-gather.2.cloned.1.call-done.wd_ref), custom_call_target="tpu_custom_call" | custom-call | tf_op jit(solution)/shard_map/pallas_call | solution.py:37
  242.7 18.6 %shard_map.328 = (bf16[1024,2048]{1,0:T(8,128)(2,1)}, bf16[1024,2048]{1,0:T(8,128)(2,1)}, f32[1024,1024]{1,0:T(8,128)}) custom-call(bf16[1024,1024]{1,0:T(8,128)(2,1)} %get-tuple-element.327.c_ref, bf16[1024,2048]{1,0:T(8,128)(2,1)} %bitcast.351, bf16[2048,1024]{1,0:T(8,128)(2,1)} %all-gather.2.cloned.1.call-done.wd_ref), custom_call_target="tpu_custom_call" | custom-call | tf_op jit(solution)/shard_map/pallas_call | solution.py:37
  262.6 8.6 %shard_map.330 = (bf16[1024,1024]{1,0:T(8,128)(2,1)}, bf16[1024,1024]{1,0:T(8,128)(2,1)}, f32[2,1024]{1,0:T(2,128)}) custom-call(f32[1024,1024]{1,0:T(8,128)} %get-tuple-element.331.m_ref, bf16[1024,1024]{1,0:T(8,128)(2,1)} %copy-done.27, f32[1024,1024]{1,0:T(8,128)} %get-tuple-element.333.h_ref, bf16[1024,1024]{1,0:T(8,128)(2,1)} %broadcast_select_fusion.2.y_ref, ...), custom_call_target="tpu_custom_call" | custom-call | tf_op jit(solution)/shard_map/pallas_call | solution.py:37
  274.7 17.5 %shard_map.332 = (bf16[1024,2048]{1,0:T(8,128)(2,1)}, f32[1024,1024]{1,0:T(8,128)}) custom-call(bf16[1024,1024]{1,0:T(8,128)(2,1)} %get-tuple-element.336.dm_ref, bf16[1024,2048]{1,0:T(8,128)(2,1)} %get-tuple-element.340.s_ref, bf16[1024,2048]{1,0:T(8,128)(2,1)} %bitcast.352, bf16[2048,1024]{1,0:T(8,128)(2,1)} %all-gather.2.cloned.1.call-done.wd_ref), custom_call_target="tpu_custom_call" | custom-call | tf_op jit(solution)/shard_map/pallas_call | solution.py:37
  292.1 12.1 %fusion.23 = bf16[2048,1024]{1,0:T(8,128)(2,1)S(1)} fusion(bf16[1024,1024]{1,0:T(8,128)(2,1)} %collective-permute-done.29.dm_ref, bf16[1024,1024]{1,0:T(8,128)(2,1)S(1)} %copy-done.21, bf16[1024,2048]{1,0:T(8,128)(2,1)} %get-tuple-element.344, bf16[1024,2048]{1,0:T(8,128)(2,1)} %get-tuple-element.343), kind=kOutput, calls=%fused_computation.20 | convolution fusion | flops 8617197568 | bytes 16777216 | tf_op jit(solution)/shard_map/dot_general | solution.py:33
  307.2 16.0 %shard_map.331 = (bf16[1024,2048]{1,0:T(8,128)(2,1)}, bf16[1024,1024]{1,0:T(8,128)(2,1)}) custom-call(bf16[1024,1024]{1,0:T(8,128)(2,1)} %collective-permute-done.29.dm_ref, bf16[1024,2048]{1,0:T(8,128)(2,1)} %get-tuple-element.337.s_ref, bf16[1024,2048]{1,0:T(8,128)(2,1)} %bitcast.353, bf16[2048,1024]{1,0:T(8,128)(2,1)} %all-gather.2.cloned.1.call-done.wd_ref), custom_call_target="tpu_custom_call" | custom-call | tf_op jit(solution)/shard_map/pallas_call | solution.py:37
  325.1 12.3 %fusion.18 = bf16[1024,2048]{1,0:T(8,128)(2,1)S(1)} fusion(bf16[1024,2048]{1,0:T(8,128)(2,1)} %get-tuple-element.350, bf16[1024,2048]{1,0:T(8,128)(2,1)} %get-tuple-element.349, bf16[1024,1024]{1,0:T(8,128)(2,1)} %collective-permute-done.27.c_ref, bf16[1024,1024]{1,0:T(8,128)(2,1)S(1)} %copy-done.20), kind=kOutput, calls=%fused_computation.19 | convolution fusion | flops 8617197568 | bytes 16777216 | tf_op jit(solution)/shard_map/dot_general | solution.py:33
  341.2 12.7 %shard_map.333 = (f32[1024,1024]{1,0:T(8,128)}, bf16[1024,1024]{1,0:T(8,128)(2,1)}, f32[2,1024]{1,0:T(2,128)}, f32[2,1024]{1,0:T(2,128)}) custom-call(f32[1024,1024]{1,0:T(8,128)} %get-tuple-element.352.dc_ref, bf16[1024,1024]{1,0:T(8,128)(2,1)} %collective-permute-done.33.r_ref, f32[1024,1024]{1,0:T(8,128)} %get-tuple-element.333.h_ref, ...), custom_call_target="tpu_custom_call" | custom-call | tf_op jit(solution)/shard_map/pallas_call | solution.py:37
  376.9 21.3 %shard_map.335 = (bf16[2048,128]{1,0:T(8,128)(2,1)}, bf16[2048,128]{1,0:T(8,128)(2,1)}, bf16[2048,128]{1,0:T(8,128)(2,1)}) custom-call(s32[4]{0:T(128)} %broadcast_select_fusion.12.inverse, bf16[2048,256]{1,0:T(8,128)(2,1)} %get-tuple-element.296.q_ref, bf16[2048,256]{1,0:T(8,128)(2,1)} %get-tuple-element.297.k_ref, ...), custom_call_target="tpu_custom_call" | custom-call | tf_op jit(solution)/shard_map/pallas_call | solution.py:37
  398.7 10.3 %collective-permute-start.37 = (bf16[2,128,512]{2,1,0:T(8,128)(2,1)S(1)}, bf16[2,128,512]{2,1,0:T(8,128)(2,1)S(1)}, u32[]{:S(2)}, u32[]{:S(2)}) collective-permute-start(bf16[2,128,512]{2,1,0:T(8,128)(2,1)S(1)} %dynamic-slice_bitcast_fusion.16), channel_id=1, source_target_pairs={{0,8},{1,9},{2,10},{3,11},{4,12},{5,13},{6,14},{7,15},{8,0},{9,1},... | collective-permute-start | bytes 786440 | tf_op jit(solution)/shard_map/ppermute | solution.py:656
  409.1 21.5 %shard_map.336 = (bf16[2048,128]{1,0:T(8,128)(2,1)}, bf16[2048,128]{1,0:T(8,128)(2,1)}, bf16[2048,128]{1,0:T(8,128)(2,1)}) custom-call(s32[4]{0:T(128)} %broadcast_select_fusion.12.inverse, bf16[2048,256]{1,0:T(8,128)(2,1)} %get-tuple-element.296.q_ref, bf16[2048,256]{1,0:T(8,128)(2,1)} %get-tuple-element.297.k_ref, ...), custom_call_target="tpu_custom_call" | custom-call | tf_op jit(solution)/shard_map/pallas_call | solution.py:37
  448.5 21.0 %shard_map.337 = (bf16[2048,128]{1,0:T(8,128)(2,1)}, bf16[2048,128]{1,0:T(8,128)(2,1)}, bf16[2048,128]{1,0:T(8,128)(2,1)}) custom-call(s32[4]{0:T(128)} %broadcast_select_fusion.12.inverse, bf16[2048,256]{1,0:T(8,128)(2,1)} %get-tuple-element.313.q_ref, bf16[2048,256]{1,0:T(8,128)(2,1)} %get-tuple-element.314.k_ref, ...), custom_call_target="tpu_custom_call" | custom-call | tf_op jit(solution)/shard_map/pallas_call | solution.py:37
  471.7 21.3 %shard_map.338 = (bf16[2048,128]{1,0:T(8,128)(2,1)}, bf16[2048,128]{1,0:T(8,128)(2,1)}, bf16[2048,128]{1,0:T(8,128)(2,1)}) custom-call(s32[4]{0:T(128)} %broadcast_select_fusion.12.inverse, bf16[2048,256]{1,0:T(8,128)(2,1)} %get-tuple-element.313.q_ref, bf16[2048,256]{1,0:T(8,128)(2,1)} %get-tuple-element.314.k_ref, ...), custom_call_target="tpu_custom_call" | custom-call | tf_op jit(solution)/shard_map/pallas_call | solution.py:37
  502.9 7.7 %shard_map.339 = bf16[1024,1024]{1,0:T(8,128)(2,1)} custom-call(s32[4]{0:T(128)} %broadcast_select_fusion.12.inverse, bf16[2048,768]{1,0:T(8,128)(2,1)} %copy-done.2, bf16[2048,768]{1,0:T(8,128)(2,1)} %copy-done.3, bf16[1024,768]{1,0:T(8,128)(2,1)} %bitcast.360, bf16[1024,768]{1,0:T(8,128)(2,1)} %bitcast.355), custom_call_target="tpu_custom_call" | custom-call | tf_op jit(solution)/shard_map/pallas_call | solution.py:37
  527.8 7.7 %collective-permute-done.49 = bf16[64,1024]{1,0:T(8,128)(2,1)S(1)} collective-permute-done((bf16[64,1024]{1,0:T(8,128)(2,1)S(1)}, bf16[64,1024]{1,0:T(8,128)(2,1)S(1)}, u32[]{:S(2)}, u32[]{:S(2)}) %collective-permute-start.49) | collective-permute-done | bytes 131104 | tf_op jit(solution)/shard_map/ppermute | solution.py:656
  541.3 13.2 %shard_map.340 = (bf16[1024,1024]{1,0:T(8,128)(2,1)}, f32[2,1024]{1,0:T(2,128)}) custom-call(s32[4]{0:T(128)} %broadcast_select_fusion.12.inverse, bf16[2048,768]{1,0:T(8,128)(2,1)} %copy-done.2, bf16[2048,768]{1,0:T(8,128)(2,1)} %copy-done.3, bf16[1024,768]{1,0:T(8,128)(2,1)} %bitcast.361, bf16[1024,768]{1,0:T(8,128)(2,1)} %bitcast.356, ...), custom_call_target="tpu_custom_call" | custom-call | tf_op jit(solution)/shard_map/pallas_call | solution.py:37
  607.2 8.1 %collective-permute-done.54 = bf16[1024,1024]{1,0:T(8,128)(2,1)} collective-permute-done((bf16[1024,1024]{1,0:T(8,128)(2,1)S(1)}, bf16[1024,1024]{1,0:T(8,128)(2,1)}, u32[]{:S(2)}, u32[]{:S(2)}) %collective-permute-start.54) | collective-permute-done | bytes 2097184 | tf_op jit(solution)/shard_map/ppermute | solution.py:662
  (513 shorter events, 249.6 us)
Async XLA Ops:
  7.2 214.0 %all-gather.2.cloned.1.call-start = ((), (), s32[]{:S(2)}) async-start(), calls=%async_computation | async-start | bytes 4456448 | tf_op jit(solution)/shard_map/all_gather | solution.py:787
  26.7 37.7 %collective-permute-start.11 = (bf16[1024,1024]{1,0:T(8,128)(2,1)S(1)}, bf16[1024,1024]{1,0:T(8,128)(2,1)}, u32[]{:S(2)}, u32[]{:S(2)}) collective-permute-start(bf16[1024,1024]{1,0:T(8,128)(2,1)S(1)} %copy-done.16), channel_id=1, source_target_pairs={{1,2},{2,1},{5,6},{6,5},{9,10},{10,9},{13,14},{14,13},{17,18},{18,... | collective-permute-start | bytes 6291464 | tf_op jit(solution)/shard_map/ppermute | solution.py:662
  100.0 52.9 %collective-permute-start.18 = (bf16[2,2,2,64,1280]{4,3,1,0,2:T(8,128)(2,1)S(1)}, bf16[2,2,2,64,1280]{4,3,1,0,2:T(8,128)(2,1)S(1)}, u32[]{:S(2)}, u32[]{:S(2)}) collective-permute-start(bf16[2,2,2,64,1280]{4,3,1,0,2:T(8,128)(2,1)S(1)} %pad_maximum_fusion.5), channel_id=1, source_target_pairs={{0,4},{1,5},{2,6},{3,7},{4,0},{5,1},{6,2},{7,3},{8,12},{9,13},{10,... | collective-permute-start | bytes 3932168 | tf_op jit(solution)/shard_map/ppermute | solution.py:656
  100.4 52.6 %collective-permute-start.19 = (bf16[2,2,64,1024]{3,2,1,0:T(8,128)(2,1)S(1)}, bf16[2,2,64,1024]{3,2,1,0:T(8,128)(2,1)S(1)}, u32[]{:S(2)}, u32[]{:S(2)}) collective-permute-start(bf16[2,2,64,1024]{3,2,1,0:T(8,128)(2,1)S(1)} %get-tuple-element.287), channel_id=1, source_target_pairs={{0,1},{1,0},{2,3},{3,2},{4,5},{5,4},{6,7},{7,6},{8,9},{9,8},{10,11... | collective-permute-start | bytes 1572872 | tf_op jit(solution)/shard_map/ppermute | solution.py:656
  100.8 52.2 %collective-permute-start.20 = (bf16[2,2,64,1024]{3,2,1,0:T(8,128)(2,1)S(1)}, bf16[2,2,64,1024]{3,2,1,0:T(8,128)(2,1)S(1)}, u32[]{:S(2)}, u32[]{:S(2)}) collective-permute-start(bf16[2,2,64,1024]{3,2,1,0:T(8,128)(2,1)S(1)} %get-tuple-element.288), channel_id=1, source_target_pairs={{0,4},{1,5},{2,6},{3,7},{4,0},{5,1},{6,2},{7,3},{8,12},{9,13},{10,... | collective-permute-start | bytes 1572872 | tf_op jit(solution)/shard_map/ppermute | solution.py:656
  117.7 82.7 %collective-permute-start.23 = (bf16[1024,1024]{1,0:T(8,128)(2,1)}, bf16[1024,1024]{1,0:T(8,128)(2,1)}, u32[]{:S(2)}, u32[]{:S(2)}) collective-permute-start(bf16[1024,1024]{1,0:T(8,128)(2,1)} %param.21), channel_id=1, source_target_pairs={{1,2},{2,1},{5,6},{6,5},{9,10},{10,9},{13,14},{14,13},{17,18},{18,... | collective-permute-start | bytes 6291464 | tf_op jit(solution)/shard_map/ppermute | solution.py:662
  153.8 46.6 %collective-permute-start.21 = (bf16[2,2,2,64,1024]{4,3,1,0,2:T(8,128)(2,1)S(1)}, bf16[2,2,2,64,1024]{4,3,1,0,2:T(8,128)(2,1)S(1)}, u32[]{:S(2)}, u32[]{:S(2)}) collective-permute-start(bf16[2,2,2,64,1024]{4,3,1,0,2:T(8,128)(2,1)S(1)} %pad_maximum_fusion.9), channel_id=1, source_target_pairs={{0,4},{1,5},{2,6},{3,7},{4,0},{5,1},{6,2},{7,3},{8,12},{9,13},{10,... | collective-permute-start | bytes 3145736 | tf_op jit(solution)/shard_map/ppermute | solution.py:656
  154.1 46.3 %collective-permute-start.22 = (bf16[2,2,2,64,1024]{4,3,2,1,0:T(8,128)(2,1)S(1)}, bf16[2,2,2,64,1024]{4,3,2,1,0:T(8,128)(2,1)S(1)}, u32[]{:S(2)}, u32[]{:S(2)}) collective-permute-start(bf16[2,2,2,64,1024]{4,3,2,1,0:T(8,128)(2,1)S(1)} %pad_maximum_fusion.10), channel_id=1, source_target_pairs={{0,1},{1,0},{2,3},{3,2},{4,5},{5,4},{6,7},{7,6},{8,9},{9,8},{10,11... | collective-permute-start | bytes 3145736 | tf_op jit(solution)/shard_map/ppermute | solution.py:656
  157.1 50.1 %collective-permute-start.26 = (bf16[512,1024]{1,0:T(8,128)(2,1)S(1)}, bf16[512,1024]{1,0:T(8,128)(2,1)}, u32[]{:S(2)}, u32[]{:S(2)}) collective-permute-start(bf16[512,1024]{1,0:T(8,128)(2,1)S(1)} %bitcast.364), channel_id=1, source_target_pairs={{0,2},{1,3},{2,0},{3,1},{4,6},{5,7},{6,4},{7,5},{8,10},{9,11},{10,... | collective-permute-start | bytes 3145736 | tf_op jit(solution)/shard_map/ppermute | solution.py:656
  162.9 44.4 %collective-permute-start.24 = (bf16[1024,256]{1,0:T(8,128)(2,1)}, bf16[1024,256]{1,0:T(8,128)(2,1)}, u32[]{:S(2)}, u32[]{:S(2)}) collective-permute-start(bf16[1024,256]{1,0:T(8,128)(2,1)} %get-tuple-element.325.sent_ref), channel_id=1, source_target_pairs={{0,2},{1,3},{2,0},{3,1},{4,6},{5,7},{6,4},{7,5},{8,10},{9,11},{10,... | collective-permute-start | bytes 1572872 | tf_op jit(solution)/shard_map/ppermute | solution.py:656
  271.4 51.8 %collective-permute-start.30 = (bf16[1024,1024]{1,0:T(8,128)(2,1)}, bf16[1024,1024]{1,0:T(8,128)(2,1)}, u32[]{:S(2)}, u32[]{:S(2)}) collective-permute-start(bf16[1024,1024]{1,0:T(8,128)(2,1)} %get-tuple-element.335), channel_id=1, source_target_pairs={{1,2},{2,1},{5,6},{6,5},{9,10},{10,9},{13,14},{14,13},{17,18},{18,... | collective-permute-start | bytes 6291464 | tf_op jit(solution)/shard_map/ppermute | solution.py:662
  323.3 30.6 %collective-permute-start.31 = (bf16[2,2,2,128,512]{4,3,0,1,2:T(8,128)(2,1)}, bf16[2,2,2,128,512]{4,3,0,1,2:T(8,128)(2,1)S(1)}, u32[]{:S(2)}, u32[]{:S(2)}) collective-permute-start(bf16[2,2,2,128,512]{4,3,0,1,2:T(8,128)(2,1)} %bitcast.379), channel_id=1, source_target_pairs={{0,4},{1,5},{2,6},{3,7},{4,0},{5,1},{6,2},{7,3},{8,12},{9,13},{10,... | collective-permute-start | bytes 3145736 | tf_op jit(solution)/shard_map/ppermute | solution.py:656
  324.3 29.6 %collective-permute-start.32 = (bf16[2,2,2,128,512]{4,3,0,1,2:T(8,128)(2,1)}, bf16[2,2,2,128,512]{4,3,0,1,2:T(8,128)(2,1)}, u32[]{:S(2)}, u32[]{:S(2)}) collective-permute-start(bf16[2,2,2,128,512]{4,3,0,1,2:T(8,128)(2,1)} %bitcast.378), channel_id=1, source_target_pairs={{0,1},{1,0},{2,3},{3,2},{4,5},{5,4},{6,7},{7,6},{8,9},{9,8},{10,11... | collective-permute-start | bytes 3145736 | tf_op jit(solution)/shard_map/ppermute | solution.py:656
  361.2 37.1 %collective-permute-start.34 = (bf16[2,2,128,512]{3,2,0,1:T(8,128)(2,1)S(1)}, bf16[2,2,128,512]{3,2,0,1:T(8,128)(2,1)S(1)}, u32[]{:S(2)}, u32[]{:S(2)}) collective-permute-start(bf16[2,2,128,512]{3,2,0,1:T(8,128)(2,1)S(1)} %copy-done.63), channel_id=1, source_target_pairs={{0,1},{1,0},{2,3},{3,2},{4,5},{5,4},{6,7},{7,6},{8,9},{9,8},{10,11... | collective-permute-start | bytes 1572872 | tf_op jit(solution)/shard_map/ppermute | solution.py:656
  362.3 36.0 %collective-permute-start.35 = (bf16[2,2,128,512]{3,2,0,1:T(8,128)(2,1)S(1)}, bf16[2,2,128,512]{3,2,0,1:T(8,128)(2,1)S(1)}, u32[]{:S(2)}, u32[]{:S(2)}) collective-permute-start(bf16[2,2,128,512]{3,2,0,1:T(8,128)(2,1)S(1)} %copy-done.62), channel_id=1, source_target_pairs={{0,4},{1,5},{2,6},{3,7},{4,0},{5,1},{6,2},{7,3},{8,12},{9,13},{10,... | collective-permute-start | bytes 1572872 | tf_op jit(solution)/shard_map/ppermute | solution.py:656
  362.8 68.0 %collective-permute-start.39 = (bf16[2,2,2,64,1024]{4,3,0,1,2:T(8,128)(2,1)}, bf16[2,2,2,64,1024]{4,3,0,1,2:T(8,128)(2,1)S(1)}, u32[]{:S(2)}, u32[]{:S(2)}) collective-permute-start(bf16[2,2,2,64,1024]{4,3,0,1,2:T(8,128)(2,1)} %bitcast.336), channel_id=1, source_target_pairs={{0,4},{1,5},{2,6},{3,7},{4,0},{5,1},{6,2},{7,3},{8,12},{9,13},{10,... | collective-permute-start | bytes 3145736 | tf_op jit(solution)/shard_map/ppermute | solution.py:656
  363.8 67.1 %collective-permute-start.40 = (bf16[2,2,2,64,1024]{4,3,2,1,0:T(8,128)(2,1)S(1)}, bf16[2,2,2,64,1024]{4,3,2,1,0:T(8,128)(2,1)}, u32[]{:S(2)}, u32[]{:S(2)}) collective-permute-start(bf16[2,2,2,64,1024]{4,3,2,1,0:T(8,128)(2,1)S(1)} %copy-done.33), channel_id=1, source_target_pairs={{0,1},{1,0},{2,3},{3,2},{4,5},{5,4},{6,7},{7,6},{8,9},{9,8},{10,11... | collective-permute-start | bytes 3145736 | tf_op jit(solution)/shard_map/ppermute | solution.py:656
  398.7 32.2 %collective-permute-start.37 = (bf16[2,128,512]{2,1,0:T(8,128)(2,1)S(1)}, bf16[2,128,512]{2,1,0:T(8,128)(2,1)S(1)}, u32[]{:S(2)}, u32[]{:S(2)}) collective-permute-start(bf16[2,128,512]{2,1,0:T(8,128)(2,1)S(1)} %dynamic-slice_bitcast_fusion.16), channel_id=1, source_target_pairs={{0,8},{1,9},{2,10},{3,11},{4,12},{5,13},{6,14},{7,15},{8,0},{9,1},... | collective-permute-start | bytes 786440 | tf_op jit(solution)/shard_map/ppermute | solution.py:656
  436.7 33.2 %collective-permute-start.43 = (bf16[2,2,64,1024]{3,2,0,1:T(8,128)(2,1)}, bf16[2,2,64,1024]{3,2,0,1:T(8,128)(2,1)S(1)}, u32[]{:S(2)}, u32[]{:S(2)}) collective-permute-start(bf16[2,2,64,1024]{3,2,0,1:T(8,128)(2,1)} %dynamic-slice_bitcast_fusion.3), channel_id=1, source_target_pairs={{0,1},{1,0},{2,3},{3,2},{4,5},{5,4},{6,7},{7,6},{8,9},{9,8},{10,11... | collective-permute-start | bytes 1572872 | tf_op jit(solution)/shard_map/ppermute | solution.py:656
  438.1 31.8 %collective-permute-start.44 = (bf16[2,2,64,1024]{3,2,1,0:T(8,128)(2,1)}, bf16[2,2,64,1024]{3,2,1,0:T(8,128)(2,1)}, u32[]{:S(2)}, u32[]{:S(2)}) collective-permute-start(bf16[2,2,64,1024]{3,2,1,0:T(8,128)(2,1)} %dynamic-slice_bitcast_fusion.2), channel_id=1, source_target_pairs={{0,4},{1,5},{2,6},{3,7},{4,0},{5,1},{6,2},{7,3},{8,12},{9,13},{10,... | collective-permute-start | bytes 1572872 | tf_op jit(solution)/shard_map/ppermute | solution.py:656
  442.9 26.6 %collective-permute-start.41 = (bf16[128,512]{1,0:T(8,128)(2,1)S(1)}, bf16[128,512]{1,0:T(8,128)(2,1)S(1)}, u32[]{:S(2)}, u32[]{:S(2)}) collective-permute-start(bf16[128,512]{1,0:T(8,128)(2,1)S(1)} %dynamic-slice_bitcast_fusion.22), channel_id=1, source_target_pairs={{0,16},{1,17},{2,18},{3,19},{4,20},{5,21},{6,22},{7,23},{8,24},{9,... | collective-permute-start | bytes 393224 | tf_op jit(solution)/shard_map/ppermute | solution.py:656
  447.4 63.3 %collective-permute-start.48 = (bf16[2,2,2,64,768]{4,3,2,1,0:T(8,128)(2,1)S(1)}, bf16[2,2,2,64,768]{4,3,2,1,0:T(8,128)(2,1)S(1)}, u32[]{:S(2)}, u32[]{:S(2)}) collective-permute-start(bf16[2,2,2,64,768]{4,3,2,1,0:T(8,128)(2,1)S(1)} %dynamic-slice_bitcast_fusion.1), channel_id=1, source_target_pairs={{0,4},{1,5},{2,6},{3,7},{4,0},{5,1},{6,2},{7,3},{8,12},{9,13},{10,... | collective-permute-start | bytes 2359304 | tf_op jit(solution)/shard_map/ppermute | solution.py:656
  469.5 41.1 %collective-permute-start.47 = (bf16[2,2,2,32,1024]{4,3,0,1,2:T(8,128)(2,1)S(1)}, bf16[2,2,2,32,1024]{4,3,0,1,2:T(8,128)(2,1)S(1)}, u32[]{:S(2)}, u32[]{:S(2)}) collective-permute-start(bf16[2,2,2,32,1024]{4,3,0,1,2:T(8,128)(2,1)S(1)} %bitcast.389), channel_id=1, source_target_pairs={{0,1},{1,0},{2,3},{3,2},{4,5},{5,4},{6,7},{7,6},{8,9},{9,8},{10,11... | collective-permute-start | bytes 1572872 | tf_op jit(solution)/shard_map/ppermute | solution.py:656
  587.9 27.4 %collective-permute-start.54 = (bf16[1024,1024]{1,0:T(8,128)(2,1)S(1)}, bf16[1024,1024]{1,0:T(8,128)(2,1)}, u32[]{:S(2)}, u32[]{:S(2)}) collective-permute-start(bf16[1024,1024]{1,0:T(8,128)(2,1)S(1)} %copy-done.19), channel_id=1, source_target_pairs={{1,2},{2,1},{5,6},{6,5},{9,10},{10,9},{13,14},{14,13},{17,18},{18,... | collective-permute-start | bytes 6291464 | tf_op jit(solution)/shard_map/ppermute | solution.py:662
  (140 other events, 1334.3 us)
Sparse Core Ops, SparseCore 0:
  87.5 95.5 all-gather.1

commit v3 on v2

--- a/solution.py
+++ b/solution.py
@@ -134,12 +134,18 @@
     x = jnp.where(pl.program_id(0) < 2, own_ref[...], other_ref[...])
     xhat, _ = ln_parts(x.astype(F32))
     norm = jnp.concatenate(
-        [w_ref[n, 2 * size : 2 * size + 8, : 2 * size] for n in range(owners)], axis=1
+        [
+            w_ref[n + side, 2 * size : 2 * size + 8, core * size : (core + 1) * size]
+            for n in range(0, owners, 2)
+            for core in range(2)
+            for side in range(2)
+        ],
+        axis=1,
     ).astype(F32)
-    a = (regroup_lanes(xhat, size) * norm[0:1, :] + norm[1:2, :]).astype(BF)
+    a = (xhat * norm[0:1, :] + norm[1:2, :]).astype(BF)
     a_ref[...] = a
     w = w_ref[:, : 2 * size, :].reshape(2 * size * owners, w_ref.shape[2])
-    qkv_rows(a, w, cos_ref[...], sin_ref[...], q_ref, k_ref, v_ref)
+    qkv_rows(regroup_lanes(a, size), w, cos_ref[...], sin_ref[...], q_ref, k_ref, v_ref)
 
 
 def next_qkv_body(a_ref, w_ref, cos_ref, sin_ref, q_ref, k_ref, v_ref):
@@ -185,85 +191,63 @@
     return lax.broadcasted_iota(jnp.int32, shape_, 1) < HEAD_DIM
 
 
-def forward_body(inverse, q_ref, k_ref, v_ref, own_ref, sent_ref, lse_ref):
-    span = q_ref.shape[0]
-    turn_index = pl.program_id(1)
-    block = inverse[turn_index]
+def forward_body(place, q_ref, k_ref, v_ref, own_ref, sent_ref, lse_ref):
+    span = own_ref.shape[0] // 2
     first = head_mask((span, 128))
-    q = q_ref[...]
-    zero = jnp.zeros_like(q)
-    heads = (jnp.where(first, q, zero), jnp.where(first, zero, q))
-    causal = lax.broadcasted_iota(jnp.int32, (span, span), 1) <= lax.broadcasted_iota(
-        jnp.int32, (span, span), 0
-    )
-
-    def step(start, carry, diagonal):
-        k = k_ref[pl.ds(start, span), :]
-        v = v_ref[pl.ds(start, span), :]
-        result = []
+    causal = lax.broadcasted_iota(jnp.int32, (span, span), 0) <= lax.broadcasted_iota(
+        jnp.int32, (span, span), 1
+    )
+    turned = v_ref[...].T
+    for block in range(k_ref.shape[0] // span):
+        rows = slice(block * span, (block + 1) * span)
+        q = q_ref[rows, :]
+        zero = jnp.zeros_like(q)
+        heads = []
         for head in range(2):
-            top, total, acc = carry[head]
-            s = dot(heads[head], k, NT) * (SCALE * LOG2E)
-            if diagonal:
-                s = jnp.where(causal, s, -jnp.inf)
-            new_top = jnp.maximum(top, jnp.max(s, axis=1, keepdims=True))
-            p = jnp.exp2(s - new_top)
-            shrink = jnp.exp2(top - new_top)
-            total = total * shrink + jnp.sum(p, axis=1, keepdims=True)
-            acc = acc * shrink + dot(p.astype(BF), v)
-            result.append((new_top, total, acc))
-        return tuple(result)
-
-    empty = (
-        jnp.full((span, 1), -1e30, F32),
-        jnp.zeros((span, 1), F32),
-        jnp.zeros((span, 128), F32),
-    )
-    carry = step(pl.multiple_of(block * span, span), (empty, empty), True)
-    carry = lax.fori_loop(
-        0, block, lambda i, c: step(pl.multiple_of(i * span, span), c, False), carry
-    )
-    (top0, total0, acc0), (top1, total1, acc1) = carry
-    o = jnp.where(first, acc0 / total0, acc1 / total1).astype(BF)
-
-    @pl.when(turn_index < 2)
-    def _():
-        own_ref[...] = o
-
-    @pl.when(turn_index >= 2)
-    def _():
-        sent_ref[...] = o
-
-    lse = jnp.where(first, top0 + jnp.log2(total0), top1 + jnp.log2(total1))
-    turned = lse.T
-    lse_ref[...] = jnp.concatenate([turned[0:8], turned[HEAD_DIM : HEAD_DIM + 8]], axis=0)
-
-
-def attend_forward(inverse, q, k, v, span):
+            mine = jnp.where(first, q, zero) if head == 0 else jnp.where(first, zero, q)
+            s = dot(k_ref[: rows.stop, :], mine, NT) * (SCALE * LOG2E)
+            diagonal = jnp.where(causal, s[rows.start :], -jnp.inf)
+            s = jnp.concatenate([s[: rows.start], diagonal], axis=0) if block else diagonal
+            top = jnp.max(s, axis=0, keepdims=True)
+            p = jnp.exp2(s - top)
+            total = jnp.sum(p, axis=0, keepdims=True)
+            lanes = slice(head * HEAD_DIM, (head + 1) * HEAD_DIM)
+            heads.append(dot(turned[lanes, : rows.stop], p.astype(BF)) / total)
+            lse_ref[head * 8 : head * 8 + 1, rows] = top + jnp.log2(total)
+        o = jnp.concatenate(heads, axis=0).T.astype(BF)
+        at = place[block]
+
+        @pl.when(at < 2)
+        def _():
+            own_ref[pl.ds(pl.multiple_of(at * span, span), span), :] = o
+
+        @pl.when(at >= 2)
+        def _():
+            sent_ref[pl.ds(pl.multiple_of((at - 2) * span, span), span), :] = o
+
+
+def attend_forward(place, q, k, v):
     tokens, width = q.shape
-    pairs, blocks = width // 128, tokens // span
-    full = pl.BlockSpec((tokens, 128), lambda h, i, p: (0, h))
+    pairs = width // 128
+    full = pl.BlockSpec((tokens, 128), lambda h, p: (0, h))
+    half = pl.BlockSpec((tokens // 2, 128), lambda h, p: (0, h))
     return call(
         forward_body,
-        (pairs, blocks),
-        [pl.BlockSpec((span, 128), lambda h, i, p: (p[i], h)), full, full],
-        [
-            pl.BlockSpec((span, 128), lambda h, i, p: (jnp.minimum(i, 1), h)),
-            pl.BlockSpec((span, 128), lambda h, i, p: (jnp.maximum(i - 2, 0), h)),
-            pl.BlockSpec((16, span), lambda h, i, p: (h, p[i])),
-        ],
+        (pairs,),
+        [full, full, full],
+        [half, half, pl.BlockSpec((16, tokens), lambda h, p: (h, 0))],
         [
             shape(tokens // 2, width, BF),
             shape(tokens // 2, width, BF),
             shape(16 * pairs, tokens, F32),
         ],
-        (inverse, q, k, v),
+        (place, q, k, v),
         scalars=1,
     )
 
 
 def backward_body(
-    inverse,
+    place,
     q_ref,
     k_ref,
     v_ref,
@@ -276,103 +260,71 @@
     dq_ref,
     dk_ref,
     dv_ref,
-    dq_acc,
-    inner,
     dk_acc,
     dv_acc,
 ):
-    span = dk_ref.shape[0]
-    blocks = q_ref.shape[0] // span
-    key_block = pl.program_id(0)
-    first = head_mask((span, 128))
-
-    @pl.when(key_block == 0)
-    def _():
-        dq_acc[...] = jnp.zeros_like(dq_acc)
-        for i in range(blocks):
-            o_ref = own_ref if i < 2 else sent_ref
-            start = pl.multiple_of(inverse[i] * span, span)
-            o = o_ref[(i % 2) * span : (i % 2 + 1) * span, :].astype(F32)
-            prod = (o * g_ref[pl.ds(start, span), :].astype(F32)).T
-            for head in range(2):
-                inner[head * 8 : head * 8 + 1, pl.ds(start, span)] = jnp.sum(
-                    prod[head * HEAD_DIM : (head + 1) * HEAD_DIM], axis=0, keepdims=True
-                )
-
+    span = own_ref.shape[0] // 2
+    rows = span // 2
+    first = head_mask((rows, 128))
+    zero = jnp.zeros((rows, 128), BF)
+    causal = lax.broadcasted_iota(jnp.int32, (rows, rows), 0) <= lax.broadcasted_iota(
+        jnp.int32, (rows, rows), 1
+    )
+    turned = k_ref[...].T
     dk_acc[...] = jnp.zeros_like(dk_acc)
     dv_acc[...] = jnp.zeros_like(dv_acc)
-    k = k_ref[...]
-    v = v_ref[...]
-    zero = jnp.zeros_like(k)
-    keys = (jnp.where(first, k, zero), jnp.where(first, zero, k))
-    values = (jnp.where(first, v, zero), jnp.where(first, zero, v))
-    causal = lax.broadcasted_iota(jnp.int32, (span, span), 0) <= lax.broadcasted_iota(
-        jnp.int32, (span, span), 1
-    )
-
-    def step(block, diagonal):
-        start = pl.multiple_of(block * span, span)
-        q = q_ref[pl.ds(start, span), :]
-        g = g_ref[pl.ds(start, span), :]
+    for block in range(q_ref.shape[0] // rows):
+        here = slice(block * rows, (block + 1) * rows)
+        q, g = q_ref[here, :], g_ref[here, :]
+        at = place[block * rows // span]
+        start = pl.multiple_of((at % 2) * span + block * rows % span, rows)
+        o = jnp.where(at < 2, own_ref[pl.ds(start, rows), :], sent_ref[pl.ds(start, rows), :])
+        prod = (o.astype(F32) * g.astype(F32)).T
+        parts = []
         for head in range(2):
-            mine = first if head == 0 else jnp.logical_not(first)
-            lse = lse_ref[head * 8 : head * 8 + 1, pl.ds(start, span)]
-            mean = inner[head * 8 : head * 8 + 1, pl.ds(start, span)]
-            s = dot(keys[head], q, NT) * (SCALE * LOG2E)
-            p = jnp.exp2(s - lse)
-            if diagonal:
-                p = jnp.where(causal, p, 0.0)
-            dp = dot(values[head], g, NT)
-            ds = (p * (dp - mean)).astype(BF)
-            dv_acc[...] += dot(p.astype(BF), jnp.where(mine, g, zero))
-            dk_acc[...] += dot(ds, jnp.where(mine, q, zero))
-            dq_acc[pl.ds(start, span), :] += dot(ds, keys[head], TN)
-
-    step(key_block, True)
-
-    @pl.loop(key_block + 1, blocks)
-    def _(block):
-        step(block, False)
-
-    start = pl.multiple_of(key_block * span, span)
-    cos, sin = cos_ref[pl.ds(start, span), :], sin_ref[pl.ds(start, span), :]
+            lanes = slice(head * HEAD_DIM, (head + 1) * HEAD_DIM)
+            q_mine = jnp.where(first, q, zero) if head == 0 else jnp.where(first, zero, q)
+            g_mine = jnp.where(first, g, zero) if head == 0 else jnp.where(first, zero, g)
+            inner = jnp.sum(prod[lanes], axis=0, keepdims=True)
+            s = dot(k_ref[: here.stop, :], q_mine, NT)
+            p = jnp.exp2(s * (SCALE * LOG2E) - lse_ref[head * 8 : head * 8 + 1, here])
+            diagonal = jnp.where(causal, p[here.start :], 0.0)
+            p = jnp.concatenate([p[: here.start], diagonal], axis=0) if block else diagonal
+            dp = dot(v_ref[: here.stop, :], g_mine, NT)
+            ds = (p * (dp - inner)).astype(BF)
+            dv_acc[: here.stop, :] += dot(p.astype(BF), g_mine)
+            dk_acc[: here.stop, :] += dot(ds, q_mine)
+            parts.append(dot(turned[lanes, : here.stop], ds))
+        dq = jnp.concatenate(parts, axis=0).T * SCALE
+        dq_ref[here, :] = (dq * cos_ref[here, :] - swapped_halves(dq) * sin_ref[here, :]).astype(BF)
     dk = dk_acc[...] * SCALE
-    dk_ref[...] = (dk * cos - swapped_halves(dk) * sin).astype(BF)
+    dk_ref[...] = (dk * cos_ref[...] - swapped_halves(dk) * sin_ref[...]).astype(BF)
     dv_ref[...] = dv_acc[...].astype(BF)
-    dq = dq_acc[pl.ds(start, span), :] * SCALE
-    dq_ref[...] = (dq * cos - swapped_halves(dq) * sin).astype(BF)
-
-
-def attend_backward(inverse, q, k, v, own, sent, g, lse, cos, sin, span, pair, g_pair):
+
+
+def attend_backward(place, q, k, v, own, sent, g, lse, cos, sin, pair, g_pair):
     tokens = q.shape[0]
-    blocks = tokens // span
     full = pl.BlockSpec((tokens, 128), lambda i, p: (0, pair))
-    part = pl.BlockSpec((span, 128), lambda i, p: (i, pair))
     side = pl.BlockSpec((tokens // 2, 128), lambda i, p: (0, pair))
-    out = pl.BlockSpec((span, 128), lambda i, p: (i, 0))
+    out = pl.BlockSpec((tokens, 128), lambda i, p: (0, 0))
     return call(
         backward_body,
-        (blocks,),
+        (1,),
         [
             full,
-            part,
-            part,
+            full,
+            full,
             side,
             side,
             pl.BlockSpec((tokens, 128), lambda i, p: (0, g_pair)),
             pl.BlockSpec((16, tokens), lambda i, p: (pair, 0)),
-            whole(cos),
-            whole(sin),
+            out,
+            out,
         ],
         [out, out, out],
         [shape(tokens, 128, BF)] * 3,
-        (inverse, q, k, v, own, sent, g, lse, cos, sin),
-        scratch=[
-            pltpu.VMEM((tokens, 128), F32),
-            pltpu.VMEM((16, tokens), F32),
-            pltpu.VMEM((span, 128), F32),
-            pltpu.VMEM((span, 128), F32),
-        ],
+        (place, q, k, v, own, sent, g, lse, cos, sin),
+        scratch=[pltpu.VMEM((tokens, 128), F32), pltpu.VMEM((tokens, 128), F32)],
         scalars=1,
     )
 
@@ -422,7 +374,7 @@
     h = x_ref[...].astype(F32) + (xhat * norm_ref[2:3, :] + norm_ref[3:4, :])
     h_ref[...] = h
     hhat, _ = ln_parts(h)
-    c_ref[...] = regroup_lanes(hhat * norm_ref[4:5, :] + norm_ref[5:6, :], size).astype(BF)
+    c_ref[...] = regroup_lanes((hhat * norm_ref[4:5, :] + norm_ref[5:6, :]).astype(BF), size)
 
 
 def project(size, mine, other, w_mine, w_other, x, norm, rows=256):
@@ -493,8 +445,46 @@
     )
 
 
+def mlp_weights(w, cols):
+    owners, rows, model = w.shape
+    down = w.reshape(owners, 2, rows // 2, model)
+    up = w.reshape(owners, 4, rows // 4, model)
+    per = cols // (rows // 2)
+    halves = model // cols
+    return (
+        [up, down],
+        [
+            pl.BlockSpec(
+                (owners, None, rows // 4, cols), lambda i: (0, 2 + i // halves, 0, i % halves)
+            ),
+            pl.BlockSpec((per, None, rows // 2, model), lambda i: (i, 0, 0, 0)),
+        ],
+    )
+
+
+def flat(ref):
+    w = ref[...]
+    return w.reshape(w.shape[0] * w.shape[1], w.shape[2])
+
+
+def add_through(acc, out_ref, value):
+    step, last = pl.program_id(0), pl.num_programs(0) - 1
+
+    @pl.when(step == 0)
+    def _():
+        acc[...] = value
+
+    @pl.when((step > 0) & (step < last))
+    def _():
+        acc[...] += value
+
+    @pl.when(step == last)
+    def _():
+        out_ref[...] = (acc[...] + value).astype(out_ref.dtype)
+
+
 def up_down_body(c_ref, wu_ref, wd_ref, g_ref, s_ref, m_ref, acc):
-    u = dot(c_ref[...], wu_ref[...])
+    u = dot(c_ref[...], flat(wu_ref))
     k = math.sqrt(2.0 / math.pi)
     square = u * u
     t = jnp.tanh(u * (k + (k * 0.044715) * square))
@@ -504,57 +494,43 @@
     s_ref[...] = (
         half + (0.5 * u) * (1.0 - t * t) * (k + (3.0 * k * 0.044715) * square)
     ).astype(BF)
-    add_to(acc, dot(g, wd_ref[...]))
-
-    @pl.when(pl.program_id(0) == pl.num_programs(0) - 1)
-    def _():
-        m_ref[...] = acc[...].astype(m_ref.dtype)
-
-
-def up_down(c, w_up, w_down, dtype, cols=512):
+    add_through(acc, m_ref, dot(g, flat(wd_ref)))
+
+
+def up_down(c, w_mlp, dtype, cols=512):
     tokens, model = c.shape
     units = 2 * model
     wide = pl.BlockSpec((tokens, cols), lambda i: (0, i))
-    specs = [
-        pl.BlockSpec((model, cols), lambda i: (0, i)),
-        pl.BlockSpec((cols, model), lambda i: (i, 0)),
-    ]
+    weights, specs = mlp_weights(w_mlp, cols)
     return call(
         up_down_body,
         (units // cols,),
         [whole(c)] + specs,
         [wide, wide, pl.BlockSpec((tokens, model), lambda i: (0, 0))],
         [shape(tokens, units, BF), shape(tokens, units, BF), shape(tokens, model, dtype)],
-        (c, w_up, w_down),
+        (c, *weights),
         scratch=[pltpu.VMEM((tokens, model), F32)],
     )
 
 
 def down_up_body(dm_ref, s_ref, wu_ref, wd_ref, du_ref, dc_ref, acc):
-    du = (dot(dm_ref[...], wd_ref[...], NT) * s_ref[...].astype(F32)).astype(BF)
+    du = (dot(dm_ref[...], flat(wd_ref), NT) * s_ref[...].astype(F32)).astype(BF)
     du_ref[...] = du
-    add_to(acc, dot(du, wu_ref[...], NT))
-
-    @pl.when(pl.program_id(0) == pl.num_programs(0) - 1)
-    def _():
-        dc_ref[...] = acc[...].astype(dc_ref.dtype)
-
-
-def down_up(dm, slope, w_up, w_down, dtype, cols=512):
+    add_through(acc, dc_ref, dot(du, flat(wu_ref), NT))
+
+
+def down_up(dm, slope, w_mlp, dtype, cols=512):
     tokens, model = dm.shape
     units = 2 * model
     wide = pl.BlockSpec((tokens, cols), lambda i: (0, i))
-    specs = [
-        pl.BlockSpec((model, cols), lambda i: (0, i)),
-        pl.BlockSpec((cols, model), lambda i: (i, 0)),
-    ]
+    weights, specs = mlp_weights(w_mlp, cols)
     return call(
         down_up_body,
         (units // cols,),
         [whole(dm), wide] + specs,
         [wide, pl.BlockSpec((tokens, model), lambda i: (0, 0))],
         [shape(tokens, units, BF), shape(tokens, model, dtype)],
-        (dm, slope, w_up, w_down),
+        (dm, slope, *weights),
         scratch=[pltpu.VMEM((tokens, model), F32)],
     )
 
@@ -564,10 +540,10 @@
 
 
 def own_body(
-    size, inverse, d0_ref, d1_ref, w0_ref, w1_ref, r_ref, x_ref, dh_ref, norm_ref, out_ref, sums_ref
+    inverse, d0_ref, d1_ref, w0_ref, w1_ref, r_ref, x_ref, dh_ref, norm_ref, out_ref, sums_ref
 ):
     z = dot(d0_ref[...], w0_ref[...], NT) + dot(d1_ref[...], w1_ref[...], NT)
-    z = regroup_lanes(z + r_ref[...].astype(F32), size)
+    z = z + r_ref[...].astype(F32)
     xhat, inv = ln_parts(x_ref[...].astype(F32))
     out_ref[...] = (dh_ref[...] + ln_grad(xhat, inv, norm_ref[0:1, :], z)).astype(BF)
     add_to(sums_ref, column_sums(z, xhat))
@@ -587,12 +563,12 @@
     )
 
 
-def input_own(size, inverse, d, w, recv, x, dh, norm, span):
+def input_own(inverse, d, w, recv, x, dh, norm, span):
     width, model = d[0].shape[1], w[0].shape[0]
     part = pl.BlockSpec((span, width), lambda i, p: (p[i], 0))
     row = pl.BlockSpec((span, model), lambda i, p: (i, 0))
     return call(
-        functools.partial(own_body, size),
+        own_body,
         (2,),
         [part, part, whole(w[0]), whole(w[1]), row, row, row, whole(norm)],
         [row, pl.BlockSpec((2, model), lambda i, p: (0, 0))],
@@ -686,8 +662,8 @@
         return result
 
     class Gather:
-        def __init__(self, value, steps):
-            self.value, self.names, self.steps = value, [], list(steps)
+        def __init__(self, value, steps, names=()):
+            self.value, self.names, self.steps = value, list(names), list(steps)
 
         def send(self):
             self.moved = [exchange(self.value, m) for m in masks(self.steps[0])[1:]]
@@ -729,12 +705,14 @@
     norm_local = jnp.pad(
         by_bit(core, norm_low, norm_moved, 1).reshape(8, -1), ((0, 0), (0, local.shape[2] - 2 * rows))
     )
-    w_local = out_weight.astype(BF).reshape(rows, 2, half).transpose(1, 0, 2).reshape(2 * rows, half)
+    w_local = out_weight.astype(BF).reshape(rows, 2, half).transpose(1, 0, 2)
     first = Gather(
         jnp.concatenate([local[0], norm_local], axis=0), far_steps + [("ctx",), (0,)]
     )
     second = Gather(
-        jnp.concatenate([local[1], w_local], axis=1), far_steps + [("ctx",), (0,)]
+        jnp.concatenate([local[1].reshape(2, rows, -1), w_local], axis=2),
+        far_steps + [("ctx",), (0,)],
+        ["core"],
     )
 
     def join_all(gathers, *rest):
@@ -747,23 +725,24 @@
         for gather in gathers:
             gather.send()
 
+    x_moved = swap_begin(tokens)
     first.send()
-    positions = jnp.arange(2 * count, dtype=jnp.int32)
-    positions, w, tokens_out, order_row = join_all(
-        [first], positions, up_weight, tokens, pair_order
-    )
+    positions, order_row, up_low, x_moved = join_all(
+        [first], jnp.arange(2 * count, dtype=jnp.int32), pair_order, up_weight, x_moved
+    )
+    x = swap_end(tokens, x_moved)
     tied([first, second], "value")
     for _ in far_steps[1:]:
         send_all([first, second])
         join_all([first, second])
     send_all([first] + [second] * (len(far_steps) == 1))
-    x_moved = swap_begin(tokens_out)
-    w = w.astype(BF).reshape(rows, chips, 2, 2 * units)
-    up_moved = to_core(pick(w, 1 - core, 2))
     order_row = jnp.where(core == side, order_row, to_core(order_row))[0]
     mine_first = pick(order_row, core, 0) == 0
     inverse = jnp.where(
         mine_first, jnp.array([0, 3, 1, 2], jnp.int32), jnp.array([1, 2, 0, 3], jnp.int32)
+    )
+    place = jnp.where(
+        mine_first, jnp.array([0, 2, 3, 1], jnp.int32), jnp.array([2, 0, 1, 3], jnp.int32)
     )
     steps = jnp.arange(HEAD_DIM // 2, dtype=F32)
     frequency = jnp.exp(steps * (-math.log(10000.0) / (HEAD_DIM // 2)))
@@ -771,35 +750,24 @@
     cos, sin = jnp.cos(angles), jnp.sin(angles)
     cos_table = jnp.concatenate([cos] * 4, axis=1)
     sin_table = jnp.concatenate([-sin, sin] * 2, axis=1)
+    x_other = to_core(x)
+    w = up_low.astype(BF).reshape(rows, chips, 2, 2 * units)
+    up_moved = to_core(pick(w, 1 - core, 2))
     local = by_bit(core, pick(w, core, 2).reshape(rows, 2, -1), up_moved.reshape(rows, 2, -1))
-    wide = Gather(local.reshape(2 * rows, -1), far_steps)
-    down_low = down_weight.astype(BF)
-    cos_table, sin_table, inverse, down_low, wide.value, x_moved = join_all(
-        [first] + [second] * (len(far_steps) == 1),
-        cos_table,
-        sin_table,
-        inverse,
-        down_low,
-        wide.value,
-        x_moved,
-    )
-    send_all([first, second, wide])
-    w_down = lax.all_gather(down_low, ("chip", "ctx"), axis=0, tiled=True)
-    x = swap_end(tokens, x_moved)
-    x_other = to_core(x)
-    for _ in far_steps[1:]:
-        join_all([wide])
-        wide.send()
-    (x_other,) = join_all([first, second, wide], x_other)
-
-    cut = wide.value.shape[-1] // 2
-    ups = []
-    for n in range(2):
-        gather = Gather(wide.value[..., n * cut : (n + 1) * cut], [("ctx",), (0,)][:: 1 - 2 * n])
-        gather.names = list(wide.names)
-        ups.append(gather)
-    x_other, y_out = tied([second] + ups, "value", x_other, cotangent)
-    send_all([second] + ups)
+    local = local.transpose(2, 0, 1, 3)
+    wide = local.shape[-1]
+    per_owner = jnp.concatenate(
+        [down_weight.astype(BF).reshape(-1, wide), local.reshape(-1, wide)], axis=0
+    )
+    w_mlp = lax.all_gather(per_owner, ("chip", "ctx"), axis=0)
+    inverse, place, x_other = join_all(
+        [first] + [second] * (len(far_steps) == 1), inverse, place, x_other
+    )
+    send_all([first, second])
+    x_other, cos_table, sin_table, y_out = join_all(
+        [first, second], x_other, cos_table, sin_table, cotangent
+    )
+    second.send()
 
     a, q0, k0, v0 = first_qkv(
         rows,
@@ -812,41 +780,35 @@
         span,
     )
     gathered = first.value.reshape(2 * chips, 2 * rows + 8, -1)
-    w_first = gathered[:, : 2 * rows].reshape(model, -1)
+    w_first = gathered[:, : 2 * rows].reshape(chips, 2, 2, rows, -1)
+    w_first = w_first.transpose(0, 2, 1, 3, 4).reshape(model, -1)
     norm = gathered[:, 2 * rows :, : 2 * rows].reshape(chips, 2, 8, 2, rows)
     norm = norm.transpose(2, 0, 3, 1, 4).reshape(8, model).astype(F32)
     q0, y_out = tie(q0, y_out)
     y_moved = swap_begin(y_out)
-    own0, sent0, lse0 = attend_forward(inverse, q0, k0, v0, span)
-    own0, sent0, a = join_all([second] + ups, own0, sent0, a)
-    send_all(ups)
+    own0, sent0, lse0 = attend_forward(place, q0, k0, v0)
+    own0, sent0, a = join_all([second], own0, sent0, a)
     while second.steps:
         second.send()
         own0, sent0, a = join_all([second], own0, sent0, a)
-    w_rest = second.value.reshape(chips * 2, 2 * rows, -1)
+    w_rest = second.value.reshape(chips, 2, 2, rows, -1)
     w_second = w_rest[..., :-half].reshape(model, -1)
-    w_out = (
-        w_rest[..., -half:]
-        .reshape(chips * 2, 2, rows, half)
-        .transpose(0, 2, 1, 3)
-        .reshape(half, model)
-    )
+    w_out = w_rest[..., -half:].transpose(0, 2, 3, 1, 4).reshape(half, model)
     w_qkv = (w_first, w_second)
     w_out_other = to_core(w_out)
     recv0 = to_core(sent0)
     q1, k1, v1 = next_qkv(a, w_second, cos_table, sin_table, span)
-    own1, sent1, lse1 = attend_forward(inverse, q1, k1, v1, span)
-    own1, sent1, y_moved = join_all(ups, own1, sent1, y_moved)
-    w_up = jnp.concatenate([gather.value for gather in ups], axis=-1).reshape(model, -1)
+    own1, sent1, lse1 = attend_forward(place, q1, k1, v1)
+    own1, sent1, y_moved = tie(own1, sent1, y_moved)
     y = swap_end(cotangent, y_moved)
     recv1 = to_core(sent1)
     projected, hidden, c = project(
         rows, (own0, own1), (recv0, recv1), w_out, w_out_other, x, norm
     )
     c_other = to_core(c)
-    g_other, slope_other, m_sent = up_down(c_other, w_up, w_down, BF)
+    g_other, slope_other, m_sent = up_down(c_other, w_mlp, BF)
     m_recv = to_core(m_sent)
-    g_mine, slope_mine, m_part = up_down(c, w_up, w_down, F32)
+    g_mine, slope_mine, m_part = up_down(c, w_mlp, F32)
     output, dm, sums4 = turn(m_part, m_recv, hidden, y, norm)
     output_moved = swap_begin(output)
 
@@ -896,37 +858,34 @@
     def slot(flying, started, main):
         return launch(flying + started, collect(flying, main))
 
-    row_names = [n for n in full_order if n != "core"]
-
-    def by_rows(g):
-        return g.reshape((2,) * (levels + 1) + (-1, g.shape[1]))
-
-    def halves(g):
+    def by_rows(g, order, owned):
+        names = [n for n in full_order if n != "core" or owned is False]
+        return Reduction(g.reshape((2,) * len(names) + (-1, g.shape[1])), names, order, BF)
+
+    def halves(g, owned):
         cut = g.shape[1] // 2
-        g = by_rows(g)
         return [
-            Reduction(g[..., n * cut : (n + 1) * cut], row_names, reduce_orders[n], BF)
-            for n in range(2)
+            by_rows(g[:, n * cut : (n + 1) * cut], reduce_orders[n], owned) for n in range(2)
         ]
 
     def joined(pair):
         return jnp.concatenate([r.value for r in pair], axis=-1)
 
     dm_other = to_core(dm)
-    du_mine, dc_part = down_up(dm, slope_mine, w_up, w_down, F32)
-    du_other, dc_sent = down_up(dm_other, slope_other, w_up, w_down, BF)
+    du_mine, dc_part = down_up(dm, slope_mine, w_mlp, F32)
+    du_other, dc_sent = down_up(dm_other, slope_other, w_mlp, BF)
     du_other, dc_sent, dc_part, output_moved = tie(du_other, dc_sent, dc_part, output_moved)
     output = swap_end(output, output_moved)
     dc_recv = to_core(dc_sent)
     g_two = jnp.concatenate([g_mine, g_other], axis=0)
     dm_two = jnp.concatenate([dm, dm_other], axis=0)
     down_grad = dot(g_two, dm_two, TN).astype(BF)
-    down = halves(down_grad)
+    down = halves(down_grad, True)
     du_mine, du_other = launch(down, (du_mine, du_other))
     c_two = jnp.concatenate([c, c_other], axis=0)
     du_two = jnp.concatenate([du_mine, du_other], axis=0)
     up_grad, dc_part = tie(dot(c_two, du_two, TN).astype(BF), dc_part)
-    up = halves(up_grad)
+    up = halves(up_grad, None)
     dh, da, sums3, sums2 = descend(rows, dc_part, dc_recv, hidden, projected, y, norm)
     da = slot(down, up, da)
     da_other = to_core(da)
@@ -936,14 +895,14 @@
         [jnp.concatenate([own0, own1], axis=1), jnp.concatenate([sent0, sent1], axis=1)], axis=0
     )
     out_grad, do = tie(dot(o_two, da_two, TN).astype(BF), do)
-    out = [Reduction(by_rows(out_grad), row_names, reduce_orders[1], BF)]
+    out = [by_rows(out_grad, short_order, True)]
 
     def attention_gradient(pair, do):
         q, k, v, own, sent, lse = (
             (q0, k0, v0, own0, sent0, lse0) if pair < 2 else (q1, k1, v1, own1, sent1, lse1)
         )
         return attend_backward(
-            inverse, q, k, v, own, sent, do, lse, cos_table, sin_table, span, pair % 2, pair
+            place, q, k, v, own, sent, do, lse, cos_table, sin_table, pair % 2, pair
         )
 
     def weave(first, second):
@@ -954,32 +913,27 @@
     d1 = attention_gradient(1, do)
     do, d1 = slot(down + up, out, (do, d1))
     d_first = weave(d0, d1)
-    qkv_first = [
-        Reduction(by_rows(dot(a, d_first, TN).astype(BF)), row_names, reduce_orders[0], BF)
-    ]
+    qkv_first = [by_rows(dot(a, d_first, TN).astype(BF), short_order, False)]
     do = launch(qkv_first, do)
     d2 = attention_gradient(2, do)
-    do, d2 = slot(down + up, [], (do, d2))
+    do, d2 = slot(down + up + out, [], (do, d2))
     d3 = attention_gradient(3, do)
     d_second = weave(d2, d3)
-    qkv_second = [Reduction(by_rows(dot(a, d_second, TN).astype(BF)), row_names, short_order, BF)]
+    qkv_second = [by_rows(dot(a, d_second, TN).astype(BF), short_order, False)]
     d_second = launch(qkv_second, d_second)
+    d_second = slot(down + up + out + qkv_first, [], d_second)
     d = (d_first, d_second)
-    dx_sent = slot(down + up + out + qkv_first, [], input_other(inverse, d, w_qkv, span))
-    dx_recv = to_core(dx_sent)
-    dx_recv = slot(down + up + out + qkv_first, [], dx_recv)
-    input_grad, sums1 = input_own(rows, inverse, d, w_qkv, dx_recv, x, dh, norm, span)
+    dx_recv = to_core(input_other(inverse, d, w_qkv, span))
+    input_grad, sums1 = input_own(inverse, d, w_qkv, dx_recv, x, dh, norm, span)
+    input_moved = swap_begin(input_grad)
     norm_grad = jnp.concatenate([sums1, sums2, sums3, sums4], axis=0)
     share = norm_grad.reshape((8,) + (2,) * (levels + 2) + (rows,))
-    share = Reduction(
-        jnp.moveaxis(share, 0, levels + 2), full_order, small_order, F32
-    )
+    share = Reduction(jnp.moveaxis(share, 0, levels + 2), full_order, small_order, F32)
     everything = down + up + out + qkv_first + qkv_second + [share]
-    input_moved = swap_begin(input_grad)
-    sums1 = slot(everything[:-1], [share], sums1)
+    sums1 = slot(qkv_second, [share], sums1)
+    sums1, input_moved = tie(sums1, input_moved)
     while any(r.flying for r in everything):
         sums1 = slot(everything, [], sums1)
-        sums1, input_moved = tie(sums1, input_moved)
     input_grad = swap_end(input_grad, input_moved)
 
     def from_cores(part):

time: 629 us -> 577 us (0.917); the launches traced: 626 us -> 567 us
  Pallas kernels: 295 us -> 252 us
  other arithmetic: 66 us -> 58.3 us
  local copies, waits for them, and re-layouts: 47.2 us -> 39.8 us
    pallas_call x18, Pallas kernels: 295 us -> 252 us  [call(): pl.pallas_call(body, grid_spec=pltpu.PrefetchScalarGridSpec(num_scalar_pr...]
    another operation x30 -> x18, other arithmetic: 14.8 us -> 4.43 us  [by_bit(): jnp.stack([jnp.where(bit == 0, mine, other), jnp.where(bit == 0, other, m...]
    unnamed x199 -> x183, local copies, waits for them, and re-layouts: 16.1 us -> 7.12 us
    all_gather x1, waiting for transfers between devices: 0.01 us -> 8.43 us  [per_device(): w_mlp = lax.all_gather(per_owner, ('chip', 'ctx'), axis=0)]
    ppermute x70 -> x67, starting transfers between devices: 76.3 us -> 72.6 us  [exchange(): return lax.ppermute(x, everyone, [(i, i ^ mask) for i in range(4 * chips)])]
    ppermute x70 -> x67, waiting for transfers between devices: 60.7 us -> 59 us  [exchange(): return lax.ppermute(x, everyone, [(i, i ^ mask) for i in range(4 * chips)])]
  transfers between devices with their start and end apart: 75 -> 72, of which waited for: 15 -> 21; matrix products, arithmetic and copies ran while one was open for 18% -> 20% of each run, Pallas kernels for 43% -> 38%
where the time goes in v3:
time: 577 us; the launch traced here: 567 us
  Pallas kernels  252 us (44%)
  starting transfers between devices  90.3 us (16%)
  waiting for transfers between devices  73.5 us (13%)
  other arithmetic  58.3 us (10%)
  local copies, waits for them, and re-layouts  39.8 us (7%)
  matrix products  36.7 us (6%)
  between operations  16.5 us (3%)
    pallas_call x18, Pallas kernels, call(): pl.pallas_call(body, grid_spec=pltpu.PrefetchScalarGridSpec(num_scalar_pr...  252 us
    ppermute x67, starting transfers between devices, exchange(): return lax.ppermute(x, everyone, [(i, i ^ mask) for i in range(4 * chips)])  72.6 us
    ppermute x67, waiting for transfers between devices, exchange(): return lax.ppermute(x, everyone, [(i, i ^ mask) for i in range(4 * chips)])  59 us
    dot_general x5, matrix products, dot(): return lax.dot_general(x, y, dims, preferred_element_type=F32)  36.7 us
    ppermute x4, starting transfers between devices, swap_begin(): return lax.ppermute(x, ('core', 'ctx'), [(1, 2), (2, 1)])  17.6 us
    convert_element_type x15, other arithmetic, add(): self.value = v.astype(self.wire) if self.order else v  11.8 us
  transfers between devices with their start and end apart: 72, of which 21 were waited for; matrix products, arithmetic and copies ran while one was open for 20% of the time, Pallas kernels for 38%

profile of v3, /device:TPU:1, one launch (start us, length us, event | category | flops | bytes accessed | tf_op | source)
XLA Modules:
  0.0 567.2 jit_solution(2631166125543788034)
XLA Ops:
  82.0 6.9 %collective-permute-done.12 = bf16[2,2,2,72,768]{4,3,1,0,2:T(8,128)(2,1)S(1)} collective-permute-done((bf16[2,2,2,72,768]{4,3,1,0,2:T(8,128)(2,1)S(1)}, bf16[2,2,2,72,768]{4,3,1,0,2:T(8,128)(2,1)S(1)}, u32[]{:S(2)}, u32[]{:S(2)}) %collective-permute-start.12) | collective-permute-done | bytes 884768 | tf_op jit(solution)/shard_map/ppermute | solution.py:632
  93.3 13.1 %shard_map.341 = (bf16[2048,1024]{1,0:T(8,128)(2,1)}, bf16[2048,256]{1,0:T(8,128)(2,1)}, bf16[2048,256]{1,0:T(8,128)(2,1)}, bf16[2048,256]{1,0:T(8,128)(2,1)}) custom-call(s32[4]{0:T(128)} %broadcast_select_fusion.11.inverse, bf16[1024,1024]{1,0:T(8,128)(2,1)} %copy-done, bf16[1024,1024]{1,0:T(8,128)(2,1)} %collective-permute-done.11.other_ref, ...), custom_call_target="tpu_custom_call" | custom-call | tf_op jit(solution)/shard_map/pallas_call | solution.py:37
  106.5 8.7 %collective-permute-start.15 = (bf16[1024,1024]{1,0:T(8,128)(2,1)S(1)}, bf16[1024,1024]{1,0:T(8,128)(2,1)}, u32[]{:S(2)}, u32[]{:S(2)}) collective-permute-start(bf16[1024,1024]{1,0:T(8,128)(2,1)S(1)} %copy-done.16), channel_id=1, source_target_pairs={{1,2},{2,1},{5,6},{6,5},{9,10},{10,9},{13,14},{14,13},{17,18},{18,... | collective-permute-start | bytes 6291464 | tf_op jit(solution)/shard_map/ppermute | solution.py:638
  115.2 19.2 %shard_map.342 = (bf16[1024,256]{1,0:T(8,128)(2,1)}, bf16[1024,256]{1,0:T(8,128)(2,1)}, f32[32,2048]{1,0:T(8,128)}) custom-call(s32[4]{0:T(128)} %broadcast_select_fusion.10.place, bf16[2048,256]{1,0:T(8,128)(2,1)} %get-tuple-element.273.q_ref, bf16[2048,256]{1,0:T(8,128)(2,1)} %get-tuple-element.274.k_ref, bf16[2048,256]{1,0:T(8,128)(2,1)} %get-tuple-element.275.v_ref), custom_call_target="tpu_custom_call" | custom-call | tf_op jit(solution)/shard_map/pallas_call | solution.py:37
  138.3 8.1 %shard_map.343 = (bf16[2048,256]{1,0:T(8,128)(2,1)}, bf16[2048,256]{1,0:T(8,128)(2,1)}, bf16[2048,256]{1,0:T(8,128)(2,1)}) custom-call(bf16[2048,1024]{1,0:T(8,128)(2,1)} %get-tuple-element.284.a_ref, bf16[1024,768]{1,0:T(8,128)(2,1)} %bitcast.339, f32[2048,128]{1,0:T(8,128)} %pad_maximum_fusion.3.cos_ref, f32[2048,128]{1,0:T(8,128)} %pad_maximum_fusion.4.sin_ref), custom_call_target="tpu_custom_call" | custom-call | tf_op jit(solution)/shard_map/pallas_call | solution.py:37
  146.4 19.7 %shard_map.344 = (bf16[1024,256]{1,0:T(8,128)(2,1)}, bf16[1024,256]{1,0:T(8,128)(2,1)}, f32[32,2048]{1,0:T(8,128)}) custom-call(s32[4]{0:T(128)} %broadcast_select_fusion.10.place, bf16[2048,256]{1,0:T(8,128)(2,1)} %get-tuple-element.286.q_ref, bf16[2048,256]{1,0:T(8,128)(2,1)} %get-tuple-element.287.k_ref, bf16[2048,256]{1,0:T(8,128)(2,1)} %get-tuple-element.288.v_ref), custom_call_target="tpu_custom_call" | custom-call | tf_op jit(solution)/shard_map/pallas_call | solution.py:37
  168.9 9.4 %shard_map.345 = (f32[1024,1024]{1,0:T(8,128)}, f32[1024,1024]{1,0:T(8,128)}, bf16[1024,1024]{1,0:T(8,128)(2,1)}) custom-call(bf16[1024,256]{1,0:T(8,128)(2,1)} %get-tuple-element.283.m0_ref.own_ref, bf16[1024,256]{1,0:T(8,128)(2,1)} %get-tuple-element.292.m1_ref.own_ref, bf16[1024,256]{1,0:T(8,128)(2,1)} %collective-permute-done.16.o0_ref, ...), custom_call_target="tpu_custom_call" | custom-call | tf_op jit(solution)/shard_map/pallas_call | solution.py:37
  182.8 8.4 %all-gather.3.cloned.1.call-done = bf16[4096,1024]{1,0:T(8,128)(2,1)} async-done(((bf16[256,1024]{1,0:T(8,128)(2,1)}), bf16[4096,1024]{1,0:T(8,128)(2,1)}) %all-gather.3.cloned.1.call-update) | async-done | bytes 8388624 | tf_op jit(solution)/shard_map/all_gather | solution.py:762
  191.3 18.0 %shard_map.347 = (bf16[1024,2048]{1,0:T(8,128)(2,1)}, bf16[1024,2048]{1,0:T(8,128)(2,1)}, bf16[1024,1024]{1,0:T(8,128)(2,1)}) custom-call(bf16[1024,1024]{1,0:T(8,128)(2,1)} %collective-permute-done.20.c_ref, bf16[16,4,64,1024]{3,2,1,0:T(8,128)(2,1)} %bitcast.331, bf16[16,2,128,1024]{3,2,1,0:T(8,128)(2,1)} %bitcast.332), custom_call_target="tpu_custom_call" | custom-call | tf_op jit(solution)/shard_map/pallas_call | solution.py:37
  213.2 18.5 %shard_map.346 = (bf16[1024,2048]{1,0:T(8,128)(2,1)}, bf16[1024,2048]{1,0:T(8,128)(2,1)}, f32[1024,1024]{1,0:T(8,128)}) custom-call(bf16[1024,1024]{1,0:T(8,128)(2,1)} %get-tuple-element.295.c_ref, bf16[16,4,64,1024]{3,2,1,0:T(8,128)(2,1)} %bitcast.333, bf16[16,2,128,1024]{3,2,1,0:T(8,128)(2,1)} %bitcast.334), custom_call_target="tpu_custom_call" | custom-call | tf_op jit(solution)/shard_map/pallas_call | solution.py:37
  233.0 8.6 %shard_map.348 = (bf16[1024,1024]{1,0:T(8,128)(2,1)}, bf16[1024,1024]{1,0:T(8,128)(2,1)}, f32[2,1024]{1,0:T(2,128)}) custom-call(f32[1024,1024]{1,0:T(8,128)} %get-tuple-element.297.m_ref, bf16[1024,1024]{1,0:T(8,128)(2,1)} %copy-done.28, f32[1024,1024]{1,0:T(8,128)} %get-tuple-element.299.h_ref, bf16[1024,1024]{1,0:T(8,128)(2,1)} %broadcast_select_fusion.2.y_ref, ...), custom_call_target="tpu_custom_call" | custom-call | tf_op jit(solution)/shard_map/pallas_call | solution.py:37
  241.7 16.3 %shard_map.350 = (bf16[1024,2048]{1,0:T(8,128)(2,1)}, f32[1024,1024]{1,0:T(8,128)}) custom-call(bf16[1024,1024]{1,0:T(8,128)(2,1)} %get-tuple-element.302.dm_ref, bf16[1024,2048]{1,0:T(8,128)(2,1)} %get-tuple-element.306.s_ref, bf16[16,4,64,1024]{3,2,1,0:T(8,128)(2,1)} %bitcast.335, bf16[16,2,128,1024]{3,2,1,0:T(8,128)(2,1)} %bitcast.336), custom_call_target="tpu_custom_call" | custom-call | tf_op jit(solution)/shard_map/pallas_call | solution.py:37
  259.9 12.3 %fusion.23 = bf16[2048,1024]{1,0:T(8,128)(2,1)S(1)} fusion(bf16[1024,1024]{1,0:T(8,128)(2,1)} %collective-permute-done.22.dm_ref, bf16[1024,1024]{1,0:T(8,128)(2,1)S(1)} %copy-done.29, bf16[1024,2048]{1,0:T(8,128)(2,1)} %get-tuple-element.310, bf16[1024,2048]{1,0:T(8,128)(2,1)} %get-tuple-element.309), kind=kOutput, calls=%fused_computation.19 | convolution fusion | flops 8617197568 | bytes 16777216 | tf_op jit(solution)/shard_map/dot_general | solution.py:33
  275.1 15.5 %shard_map.349 = (bf16[1024,2048]{1,0:T(8,128)(2,1)}, bf16[1024,1024]{1,0:T(8,128)(2,1)}) custom-call(bf16[1024,1024]{1,0:T(8,128)(2,1)} %collective-permute-done.22.dm_ref, bf16[1024,2048]{1,0:T(8,128)(2,1)} %get-tuple-element.303.s_ref, bf16[16,4,64,1024]{3,2,1,0:T(8,128)(2,1)} %bitcast.337, bf16[16,2,128,1024]{3,2,1,0:T(8,128)(2,1)} %bitcast.338), custom_call_target="tpu_custom_call" | custom-call | tf_op jit(solution)/shard_map/pallas_call | solution.py:37
  294.2 12.5 %fusion.18 = bf16[1024,2048]{1,0:T(8,128)(2,1)S(1)} fusion(bf16[1024,2048]{1,0:T(8,128)(2,1)} %get-tuple-element.316, bf16[1024,2048]{1,0:T(8,128)(2,1)} %get-tuple-element.315, bf16[1024,1024]{1,0:T(8,128)(2,1)} %collective-permute-done.20.c_ref, bf16[1024,1024]{1,0:T(8,128)(2,1)S(1)} %copy-done.20), kind=kOutput, calls=%fused_computation.18 | convolution fusion | flops 8617197568 | bytes 16777216 | tf_op jit(solution)/shard_map/dot_general | solution.py:33
  310.6 12.7 %shard_map.351 = (f32[1024,1024]{1,0:T(8,128)}, bf16[1024,1024]{1,0:T(8,128)(2,1)}, f32[2,1024]{1,0:T(2,128)}, f32[2,1024]{1,0:T(2,128)}) custom-call(f32[1024,1024]{1,0:T(8,128)} %get-tuple-element.318.dc_ref, bf16[1024,1024]{1,0:T(8,128)(2,1)} %collective-permute-done.26.r_ref, f32[1024,1024]{1,0:T(8,128)} %get-tuple-element.299.h_ref, ...), custom_call_target="tpu_custom_call" | custom-call | tf_op jit(solution)/shard_map/pallas_call | solution.py:37
  333.6 7.2 %shard_map.352.g_ref = bf16[2048,512]{1,0:T(8,128)(2,1)} custom-call(s32[4]{0:T(128)} %broadcast_select_fusion.11.inverse, bf16[1024,1024]{1,0:T(8,128)(2,1)} %get-tuple-element.328.own_ref, bf16[1024,1024]{1,0:T(8,128)(2,1)} %collective-permute-done.29.other_ref, bf16[512,1024]{1,0:T(8,128)(2,1)} %bitcast.351), custom_call_target="tpu_custom_call" | custom-call | tf_op jit(solution)/shard_map/pallas_call | solution.py:37
  345.5 16.6 %shard_map.353 = (bf16[2048,128]{1,0:T(8,128)(2,1)}, bf16[2048,128]{1,0:T(8,128)(2,1)}, bf16[2048,128]{1,0:T(8,128)(2,1)}) custom-call(s32[4]{0:T(128)} %broadcast_select_fusion.10.place, bf16[2048,256]{1,0:T(8,128)(2,1)} %get-tuple-element.273.q_ref, bf16[2048,256]{1,0:T(8,128)(2,1)} %get-tuple-element.274.k_ref, ...), custom_call_target="tpu_custom_call" | custom-call | tf_op jit(solution)/shard_map/pallas_call | solution.py:37
  369.3 16.8 %shard_map.354 = (bf16[2048,128]{1,0:T(8,128)(2,1)}, bf16[2048,128]{1,0:T(8,128)(2,1)}, bf16[2048,128]{1,0:T(8,128)(2,1)}) custom-call(s32[4]{0:T(128)} %broadcast_select_fusion.10.place, bf16[2048,256]{1,0:T(8,128)(2,1)} %get-tuple-element.273.q_ref, bf16[2048,256]{1,0:T(8,128)(2,1)} %get-tuple-element.274.k_ref, ...), custom_call_target="tpu_custom_call" | custom-call | tf_op jit(solution)/shard_map/pallas_call | solution.py:37
  397.0 8.1 %collective-permute-done.34 = bf16[128,512]{1,0:T(8,128)(2,1)S(1)} collective-permute-done((bf16[128,512]{1,0:T(8,128)(2,1)S(1)}, bf16[128,512]{1,0:T(8,128)(2,1)S(1)}, u32[]{:S(2)}, u32[]{:S(2)}) %collective-permute-start.34) | collective-permute-done | bytes 131104 | tf_op jit(solution)/shard_map/ppermute | solution.py:632
  414.4 16.6 %shard_map.355 = (bf16[2048,128]{1,0:T(8,128)(2,1)}, bf16[2048,128]{1,0:T(8,128)(2,1)}, bf16[2048,128]{1,0:T(8,128)(2,1)}) custom-call(s32[4]{0:T(128)} %broadcast_select_fusion.10.place, bf16[2048,256]{1,0:T(8,128)(2,1)} %get-tuple-element.286.q_ref, bf16[2048,256]{1,0:T(8,128)(2,1)} %get-tuple-element.287.k_ref, ...), custom_call_target="tpu_custom_call" | custom-call | tf_op jit(solution)/shard_map/pallas_call | solution.py:37
  435.9 16.6 %shard_map.356 = (bf16[2048,128]{1,0:T(8,128)(2,1)}, bf16[2048,128]{1,0:T(8,128)(2,1)}, bf16[2048,128]{1,0:T(8,128)(2,1)}) custom-call(s32[4]{0:T(128)} %broadcast_select_fusion.10.place, bf16[2048,256]{1,0:T(8,128)(2,1)} %get-tuple-element.286.q_ref, bf16[2048,256]{1,0:T(8,128)(2,1)} %get-tuple-element.287.k_ref, ...), custom_call_target="tpu_custom_call" | custom-call | tf_op jit(solution)/shard_map/pallas_call | solution.py:37
  472.5 7.7 %shard_map.357 = bf16[1024,1024]{1,0:T(8,128)(2,1)} custom-call(s32[4]{0:T(128)} %broadcast_select_fusion.11.inverse, bf16[2048,768]{1,0:T(8,128)(2,1)} %copy-done.2, bf16[2048,768]{1,0:T(8,128)(2,1)} %copy-done.3, bf16[1024,768]{1,0:T(8,128)(2,1)} %bitcast.345, bf16[1024,768]{1,0:T(8,128)(2,1)} %bitcast.340), custom_call_target="tpu_custom_call" | custom-call | tf_op jit(solution)/shard_map/pallas_call | solution.py:37
  492.7 11.6 %shard_map.358 = (bf16[1024,1024]{1,0:T(8,128)(2,1)}, f32[2,1024]{1,0:T(2,128)}) custom-call(s32[4]{0:T(128)} %broadcast_select_fusion.11.inverse, bf16[2048,768]{1,0:T(8,128)(2,1)} %copy-done.2, bf16[2048,768]{1,0:T(8,128)(2,1)} %copy-done.3, bf16[1024,768]{1,0:T(8,128)(2,1)} %bitcast.346, bf16[1024,768]{1,0:T(8,128)(2,1)} %bitcast.341, ...), custom_call_target="tpu_custom_call" | custom-call | tf_op jit(solution)/shard_map/pallas_call | solution.py:37
  (474 shorter events, 241.6 us)
Async XLA Ops:
  7.2 184.1 %all-gather.3.cloned.1.call-start = ((), (), s32[]{:S(2)}) async-start(), calls=%async_computation | async-start | bytes 8912896 | tf_op jit(solution)/shard_map/all_gather | solution.py:762
  7.2 28.5 %collective-permute-start.5 = (bf16[1024,1024]{1,0:T(8,128)(2,1)}, bf16[1024,1024]{1,0:T(8,128)(2,1)S(1)}, u32[]{:S(2)}, u32[]{:S(2)}) collective-permute-start(bf16[1024,1024]{1,0:T(8,128)(2,1)} %param.22), channel_id=1, source_target_pairs={{1,2},{2,1},{5,6},{6,5},{9,10},{10,9},{13,14},{14,13},{17,18},{18,... | collective-permute-start | bytes 6291464 | tf_op jit(solution)/shard_map/ppermute | solution.py:638
  89.6 44.7 %collective-permute-start.14 = (bf16[2,2,2,2,32,1280]{5,4,2,1,0,3:T(8,128)(2,1)S(1)}, bf16[2,2,2,2,32,1280]{5,4,2,1,0,3:T(8,128)(2,1)S(1)}, u32[]{:S(2)}, u32[]{:S(2)}) collective-permute-start(bf16[2,2,2,2,32,1280]{5,4,2,1,0,3:T(8,128)(2,1)S(1)} %pad_maximum_fusion.2), channel_id=1, source_target_pairs={{0,4},{1,5},{2,6},{3,7},{4,0},{5,1},{6,2},{7,3},{8,12},{9,13},{10,... | collective-permute-start | bytes 3932168 | tf_op jit(solution)/shard_map/ppermute | solution.py:632
  106.5 59.6 %collective-permute-start.15 = (bf16[1024,1024]{1,0:T(8,128)(2,1)S(1)}, bf16[1024,1024]{1,0:T(8,128)(2,1)}, u32[]{:S(2)}, u32[]{:S(2)}) collective-permute-start(bf16[1024,1024]{1,0:T(8,128)(2,1)S(1)} %copy-done.16), channel_id=1, source_target_pairs={{1,2},{2,1},{5,6},{6,5},{9,10},{10,9},{13,14},{14,13},{17,18},{18,... | collective-permute-start | bytes 6291464 | tf_op jit(solution)/shard_map/ppermute | solution.py:638
  136.4 32.5 %collective-permute-start.18 = (bf16[512,1024]{1,0:T(8,128)(2,1)S(1)}, bf16[512,1024]{1,0:T(8,128)(2,1)}, u32[]{:S(2)}, u32[]{:S(2)}) collective-permute-start(bf16[512,1024]{1,0:T(8,128)(2,1)S(1)} %bitcast.349), channel_id=1, source_target_pairs={{0,2},{1,3},{2,0},{3,1},{4,6},{5,7},{6,4},{7,5},{8,10},{9,11},{10,... | collective-permute-start | bytes 3145736 | tf_op jit(solution)/shard_map/ppermute | solution.py:632
  138.0 30.9 %collective-permute-start.16 = (bf16[1024,256]{1,0:T(8,128)(2,1)S(1)}, bf16[1024,256]{1,0:T(8,128)(2,1)}, u32[]{:S(2)}, u32[]{:S(2)}) collective-permute-start(bf16[1024,256]{1,0:T(8,128)(2,1)S(1)} %copy-done.23), channel_id=1, source_target_pairs={{0,2},{1,3},{2,0},{3,1},{4,6},{5,7},{6,4},{7,5},{8,10},{9,11},{10,... | collective-permute-start | bytes 1572872 | tf_op jit(solution)/shard_map/ppermute | solution.py:632
  258.0 32.5 %collective-permute-start.23 = (bf16[1024,1024]{1,0:T(8,128)(2,1)}, bf16[1024,1024]{1,0:T(8,128)(2,1)}, u32[]{:S(2)}, u32[]{:S(2)}) collective-permute-start(bf16[1024,1024]{1,0:T(8,128)(2,1)} %get-tuple-element.301), channel_id=1, source_target_pairs={{1,2},{2,1},{5,6},{6,5},{9,10},{10,9},{13,14},{14,13},{17,18},{18,... | collective-permute-start | bytes 6291464 | tf_op jit(solution)/shard_map/ppermute | solution.py:638
  291.2 32.1 %collective-permute-start.24 = (bf16[2,2,2,128,512]{4,3,0,1,2:T(8,128)(2,1)}, bf16[2,2,2,128,512]{4,3,0,1,2:T(8,128)(2,1)S(1)}, u32[]{:S(2)}, u32[]{:S(2)}) collective-permute-start(bf16[2,2,2,128,512]{4,3,0,1,2:T(8,128)(2,1)} %bitcast.369), channel_id=1, source_target_pairs={{0,4},{1,5},{2,6},{3,7},{4,0},{5,1},{6,2},{7,3},{8,12},{9,13},{10,... | collective-permute-start | bytes 3145736 | tf_op jit(solution)/shard_map/ppermute | solution.py:632
  292.9 30.4 %collective-permute-start.25 = (bf16[2,2,2,128,512]{4,3,0,1,2:T(8,128)(2,1)}, bf16[2,2,2,128,512]{4,3,0,1,2:T(8,128)(2,1)}, u32[]{:S(2)}, u32[]{:S(2)}) collective-permute-start(bf16[2,2,2,128,512]{4,3,0,1,2:T(8,128)(2,1)} %bitcast.368), channel_id=1, source_target_pairs={{0,1},{1,0},{2,3},{3,2},{4,5},{5,4},{6,7},{7,6},{8,9},{9,8},{10,11... | collective-permute-start | bytes 3145736 | tf_op jit(solution)/shard_map/ppermute | solution.py:632
  330.6 31.4 %collective-permute-start.27 = (bf16[2,2,128,512]{3,2,0,1:T(8,128)(2,1)S(1)}, bf16[2,2,128,512]{3,2,0,1:T(8,128)(2,1)S(1)}, u32[]{:S(2)}, u32[]{:S(2)}) collective-permute-start(bf16[2,2,128,512]{3,2,0,1:T(8,128)(2,1)S(1)} %copy-done.53), channel_id=1, source_target_pairs={{0,1},{1,0},{2,3},{3,2},{4,5},{5,4},{6,7},{7,6},{8,9},{9,8},{10,11... | collective-permute-start | bytes 1572872 | tf_op jit(solution)/shard_map/ppermute | solution.py:632
  330.9 31.2 %collective-permute-start.28 = (bf16[2,2,128,512]{3,2,0,1:T(8,128)(2,1)S(1)}, bf16[2,2,128,512]{3,2,0,1:T(8,128)(2,1)S(1)}, u32[]{:S(2)}, u32[]{:S(2)}) collective-permute-start(bf16[2,2,128,512]{3,2,0,1:T(8,128)(2,1)S(1)} %copy-done.52), channel_id=1, source_target_pairs={{0,4},{1,5},{2,6},{3,7},{4,0},{5,1},{6,2},{7,3},{8,12},{9,13},{10,... | collective-permute-start | bytes 1572872 | tf_op jit(solution)/shard_map/ppermute | solution.py:632
  330.9 55.4 %collective-permute-start.32 = (bf16[2,2,2,64,1024]{4,3,0,1,2:T(8,128)(2,1)}, bf16[2,2,2,64,1024]{4,3,0,1,2:T(8,128)(2,1)}, u32[]{:S(2)}, u32[]{:S(2)}) collective-permute-start(bf16[2,2,2,64,1024]{4,3,0,1,2:T(8,128)(2,1)} %bitcast.316), channel_id=1, source_target_pairs={{0,4},{1,5},{2,6},{3,7},{4,0},{5,1},{6,2},{7,3},{8,12},{9,13},{10,... | collective-permute-start | bytes 3145736 | tf_op jit(solution)/shard_map/ppermute | solution.py:632
  332.3 53.9 %collective-permute-start.33 = (bf16[2,2,2,64,1024]{4,3,2,1,0:T(8,128)(2,1)}, bf16[2,2,2,64,1024]{4,3,2,1,0:T(8,128)(2,1)}, u32[]{:S(2)}, u32[]{:S(2)}) collective-permute-start(bf16[2,2,2,64,1024]{4,3,2,1,0:T(8,128)(2,1)} %dynamic-slice_bitcast_fusion), channel_id=1, source_target_pairs={{0,1},{1,0},{2,3},{3,2},{4,5},{5,4},{6,7},{7,6},{8,9},{9,8},{10,11... | collective-permute-start | bytes 3145736 | tf_op jit(solution)/shard_map/ppermute | solution.py:632
  391.0 42.6 %collective-permute-start.36 = (bf16[2,2,64,1024]{3,2,0,1:T(8,128)(2,1)S(1)}, bf16[2,2,64,1024]{3,2,0,1:T(8,128)(2,1)S(1)}, u32[]{:S(2)}, u32[]{:S(2)}) collective-permute-start(bf16[2,2,64,1024]{3,2,0,1:T(8,128)(2,1)S(1)} %dynamic-slice_bitcast_fusion.2), channel_id=1, source_target_pairs={{0,1},{1,0},{2,3},{3,2},{4,5},{5,4},{6,7},{7,6},{8,9},{9,8},{10,11... | collective-permute-start | bytes 1572872 | tf_op jit(solution)/shard_map/ppermute | solution.py:632
  392.2 41.4 %collective-permute-start.37 = (bf16[2,2,64,1024]{3,2,1,0:T(8,128)(2,1)S(1)}, bf16[2,2,64,1024]{3,2,1,0:T(8,128)(2,1)S(1)}, u32[]{:S(2)}, u32[]{:S(2)}) collective-permute-start(bf16[2,2,64,1024]{3,2,1,0:T(8,128)(2,1)S(1)} %dynamic-slice_bitcast_fusion.1), channel_id=1, source_target_pairs={{0,4},{1,5},{2,6},{3,7},{4,0},{5,1},{6,2},{7,3},{8,12},{9,13},{10,... | collective-permute-start | bytes 1572872 | tf_op jit(solution)/shard_map/ppermute | solution.py:632
  392.4 38.5 %collective-permute-start.38 = (bf16[2,2,32,1024]{3,2,1,0:T(8,128)(2,1)S(1)}, bf16[2,2,32,1024]{3,2,1,0:T(8,128)(2,1)}, u32[]{:S(2)}, u32[]{:S(2)}) collective-permute-start(bf16[2,2,32,1024]{3,2,1,0:T(8,128)(2,1)S(1)} %get-tuple-element.367), channel_id=1, source_target_pairs={{0,1},{1,0},{2,3},{3,2},{4,5},{5,4},{6,7},{7,6},{8,9},{9,8},{10,11... | collective-permute-start | bytes 786440 | tf_op jit(solution)/shard_map/ppermute | solution.py:632
  405.1 26.1 %collective-permute-start.39 = (bf16[2,2,32,1024]{3,2,1,0:T(8,128)(2,1)S(1)}, bf16[2,2,32,1024]{3,2,1,0:T(8,128)(2,1)S(1)}, u32[]{:S(2)}, u32[]{:S(2)}) collective-permute-start(bf16[2,2,32,1024]{3,2,1,0:T(8,128)(2,1)S(1)} %get-tuple-element.368), channel_id=1, source_target_pairs={{0,4},{1,5},{2,6},{3,7},{4,0},{5,1},{6,2},{7,3},{8,12},{9,13},{10,... | collective-permute-start | bytes 786440 | tf_op jit(solution)/shard_map/ppermute | solution.py:632
  407.9 23.9 %collective-permute-start.40 = (bf16[2,2,32,1024]{3,2,1,0:T(8,128)(2,1)S(1)}, bf16[2,2,32,1024]{3,2,1,0:T(8,128)(2,1)S(1)}, u32[]{:S(2)}, u32[]{:S(2)}) collective-permute-start(bf16[2,2,32,1024]{3,2,1,0:T(8,128)(2,1)S(1)} %get-tuple-element.369), channel_id=1, source_target_pairs={{0,5},{1,4},{2,7},{3,6},{4,1},{5,0},{6,3},{7,2},{8,13},{9,12},{10,... | collective-permute-start | bytes 786440 | tf_op jit(solution)/shard_map/ppermute | solution.py:632
  430.9 29.7 %collective-permute-start.46 = (bf16[2,2,2,32,768]{4,3,2,1,0:T(8,128)(2,1)}, bf16[2,2,2,32,768]{4,3,2,1,0:T(8,128)(2,1)S(1)}, u32[]{:S(2)}, u32[]{:S(2)}) collective-permute-start(bf16[2,2,2,32,768]{4,3,2,1,0:T(8,128)(2,1)} %get-tuple-element.390), channel_id=1, source_target_pairs={{0,1},{1,0},{2,3},{3,2},{4,5},{5,4},{6,7},{7,6},{8,9},{9,8},{10,11... | collective-permute-start | bytes 1179656 | tf_op jit(solution)/shard_map/ppermute | solution.py:632
  431.1 30.2 %collective-permute-start.47 = (bf16[2,2,2,32,768]{4,3,2,1,0:T(8,128)(2,1)}, bf16[2,2,2,32,768]{4,3,2,1,0:T(8,128)(2,1)S(1)}, u32[]{:S(2)}, u32[]{:S(2)}) collective-permute-start(bf16[2,2,2,32,768]{4,3,2,1,0:T(8,128)(2,1)} %get-tuple-element.391), channel_id=1, source_target_pairs={{0,4},{1,5},{2,6},{3,7},{4,0},{5,1},{6,2},{7,3},{8,12},{9,13},{10,... | collective-permute-start | bytes 1179656 | tf_op jit(solution)/shard_map/ppermute | solution.py:632
  431.8 30.9 %collective-permute-start.48 = (bf16[2,2,2,32,768]{4,3,2,1,0:T(8,128)(2,1)}, bf16[2,2,2,32,768]{4,3,2,1,0:T(8,128)(2,1)S(1)}, u32[]{:S(2)}, u32[]{:S(2)}) collective-permute-start(bf16[2,2,2,32,768]{4,3,2,1,0:T(8,128)(2,1)} %get-tuple-element.392), channel_id=1, source_target_pairs={{0,5},{1,4},{2,7},{3,6},{4,1},{5,0},{6,3},{7,2},{8,13},{9,12},{10,... | collective-permute-start | bytes 1179656 | tf_op jit(solution)/shard_map/ppermute | solution.py:632
  490.3 28.2 %collective-permute-start.51 = (bf16[64,1024]{1,0:T(8,128)(2,1)}, bf16[64,1024]{1,0:T(8,128)(2,1)}, u32[]{:S(2)}, u32[]{:S(2)}) collective-permute-start(bf16[64,1024]{1,0:T(8,128)(2,1)} %dynamic-slice_bitcast_fusion.21), channel_id=1, source_target_pairs={{0,16},{1,17},{2,18},{3,19},{4,20},{5,21},{6,22},{7,23},{8,24},{9,... | collective-permute-start | bytes 393224 | tf_op jit(solution)/shard_map/ppermute | solution.py:632
  490.4 29.2 %collective-permute-start.52 = (bf16[64,1024]{1,0:T(8,128)(2,1)}, bf16[64,1024]{1,0:T(8,128)(2,1)}, u32[]{:S(2)}, u32[]{:S(2)}) collective-permute-start(bf16[64,1024]{1,0:T(8,128)(2,1)} %dynamic-slice_bitcast_fusion.20), channel_id=1, source_target_pairs={{0,16},{1,17},{2,18},{3,19},{4,20},{5,21},{6,22},{7,23},{8,24},{9,... | collective-permute-start | bytes 393224 | tf_op jit(solution)/shard_map/ppermute | solution.py:632
  527.4 29.4 %collective-permute-start.50 = (bf16[1024,1024]{1,0:T(8,128)(2,1)S(1)}, bf16[1024,1024]{1,0:T(8,128)(2,1)}, u32[]{:S(2)}, u32[]{:S(2)}) collective-permute-start(bf16[1024,1024]{1,0:T(8,128)(2,1)S(1)} %copy-done.18), channel_id=1, source_target_pairs={{1,2},{2,1},{5,6},{6,5},{9,10},{10,9},{13,14},{14,13},{17,18},{18,... | collective-permute-start | bytes 6291464 | tf_op jit(solution)/shard_map/ppermute | solution.py:638
  (131 other events, 1435.2 us)
Sparse Core Ops, SparseCore 0:
  41.8 149.3 all-gather.2

commit v4 on v3

--- a/solution.py
+++ b/solution.py
@@ -275,8 +275,9 @@
     dv_acc[...] = jnp.zeros_like(dv_acc)
     for block in range(q_ref.shape[0] // rows):
         here = slice(block * rows, (block + 1) * rows)
-        q, g = q_ref[here, :], g_ref[here, :]
         at = place[block * rows // span]
+        q = q_ref[here, :]
+        g = g_ref[pl.ds(pl.multiple_of(at * span + block * rows % span, rows), rows), :]
         start = pl.multiple_of((at % 2) * span + block * rows % span, rows)
         o = jnp.where(at < 2, own_ref[pl.ds(start, rows), :], sent_ref[pl.ds(start, rows), :])
         prod = (o.astype(F32) * g.astype(F32)).T
@@ -325,36 +326,6 @@
         [shape(tokens, 128, BF)] * 3,
         (place, q, k, v, own, sent, g, lse, cos, sin),
         scratch=[pltpu.VMEM((tokens, 128), F32), pltpu.VMEM((tokens, 128), F32)],
-        scalars=1,
-    )
-
-
-def mix_body(inverse, own_ref, other_ref, w_ref, out_ref):
-    index = pl.program_id(0)
-
-    @pl.when(index < 2)
-    def _():
-        out_ref[...] = dot(own_ref[...], w_ref[...], NT).astype(BF)
-
-    @pl.when(index >= 2)
-    def _():
-        out_ref[...] = dot(other_ref[...], w_ref[...], NT).astype(BF)
-
-
-def mix_gradient(inverse, own, other, w_out, span):
-    model = own.shape[1]
-    width = w_out.shape[0]
-    return call(
-        mix_body,
-        (4,),
-        [
-            pl.BlockSpec((span, model), lambda i, p: (jnp.minimum(i, 1), 0)),
-            pl.BlockSpec((span, model), lambda i, p: (jnp.maximum(i - 2, 0), 0)),
-            whole(w_out),
-        ],
-        pl.BlockSpec((span, width), lambda i, p: (p[i], 0)),
-        shape(4 * span, width, BF),
-        (inverse, own, other, w_out),
         scalars=1,
     )
 
@@ -694,12 +665,12 @@
     )
     chain = [0, "ctx"] + high
     short_order = [tuple(chain[n : n + 2]) for n in range(0, len(chain), 2)]
-    chain = ["core", "ctx", 0] + high
-    small_order = [tuple(chain[n : n + 2]) for n in range(0, len(chain), 2)]
 
     w = qkv_weight.astype(BF).reshape(rows, 3, 2, part_heads, 2, HEAD_DIM)
     norm_low = norm_weight.astype(BF)
     qkv_moved, norm_moved = to_core(pick(w, 1 - core, 4)), to_core(norm_low)
+    w_wide = up_weight.astype(BF).reshape(rows, chips, 2, 2 * units)
+    up_moved = to_core(pick(w_wide, 1 - core, 2))
     local = by_bit(core, pick(w, core, 4), qkv_moved).transpose(3, 0, 1, 2, 4, 5)
     local = local.reshape(2, 2 * rows, -1)
     norm_local = jnp.pad(
@@ -727,8 +698,14 @@
 
     x_moved = swap_begin(tokens)
     first.send()
-    positions, order_row, up_low, x_moved = join_all(
-        [first], jnp.arange(2 * count, dtype=jnp.int32), pair_order, up_weight, x_moved
+    local = by_bit(core, pick(w_wide, core, 2).reshape(rows, 2, -1), up_moved.reshape(rows, 2, -1))
+    local = local.transpose(2, 0, 1, 3)
+    wide = local.shape[-1]
+    per_owner = jnp.concatenate(
+        [down_weight.astype(BF).reshape(-1, wide), local.reshape(-1, wide)], axis=0
+    )
+    positions, order_row, per_owner, x_moved = join_all(
+        [first], jnp.arange(2 * count, dtype=jnp.int32), pair_order, per_owner, x_moved
     )
     x = swap_end(tokens, x_moved)
     tied([first, second], "value")
@@ -751,14 +728,6 @@
     cos_table = jnp.concatenate([cos] * 4, axis=1)
     sin_table = jnp.concatenate([-sin, sin] * 2, axis=1)
     x_other = to_core(x)
-    w = up_low.astype(BF).reshape(rows, chips, 2, 2 * units)
-    up_moved = to_core(pick(w, 1 - core, 2))
-    local = by_bit(core, pick(w, core, 2).reshape(rows, 2, -1), up_moved.reshape(rows, 2, -1))
-    local = local.transpose(2, 0, 1, 3)
-    wide = local.shape[-1]
-    per_owner = jnp.concatenate(
-        [down_weight.astype(BF).reshape(-1, wide), local.reshape(-1, wide)], axis=0
-    )
     w_mlp = lax.all_gather(per_owner, ("chip", "ctx"), axis=0)
     inverse, place, x_other = join_all(
         [first] + [second] * (len(far_steps) == 1), inverse, place, x_other
@@ -889,13 +858,19 @@
     dh, da, sums3, sums2 = descend(rows, dc_part, dc_recv, hidden, projected, y, norm)
     da = slot(down, up, da)
     da_other = to_core(da)
-    do = mix_gradient(inverse, da, da_other, w_out, span)
     da_two = jnp.concatenate([da, da_other], axis=0)
+    do = dot(da_two, w_out, NT).astype(BF)
     o_two = jnp.concatenate(
         [jnp.concatenate([own0, own1], axis=1), jnp.concatenate([sent0, sent1], axis=1)], axis=0
     )
-    out_grad, do = tie(dot(o_two, da_two, TN).astype(BF), do)
-    out = [by_rows(out_grad, short_order, True)]
+    out_grad = jnp.stack(
+        [
+            dot(o_two, da_two[:, n : n + half], TN).astype(BF).reshape(2**levels, 2, rows, half)
+            for n in (0, half)
+        ],
+        axis=1,
+    )
+    out_grad, do = tie(out_grad, do)
 
     def attention_gradient(pair, do):
         q, k, v, own, sent, lse = (
@@ -911,40 +886,43 @@
     d0 = attention_gradient(0, do)
     do, d0 = slot(down, [], (do, d0))
     d1 = attention_gradient(1, do)
-    do, d1 = slot(down + up, out, (do, d1))
+    do, d1 = slot(down + up, [], (do, d1))
     d_first = weave(d0, d1)
-    qkv_first = [by_rows(dot(a, d_first, TN).astype(BF), short_order, False)]
-    do = launch(qkv_first, do)
+    first_grad = dot(a, d_first, TN).astype(BF).reshape(*out_grad.shape[:-1], -1)
+    both = jnp.concatenate([first_grad, out_grad], axis=-1)
+    mid = [by_rows(both.reshape(model, -1), short_order, False)]
     d2 = attention_gradient(2, do)
-    do, d2 = slot(down + up + out, [], (do, d2))
-    d3 = attention_gradient(3, do)
+    do, d2 = slot(down + up, mid, (do, d2))
+    d3 = slot(down + up + mid, [], attention_gradient(3, do))
     d_second = weave(d2, d3)
     qkv_second = [by_rows(dot(a, d_second, TN).astype(BF), short_order, False)]
     d_second = launch(qkv_second, d_second)
-    d_second = slot(down + up + out + qkv_first, [], d_second)
-    d = (d_first, d_second)
-    dx_recv = to_core(input_other(inverse, d, w_qkv, span))
-    input_grad, sums1 = input_own(inverse, d, w_qkv, dx_recv, x, dh, norm, span)
+    dx_sent = input_other(inverse, (d_first, d_second), w_qkv, span)
+    dx_recv = to_core(dx_sent)
+    input_grad, sums1 = input_own(
+        inverse, (d_first, d_second), w_qkv, dx_recv, x, dh, norm, span
+    )
     input_moved = swap_begin(input_grad)
     norm_grad = jnp.concatenate([sums1, sums2, sums3, sums4], axis=0)
-    share = norm_grad.reshape((8,) + (2,) * (levels + 2) + (rows,))
-    share = Reduction(jnp.moveaxis(share, 0, levels + 2), full_order, small_order, F32)
-    everything = down + up + out + qkv_first + qkv_second + [share]
-    sums1 = slot(qkv_second, [share], sums1)
-    sums1, input_moved = tie(sums1, input_moved)
+    tiles = norm_grad.reshape(8, -1, rows).transpose(1, 0, 2)
+    tiles = lax.all_to_all(tiles, everyone, 0, 0, tiled=True)
+    everything = down + up + mid + qkv_second
+    tiles = slot(everything, [], tiles)
     while any(r.flying for r in everything):
-        sums1 = slot(everything, [], sums1)
-    input_grad = swap_end(input_grad, input_moved)
+        tiles = slot(everything, [], tiles)
 
     def from_cores(part):
         return by_bit(core, pick(part, core, 0), to_core(pick(part, 1 - core, 0)))
 
     down_sum = joined(down).reshape(units, model)
-    out_sum = out[0].value.reshape(rows, model)
+    out_sum = mid[0].value[..., -half:].reshape(2, rows, half).swapaxes(0, 1).reshape(rows, model)
     up_part = joined(up).reshape(2, rows, chips, 2 * units)
     up_sum = from_cores(up_part).transpose(1, 2, 0, 3).reshape(rows, -1)
     qkv_part = jnp.stack(
-        [p[0].value.reshape(2, rows, 3, part_heads, HEAD_DIM) for p in (qkv_first, qkv_second)],
+        [
+            part.reshape(2, rows, 3, part_heads, HEAD_DIM)
+            for part in (mid[0].value[..., :-half], qkv_second[0].value)
+        ],
         axis=3,
     )
     qkv_sum = from_cores(qkv_part).transpose(1, 2, 3, 4, 0, 5).reshape(rows, -1)
@@ -952,7 +930,12 @@
     out_new = nesterov(out_sum, out_momentum, out_weight, out_average, rate_out, token_total)
     up_new = nesterov(up_sum, up_momentum, up_weight, up_average, rate_up, token_total)
     down_new = nesterov(down_sum, down_momentum, down_weight, down_average, rate_down, token_total)
-    norm_new = nesterov(share.value, norm_momentum, norm_weight, norm_average, rate_norm, token_total)
+    qkv_new, up_new, out_new, down_new, tiles, input_moved = tie(
+        qkv_new, up_new, out_new, down_new, tiles, input_moved
+    )
+    norm_sum = jnp.sum(tiles, axis=0)
+    input_grad = swap_end(input_grad, input_moved)
+    norm_new = nesterov(norm_sum, norm_momentum, norm_weight, norm_average, rate_norm, token_total)
     return (output, input_grad, *qkv_new, *out_new, *up_new, *down_new, *norm_new)
 
 

time: 577 us -> 569 us (0.986)
  waiting for transfers between devices: 73.5 us -> 53.8 us
  local copies, waits for them, and re-layouts: 39.8 us -> 58.9 us
  starting transfers between devices: 90.3 us -> 80.9 us
  other arithmetic: 58.3 us -> 66.1 us
  Pallas kernels: 252 us -> 245 us
    ppermute x67 -> x54, starting transfers between devices: 72.6 us -> 52.8 us  [exchange(): return lax.ppermute(x, everyone, [(i, i ^ mask) for i in range(4 * chips)])]
    ppermute x67 -> x54, waiting for transfers between devices: 59 us -> 47.6 us  [exchange(): return lax.ppermute(x, everyone, [(i, i ^ mask) for i in range(4 * chips)])]
    all_gather x1, waiting for transfers between devices: 8.43 us -> 0.01 us  [per_device(): w_mlp = lax.all_gather(per_owner, ('chip', 'ctx'), axis=0)]
    unnamed x183 -> x180, local copies, waits for them, and re-layouts: 7.12 us -> 15 us
    pallas_call x18 -> x17, Pallas kernels: 252 us -> 245 us  [call(): pl.pallas_call(body, grid_spec=pltpu.PrefetchScalarGridSpec(num_scalar_pr...]
    squeeze x23 -> x18, local copies, waits for them, and re-layouts: 8.19 us -> 12.4 us  [pick(): return lax.dynamic_index_in_dim(x, index, dim, keepdims=False)]
    convert_element_type x15 -> x14, other arithmetic: 11.8 us -> 13.7 us  [add(): self.value = v.astype(self.wire) if self.order else v]
    dot_general x5 -> x7, matrix products: 36.7 us -> 38.3 us  [dot(): return lax.dot_general(x, y, dims, preferred_element_type=F32)]
  transfers between devices with their start and end apart: 72 -> 60, of which waited for: 21 -> 14; matrix products, arithmetic and copies ran while one was open for 20% -> 22% of each run, Pallas kernels for 38% -> 38%
where the time goes in v4:
time: 569 us; the launch traced here: 559 us
  Pallas kernels  245 us (43%)
  starting transfers between devices  80.9 us (14%)
  other arithmetic  66.1 us (12%)
  local copies, waits for them, and re-layouts  58.9 us (10%)
  waiting for transfers between devices  53.8 us (9%)
  matrix products  38.3 us (7%)
  between operations  15.9 us (3%)
    pallas_call x17, Pallas kernels, call(): pl.pallas_call(body, grid_spec=pltpu.PrefetchScalarGridSpec(num_scalar_pr...  245 us
    ppermute x54, starting transfers between devices, exchange(): return lax.ppermute(x, everyone, [(i, i ^ mask) for i in range(4 * chips)])  52.8 us
    ppermute x54, waiting for transfers between devices, exchange(): return lax.ppermute(x, everyone, [(i, i ^ mask) for i in range(4 * chips)])  47.6 us
    dot_general x7, matrix products, dot(): return lax.dot_general(x, y, dims, preferred_element_type=F32)  38.3 us
    ppermute x4, starting transfers between devices, swap_begin(): return lax.ppermute(x, ('core', 'ctx'), [(1, 2), (2, 1)])  22.9 us
    unnamed x180, local copies, waits for them, and re-layouts  15 us
    convert_element_type x14, other arithmetic, add(): self.value = v.astype(self.wire) if self.order else v  13.7 us
    squeeze x18, local copies, waits for them, and re-layouts, pick(): return lax.dynamic_index_in_dim(x, index, dim, keepdims=False)  12.4 us
  transfers between devices with their start and end apart: 60, of which 14 were waited for; matrix products, arithmetic and copies ran while one was open for 22% of the time, Pallas kernels for 38%

profile of v4, /device:TPU:1, one launch (start us, length us, event | category | flops | bytes accessed | tf_op | source)
XLA Modules:
  0.0 558.7 jit_solution(15920053989435177307)
XLA Ops:
  55.3 9.0 %collective-permute-done.9 = bf16[2,32,1280]{2,1,0:T(8,128)(2,1)S(1)} collective-permute-done((bf16[2,32,1280]{2,1,0:T(8,128)(2,1)S(1)}, bf16[2,32,1280]{2,1,0:T(8,128)(2,1)S(1)}, u32[]{:S(2)}, u32[]{:S(2)}) %collective-permute-start.9) | collective-permute-done | bytes 163872 | tf_op jit(solution)/shard_map/ppermute | solution.py:603
  75.5 9.4 %collective-permute-done.14 = bf16[2,2,2,32,1280]{4,3,2,1,0:T(8,128)(2,1)S(1)} collective-permute-done((bf16[2,2,2,32,1280]{4,3,2,1,0:T(8,128)(2,1)S(1)}, bf16[2,2,2,32,1280]{4,3,2,1,0:T(8,128)(2,1)S(1)}, u32[]{:S(2)}, u32[]{:S(2)}) %collective-permute-start.14) | collective-permute-done | bytes 655392 | tf_op jit(solution)/shard_map/ppermute | solution.py:603
  84.9 5.9 %collective-permute-done.13 = bf16[2,2,2,72,768]{4,3,1,0,2:T(8,128)(2,1)S(1)} collective-permute-done((bf16[2,2,2,72,768]{4,3,1,0,2:T(8,128)(2,1)S(1)}, bf16[2,2,2,72,768]{4,3,1,0,2:T(8,128)(2,1)S(1)}, u32[]{:S(2)}, u32[]{:S(2)}) %collective-permute-start.13) | collective-permute-done | bytes 884768 | tf_op jit(solution)/shard_map/ppermute | solution.py:603
  95.5 13.1 %shard_map.341 = (bf16[2048,1024]{1,0:T(8,128)(2,1)}, bf16[2048,256]{1,0:T(8,128)(2,1)}, bf16[2048,256]{1,0:T(8,128)(2,1)}, bf16[2048,256]{1,0:T(8,128)(2,1)}) custom-call(s32[4]{0:T(128)} %broadcast_select_fusion.11.inverse, bf16[1024,1024]{1,0:T(8,128)(2,1)} %copy-done, bf16[1024,1024]{1,0:T(8,128)(2,1)} %collective-permute-done.12.other_ref, ...), custom_call_target="tpu_custom_call" | custom-call | tf_op jit(solution)/shard_map/pallas_call | solution.py:37
  108.6 12.7 %collective-permute-start.16 = (bf16[1024,1024]{1,0:T(8,128)(2,1)S(1)}, bf16[1024,1024]{1,0:T(8,128)(2,1)}, u32[]{:S(2)}, u32[]{:S(2)}) collective-permute-start(bf16[1024,1024]{1,0:T(8,128)(2,1)S(1)} %copy-done.21), channel_id=1, source_target_pairs={{1,2},{2,1},{5,6},{6,5},{9,10},{10,9},{13,14},{14,13},{17,18},{18,... | collective-permute-start | bytes 6291464 | tf_op jit(solution)/shard_map/ppermute | solution.py:609
  121.3 19.2 %shard_map.342 = (bf16[1024,256]{1,0:T(8,128)(2,1)}, bf16[1024,256]{1,0:T(8,128)(2,1)}, f32[32,2048]{1,0:T(8,128)}) custom-call(s32[4]{0:T(128)} %broadcast_select_fusion.10.place, bf16[2048,256]{1,0:T(8,128)(2,1)} %get-tuple-element.269.q_ref, bf16[2048,256]{1,0:T(8,128)(2,1)} %get-tuple-element.270.k_ref, bf16[2048,256]{1,0:T(8,128)(2,1)} %get-tuple-element.271.v_ref), custom_call_target="tpu_custom_call" | custom-call | tf_op jit(solution)/shard_map/pallas_call | solution.py:37
  144.5 8.0 %shard_map.343 = (bf16[2048,256]{1,0:T(8,128)(2,1)}, bf16[2048,256]{1,0:T(8,128)(2,1)}, bf16[2048,256]{1,0:T(8,128)(2,1)}) custom-call(bf16[2048,1024]{1,0:T(8,128)(2,1)} %get-tuple-element.280.a_ref, bf16[1024,768]{1,0:T(8,128)(2,1)} %bitcast.273, f32[2048,128]{1,0:T(8,128)} %pad_maximum_fusion.3.cos_ref, f32[2048,128]{1,0:T(8,128)} %pad_maximum_fusion.4.sin_ref), custom_call_target="tpu_custom_call" | custom-call | tf_op jit(solution)/shard_map/pallas_call | solution.py:37
  152.5 19.5 %shard_map.344 = (bf16[1024,256]{1,0:T(8,128)(2,1)}, bf16[1024,256]{1,0:T(8,128)(2,1)}, f32[32,2048]{1,0:T(8,128)}) custom-call(s32[4]{0:T(128)} %broadcast_select_fusion.10.place, bf16[2048,256]{1,0:T(8,128)(2,1)} %get-tuple-element.282.q_ref, bf16[2048,256]{1,0:T(8,128)(2,1)} %get-tuple-element.283.k_ref, bf16[2048,256]{1,0:T(8,128)(2,1)} %get-tuple-element.284.v_ref), custom_call_target="tpu_custom_call" | custom-call | tf_op jit(solution)/shard_map/pallas_call | solution.py:37
  177.6 9.3 %shard_map.345 = (f32[1024,1024]{1,0:T(8,128)}, f32[1024,1024]{1,0:T(8,128)}, bf16[1024,1024]{1,0:T(8,128)(2,1)}) custom-call(bf16[1024,256]{1,0:T(8,128)(2,1)} %get-tuple-element.279.m0_ref.own_ref, bf16[1024,256]{1,0:T(8,128)(2,1)} %get-tuple-element.288.m1_ref.own_ref, bf16[1024,256]{1,0:T(8,128)(2,1)} %collective-permute-done.17.o0_ref, ...), custom_call_target="tpu_custom_call" | custom-call | tf_op jit(solution)/shard_map/pallas_call | solution.py:37
  191.4 18.1 %shard_map.347 = (bf16[1024,2048]{1,0:T(8,128)(2,1)}, bf16[1024,2048]{1,0:T(8,128)(2,1)}, bf16[1024,1024]{1,0:T(8,128)(2,1)}) custom-call(bf16[1024,1024]{1,0:T(8,128)(2,1)} %collective-permute-done.20.c_ref, bf16[16,4,64,1024]{3,2,1,0:T(8,128)(2,1)} %bitcast.265, bf16[16,2,128,1024]{3,2,1,0:T(8,128)(2,1)} %bitcast.266), custom_call_target="tpu_custom_call" | custom-call | tf_op jit(solution)/shard_map/pallas_call | solution.py:37
  213.2 18.4 %shard_map.346 = (bf16[1024,2048]{1,0:T(8,128)(2,1)}, bf16[1024,2048]{1,0:T(8,128)(2,1)}, f32[1024,1024]{1,0:T(8,128)}) custom-call(bf16[1024,1024]{1,0:T(8,128)(2,1)} %get-tuple-element.291.c_ref, bf16[16,4,64,1024]{3,2,1,0:T(8,128)(2,1)} %bitcast.267, bf16[16,2,128,1024]{3,2,1,0:T(8,128)(2,1)} %bitcast.268), custom_call_target="tpu_custom_call" | custom-call | tf_op jit(solution)/shard_map/pallas_call | solution.py:37
  233.0 8.7 %shard_map.348 = (bf16[1024,1024]{1,0:T(8,128)(2,1)}, bf16[1024,1024]{1,0:T(8,128)(2,1)}, f32[2,1024]{1,0:T(2,128)}) custom-call(f32[1024,1024]{1,0:T(8,128)} %get-tuple-element.293.m_ref, bf16[1024,1024]{1,0:T(8,128)(2,1)} %copy-done.38, f32[1024,1024]{1,0:T(8,128)} %get-tuple-element.295.h_ref, bf16[1024,1024]{1,0:T(8,128)(2,1)} %broadcast_select_fusion.2.y_ref, ...), custom_call_target="tpu_custom_call" | custom-call | tf_op jit(solution)/shard_map/pallas_call | solution.py:37
  241.7 16.3 %shard_map.350 = (bf16[1024,2048]{1,0:T(8,128)(2,1)}, f32[1024,1024]{1,0:T(8,128)}) custom-call(bf16[1024,1024]{1,0:T(8,128)(2,1)} %get-tuple-element.298.dm_ref, bf16[1024,2048]{1,0:T(8,128)(2,1)} %get-tuple-element.302.s_ref, bf16[16,4,64,1024]{3,2,1,0:T(8,128)(2,1)} %bitcast.269, bf16[16,2,128,1024]{3,2,1,0:T(8,128)(2,1)} %bitcast.270), custom_call_target="tpu_custom_call" | custom-call | tf_op jit(solution)/shard_map/pallas_call | solution.py:37
  260.3 12.6 %fusion.19 = bf16[2048,1024]{1,0:T(8,128)(2,1)S(1)} fusion(bf16[1024,1024]{1,0:T(8,128)(2,1)} %collective-permute-done.22.dm_ref, bf16[1024,1024]{1,0:T(8,128)(2,1)S(1)} %copy-done.39, bf16[1024,2048]{1,0:T(8,128)(2,1)} %get-tuple-element.306, bf16[1024,2048]{1,0:T(8,128)(2,1)} %get-tuple-element.305), kind=kOutput, calls=%fused_computation.19 | convolution fusion | flops 8617197568 | bytes 16777216 | tf_op jit(solution)/shard_map/dot_general | solution.py:33
  275.5 15.5 %shard_map.349 = (bf16[1024,2048]{1,0:T(8,128)(2,1)}, bf16[1024,1024]{1,0:T(8,128)(2,1)}) custom-call(bf16[1024,1024]{1,0:T(8,128)(2,1)} %collective-permute-done.22.dm_ref, bf16[1024,2048]{1,0:T(8,128)(2,1)} %get-tuple-element.299.s_ref, bf16[16,4,64,1024]{3,2,1,0:T(8,128)(2,1)} %bitcast.271, bf16[16,2,128,1024]{3,2,1,0:T(8,128)(2,1)} %bitcast.272), custom_call_target="tpu_custom_call" | custom-call | tf_op jit(solution)/shard_map/pallas_call | solution.py:37
  292.7 12.1 %fusion.14 = bf16[1024,2048]{1,0:T(8,128)(2,1)S(1)} fusion(bf16[1024,2048]{1,0:T(8,128)(2,1)} %get-tuple-element.312, bf16[1024,2048]{1,0:T(8,128)(2,1)} %get-tuple-element.311, bf16[1024,1024]{1,0:T(8,128)(2,1)} %collective-permute-done.20.c_ref, bf16[1024,1024]{1,0:T(8,128)(2,1)S(1)} %copy-done.25), kind=kOutput, calls=%fused_computation.18 | convolution fusion | flops 8617197568 | bytes 16777216 | tf_op jit(solution)/shard_map/dot_general | solution.py:33
  308.7 12.8 %shard_map.351 = (f32[1024,1024]{1,0:T(8,128)}, bf16[1024,1024]{1,0:T(8,128)(2,1)}, f32[2,1024]{1,0:T(2,128)}, f32[2,1024]{1,0:T(2,128)}) custom-call(f32[1024,1024]{1,0:T(8,128)} %get-tuple-element.314.dc_ref, bf16[1024,1024]{1,0:T(8,128)(2,1)} %collective-permute-done.26.r_ref, f32[1024,1024]{1,0:T(8,128)} %get-tuple-element.295.h_ref, ...), custom_call_target="tpu_custom_call" | custom-call | tf_op jit(solution)/shard_map/pallas_call | solution.py:37
  340.5 16.6 %shard_map.352 = (bf16[2048,128]{1,0:T(8,128)(2,1)}, bf16[2048,128]{1,0:T(8,128)(2,1)}, bf16[2048,128]{1,0:T(8,128)(2,1)}) custom-call(s32[4]{0:T(128)} %broadcast_select_fusion.10.place, bf16[2048,256]{1,0:T(8,128)(2,1)} %get-tuple-element.269.q_ref, bf16[2048,256]{1,0:T(8,128)(2,1)} %get-tuple-element.270.k_ref, ...), custom_call_target="tpu_custom_call" | custom-call | tf_op jit(solution)/shard_map/pallas_call | solution.py:37
  361.1 16.8 %shard_map.353 = (bf16[2048,128]{1,0:T(8,128)(2,1)}, bf16[2048,128]{1,0:T(8,128)(2,1)}, bf16[2048,128]{1,0:T(8,128)(2,1)}) custom-call(s32[4]{0:T(128)} %broadcast_select_fusion.10.place, bf16[2048,256]{1,0:T(8,128)(2,1)} %get-tuple-element.269.q_ref, bf16[2048,256]{1,0:T(8,128)(2,1)} %get-tuple-element.270.k_ref, ...), custom_call_target="tpu_custom_call" | custom-call | tf_op jit(solution)/shard_map/pallas_call | solution.py:37
  395.8 16.5 %shard_map.354 = (bf16[2048,128]{1,0:T(8,128)(2,1)}, bf16[2048,128]{1,0:T(8,128)(2,1)}, bf16[2048,128]{1,0:T(8,128)(2,1)}) custom-call(s32[4]{0:T(128)} %broadcast_select_fusion.10.place, bf16[2048,256]{1,0:T(8,128)(2,1)} %get-tuple-element.282.q_ref, bf16[2048,256]{1,0:T(8,128)(2,1)} %get-tuple-element.283.k_ref, ...), custom_call_target="tpu_custom_call" | custom-call | tf_op jit(solution)/shard_map/pallas_call | solution.py:37
  420.7 16.6 %shard_map.355 = (bf16[2048,128]{1,0:T(8,128)(2,1)}, bf16[2048,128]{1,0:T(8,128)(2,1)}, bf16[2048,128]{1,0:T(8,128)(2,1)}) custom-call(s32[4]{0:T(128)} %broadcast_select_fusion.10.place, bf16[2048,256]{1,0:T(8,128)(2,1)} %get-tuple-element.282.q_ref, bf16[2048,256]{1,0:T(8,128)(2,1)} %get-tuple-element.283.k_ref, ...), custom_call_target="tpu_custom_call" | custom-call | tf_op jit(solution)/shard_map/pallas_call | solution.py:37
  437.4 6.3 %collective-permute-done.42 = bf16[2,2,2,32,1280]{4,3,2,1,0:T(8,128)(2,1)} collective-permute-done((bf16[2,2,2,32,1280]{4,3,2,1,0:T(8,128)(2,1)}, bf16[2,2,2,32,1280]{4,3,2,1,0:T(8,128)(2,1)}, u32[]{:S(2)}, u32[]{:S(2)}) %collective-permute-start.42) | collective-permute-done | bytes 655392 | tf_op jit(solution)/shard_map/ppermute | solution.py:603
  457.1 7.7 %shard_map.356 = bf16[1024,1024]{1,0:T(8,128)(2,1)} custom-call(s32[4]{0:T(128)} %broadcast_select_fusion.11.inverse, bf16[2048,768]{1,0:T(8,128)(2,1)} %copy-done.2, bf16[2048,768]{1,0:T(8,128)(2,1)} %copy-done.3, bf16[1024,768]{1,0:T(8,128)(2,1)} %bitcast.279, bf16[1024,768]{1,0:T(8,128)(2,1)} %bitcast.274), custom_call_target="tpu_custom_call" | custom-call | tf_op jit(solution)/shard_map/pallas_call | solution.py:37
  480.0 11.6 %shard_map.357 = (bf16[1024,1024]{1,0:T(8,128)(2,1)}, f32[2,1024]{1,0:T(2,128)}) custom-call(s32[4]{0:T(128)} %broadcast_select_fusion.11.inverse, bf16[2048,768]{1,0:T(8,128)(2,1)} %copy-done.2, bf16[2048,768]{1,0:T(8,128)(2,1)} %copy-done.3, bf16[1024,768]{1,0:T(8,128)(2,1)} %bitcast.280, bf16[1024,768]{1,0:T(8,128)(2,1)} %bitcast.275, ...), custom_call_target="tpu_custom_call" | custom-call | tf_op jit(solution)/shard_map/pallas_call | solution.py:37
  (450 shorter events, 230.0 us)
Async XLA Ops:
  7.2 184.2 %all-gather.3.cloned.1.call-start = ((), (), s32[]{:S(2)}) async-start(), calls=%async_computation.1 | async-start | bytes 8912896 | tf_op jit(solution)/shard_map/all_gather | solution.py:731
  7.3 28.6 %collective-permute-start.6 = (bf16[1024,1024]{1,0:T(8,128)(2,1)}, bf16[1024,1024]{1,0:T(8,128)(2,1)S(1)}, u32[]{:S(2)}, u32[]{:S(2)}) collective-permute-start(bf16[1024,1024]{1,0:T(8,128)(2,1)} %param.22), channel_id=1, source_target_pairs={{1,2},{2,1},{5,6},{6,5},{9,10},{10,9},{13,14},{14,13},{17,18},{18,... | collective-permute-start | bytes 6291464 | tf_op jit(solution)/shard_map/ppermute | solution.py:609
  39.4 24.9 %collective-permute-start.12 = (bf16[1024,1024]{1,0:T(8,128)(2,1)S(1)}, bf16[1024,1024]{1,0:T(8,128)(2,1)}, u32[]{:S(2)}, u32[]{:S(2)}) collective-permute-start(bf16[1024,1024]{1,0:T(8,128)(2,1)S(1)} %broadcast_select_fusion.3.own_ref.x_ref), channel_id=1, source_target_pairs={{0,2},{1,3},{2,0},{3,1},{4,6},{5,7},{6,4},{7,5},{8,10},{9,11},{10,... | collective-permute-start | bytes 6291464 | tf_op jit(solution)/shard_map/ppermute | solution.py:603
  64.7 26.1 %collective-permute-start.13 = (bf16[2,2,2,72,768]{4,3,1,0,2:T(8,128)(2,1)S(1)}, bf16[2,2,2,72,768]{4,3,1,0,2:T(8,128)(2,1)S(1)}, u32[]{:S(2)}, u32[]{:S(2)}) collective-permute-start(bf16[2,2,2,72,768]{4,3,1,0,2:T(8,128)(2,1)S(1)} %pad_maximum_fusion.6), channel_id=1, source_target_pairs={{0,4},{1,5},{2,6},{3,7},{4,0},{5,1},{6,2},{7,3},{8,12},{9,13},{10,... | collective-permute-start | bytes 2654216 | tf_op jit(solution)/shard_map/ppermute | solution.py:603
  91.8 48.7 %collective-permute-start.15 = (bf16[2,2,2,2,32,1280]{5,4,2,1,0,3:T(8,128)(2,1)S(1)}, bf16[2,2,2,2,32,1280]{5,4,2,1,0,3:T(8,128)(2,1)S(1)}, u32[]{:S(2)}, u32[]{:S(2)}) collective-permute-start(bf16[2,2,2,2,32,1280]{5,4,2,1,0,3:T(8,128)(2,1)S(1)} %pad_maximum_fusion.2), channel_id=1, source_target_pairs={{0,4},{1,5},{2,6},{3,7},{4,0},{5,1},{6,2},{7,3},{8,12},{9,13},{10,... | collective-permute-start | bytes 3932168 | tf_op jit(solution)/shard_map/ppermute | solution.py:603
  108.6 66.4 %collective-permute-start.16 = (bf16[1024,1024]{1,0:T(8,128)(2,1)S(1)}, bf16[1024,1024]{1,0:T(8,128)(2,1)}, u32[]{:S(2)}, u32[]{:S(2)}) collective-permute-start(bf16[1024,1024]{1,0:T(8,128)(2,1)S(1)} %copy-done.21), channel_id=1, source_target_pairs={{1,2},{2,1},{5,6},{6,5},{9,10},{10,9},{13,14},{14,13},{17,18},{18,... | collective-permute-start | bytes 6291464 | tf_op jit(solution)/shard_map/ppermute | solution.py:609
  142.6 35.0 %collective-permute-start.19 = (bf16[512,1024]{1,0:T(8,128)(2,1)S(1)}, bf16[512,1024]{1,0:T(8,128)(2,1)}, u32[]{:S(2)}, u32[]{:S(2)}) collective-permute-start(bf16[512,1024]{1,0:T(8,128)(2,1)S(1)} %bitcast.294), channel_id=1, source_target_pairs={{0,2},{1,3},{2,0},{3,1},{4,6},{5,7},{6,4},{7,5},{8,10},{9,11},{10,... | collective-permute-start | bytes 3145736 | tf_op jit(solution)/shard_map/ppermute | solution.py:603
  144.1 33.4 %collective-permute-start.17 = (bf16[1024,256]{1,0:T(8,128)(2,1)S(1)}, bf16[1024,256]{1,0:T(8,128)(2,1)}, u32[]{:S(2)}, u32[]{:S(2)}) collective-permute-start(bf16[1024,256]{1,0:T(8,128)(2,1)S(1)} %copy-done.28), channel_id=1, source_target_pairs={{0,2},{1,3},{2,0},{3,1},{4,6},{5,7},{6,4},{7,5},{8,10},{9,11},{10,... | collective-permute-start | bytes 1572872 | tf_op jit(solution)/shard_map/ppermute | solution.py:603
  258.0 33.0 %collective-permute-start.23 = (bf16[1024,1024]{1,0:T(8,128)(2,1)}, bf16[1024,1024]{1,0:T(8,128)(2,1)}, u32[]{:S(2)}, u32[]{:S(2)}) collective-permute-start(bf16[1024,1024]{1,0:T(8,128)(2,1)} %get-tuple-element.297), channel_id=1, source_target_pairs={{1,2},{2,1},{5,6},{6,5},{9,10},{10,9},{13,14},{14,13},{17,18},{18,... | collective-permute-start | bytes 6291464 | tf_op jit(solution)/shard_map/ppermute | solution.py:609
  291.3 30.3 %collective-permute-start.24 = (bf16[2,2,2,128,512]{4,3,0,1,2:T(8,128)(2,1)}, bf16[2,2,2,128,512]{4,3,0,1,2:T(8,128)(2,1)S(1)}, u32[]{:S(2)}, u32[]{:S(2)}) collective-permute-start(bf16[2,2,2,128,512]{4,3,0,1,2:T(8,128)(2,1)} %bitcast.304), channel_id=1, source_target_pairs={{0,4},{1,5},{2,6},{3,7},{4,0},{5,1},{6,2},{7,3},{8,12},{9,13},{10,... | collective-permute-start | bytes 3145736 | tf_op jit(solution)/shard_map/ppermute | solution.py:603
  292.5 29.1 %collective-permute-start.25 = (bf16[2,2,2,128,512]{4,3,0,1,2:T(8,128)(2,1)}, bf16[2,2,2,128,512]{4,3,0,1,2:T(8,128)(2,1)}, u32[]{:S(2)}, u32[]{:S(2)}) collective-permute-start(bf16[2,2,2,128,512]{4,3,0,1,2:T(8,128)(2,1)} %bitcast.303), channel_id=1, source_target_pairs={{0,1},{1,0},{2,3},{3,2},{4,5},{5,4},{6,7},{7,6},{8,9},{9,8},{10,11... | collective-permute-start | bytes 3145736 | tf_op jit(solution)/shard_map/ppermute | solution.py:603
  327.4 29.7 %collective-permute-start.27 = (bf16[2,2,128,512]{3,2,0,1:T(8,128)(2,1)}, bf16[2,2,128,512]{3,2,0,1:T(8,128)(2,1)S(1)}, u32[]{:S(2)}, u32[]{:S(2)}) collective-permute-start(bf16[2,2,128,512]{3,2,0,1:T(8,128)(2,1)} %dynamic-slice_bitcast_fusion.4), channel_id=1, source_target_pairs={{0,1},{1,0},{2,3},{3,2},{4,5},{5,4},{6,7},{7,6},{8,9},{9,8},{10,11... | collective-permute-start | bytes 1572872 | tf_op jit(solution)/shard_map/ppermute | solution.py:603
  328.7 28.4 %collective-permute-start.28 = (bf16[2,2,128,512]{3,2,0,1:T(8,128)(2,1)}, bf16[2,2,128,512]{3,2,0,1:T(8,128)(2,1)S(1)}, u32[]{:S(2)}, u32[]{:S(2)}) collective-permute-start(bf16[2,2,128,512]{3,2,0,1:T(8,128)(2,1)} %dynamic-slice_bitcast_fusion.3), channel_id=1, source_target_pairs={{0,4},{1,5},{2,6},{3,7},{4,0},{5,1},{6,2},{7,3},{8,12},{9,13},{10,... | collective-permute-start | bytes 1572872 | tf_op jit(solution)/shard_map/ppermute | solution.py:603
  328.8 49.2 %collective-permute-start.32 = (bf16[2,2,2,64,1024]{4,3,0,1,2:T(8,128)(2,1)}, bf16[2,2,2,64,1024]{4,3,0,1,2:T(8,128)(2,1)}, u32[]{:S(2)}, u32[]{:S(2)}) collective-permute-start(bf16[2,2,2,64,1024]{4,3,0,1,2:T(8,128)(2,1)} %bitcast.302), channel_id=1, source_target_pairs={{0,4},{1,5},{2,6},{3,7},{4,0},{5,1},{6,2},{7,3},{8,12},{9,13},{10,... | collective-permute-start | bytes 3145736 | tf_op jit(solution)/shard_map/ppermute | solution.py:603
  330.1 47.9 %collective-permute-start.33 = (bf16[2,2,2,64,1024]{4,3,2,1,0:T(8,128)(2,1)}, bf16[2,2,2,64,1024]{4,3,2,1,0:T(8,128)(2,1)}, u32[]{:S(2)}, u32[]{:S(2)}) collective-permute-start(bf16[2,2,2,64,1024]{4,3,2,1,0:T(8,128)(2,1)} %dynamic-slice_bitcast_fusion), channel_id=1, source_target_pairs={{0,1},{1,0},{2,3},{3,2},{4,5},{5,4},{6,7},{7,6},{8,9},{9,8},{10,11... | collective-permute-start | bytes 3145736 | tf_op jit(solution)/shard_map/ppermute | solution.py:603
  385.0 27.3 %collective-permute-start.36 = (bf16[2,2,64,1024]{3,2,0,1:T(8,128)(2,1)S(1)}, bf16[2,2,64,1024]{3,2,0,1:T(8,128)(2,1)S(1)}, u32[]{:S(2)}, u32[]{:S(2)}) collective-permute-start(bf16[2,2,64,1024]{3,2,0,1:T(8,128)(2,1)S(1)} %dynamic-slice_bitcast_fusion.2), channel_id=1, source_target_pairs={{0,1},{1,0},{2,3},{3,2},{4,5},{5,4},{6,7},{7,6},{8,9},{9,8},{10,11... | collective-permute-start | bytes 1572872 | tf_op jit(solution)/shard_map/ppermute | solution.py:603
  386.4 26.0 %collective-permute-start.37 = (bf16[2,2,64,1024]{3,2,1,0:T(8,128)(2,1)S(1)}, bf16[2,2,64,1024]{3,2,1,0:T(8,128)(2,1)S(1)}, u32[]{:S(2)}, u32[]{:S(2)}) collective-permute-start(bf16[2,2,64,1024]{3,2,1,0:T(8,128)(2,1)S(1)} %dynamic-slice_bitcast_fusion.1), channel_id=1, source_target_pairs={{0,4},{1,5},{2,6},{3,7},{4,0},{5,1},{6,2},{7,3},{8,12},{9,13},{10,... | collective-permute-start | bytes 1572872 | tf_op jit(solution)/shard_map/ppermute | solution.py:603
  386.5 25.8 %collective-permute-start.34 = (bf16[128,512]{1,0:T(8,128)(2,1)S(1)}, bf16[128,512]{1,0:T(8,128)(2,1)S(1)}, u32[]{:S(2)}, u32[]{:S(2)}) collective-permute-start(bf16[128,512]{1,0:T(8,128)(2,1)S(1)} %dynamic-slice_bitcast_fusion.20), channel_id=1, source_target_pairs={{0,16},{1,17},{2,18},{3,19},{4,20},{5,21},{6,22},{7,23},{8,24},{9,... | collective-permute-start | bytes 393224 | tf_op jit(solution)/shard_map/ppermute | solution.py:603
  416.6 27.2 %collective-permute-start.42 = (bf16[2,2,2,32,1280]{4,3,2,1,0:T(8,128)(2,1)}, bf16[2,2,2,32,1280]{4,3,2,1,0:T(8,128)(2,1)}, u32[]{:S(2)}, u32[]{:S(2)}) collective-permute-start(bf16[2,2,2,32,1280]{4,3,2,1,0:T(8,128)(2,1)} %get-tuple-element.379), channel_id=1, source_target_pairs={{0,5},{1,4},{2,7},{3,6},{4,1},{5,0},{6,3},{7,2},{8,13},{9,12},{10,... | collective-permute-start | bytes 1966088 | tf_op jit(solution)/shard_map/ppermute | solution.py:603
  472.8 28.6 %collective-permute-start.46 = (bf16[2,32,1280]{2,1,0:T(8,128)(2,1)}, bf16[2,32,1280]{2,1,0:T(8,128)(2,1)}, u32[]{:S(2)}, u32[]{:S(2)}) collective-permute-start(bf16[2,32,1280]{2,1,0:T(8,128)(2,1)} %get-tuple-element.402), channel_id=1, source_target_pairs={{0,16},{1,17},{2,18},{3,19},{4,20},{5,21},{6,22},{7,23},{8,24},{9,... | collective-permute-start | bytes 491528 | tf_op jit(solution)/shard_map/ppermute | solution.py:603
  475.2 24.8 %collective-permute-start.45 = (bf16[64,1024]{1,0:T(8,128)(2,1)}, bf16[64,1024]{1,0:T(8,128)(2,1)}, u32[]{:S(2)}, u32[]{:S(2)}) collective-permute-start(bf16[64,1024]{1,0:T(8,128)(2,1)} %dynamic-slice_bitcast_fusion.17), channel_id=1, source_target_pairs={{0,16},{1,17},{2,18},{3,19},{4,20},{5,21},{6,22},{7,23},{8,24},{9,... | collective-permute-start | bytes 393224 | tf_op jit(solution)/shard_map/ppermute | solution.py:603
  478.1 34.2 %collective-permute-start.49 = (bf16[2,2,2,32,768]{4,3,2,1,0:T(8,128)(2,1)}, bf16[2,2,2,32,768]{4,3,2,1,0:T(8,128)(2,1)}, u32[]{:S(2)}, u32[]{:S(2)}) collective-permute-start(bf16[2,2,2,32,768]{4,3,2,1,0:T(8,128)(2,1)} %get-tuple-element.405), channel_id=1, source_target_pairs={{0,1},{1,0},{2,3},{3,2},{4,5},{5,4},{6,7},{7,6},{8,9},{9,8},{10,11... | collective-permute-start | bytes 1179656 | tf_op jit(solution)/shard_map/ppermute | solution.py:603
  478.6 33.7 %collective-permute-start.50 = (bf16[2,2,2,32,768]{4,3,2,1,0:T(8,128)(2,1)}, bf16[2,2,2,32,768]{4,3,2,1,0:T(8,128)(2,1)}, u32[]{:S(2)}, u32[]{:S(2)}) collective-permute-start(bf16[2,2,2,32,768]{4,3,2,1,0:T(8,128)(2,1)} %get-tuple-element.406), channel_id=1, source_target_pairs={{0,4},{1,5},{2,6},{3,7},{4,0},{5,1},{6,2},{7,3},{8,12},{9,13},{10,... | collective-permute-start | bytes 1179656 | tf_op jit(solution)/shard_map/ppermute | solution.py:603
  509.0 38.8 %collective-permute-start.57 = (bf16[1024,1024]{1,0:T(8,128)(2,1)S(1)}, bf16[1024,1024]{1,0:T(8,128)(2,1)}, u32[]{:S(2)}, u32[]{:S(2)}) collective-permute-start(bf16[1024,1024]{1,0:T(8,128)(2,1)S(1)} %copy-done.23), channel_id=1, source_target_pairs={{1,2},{2,1},{5,6},{6,5},{9,10},{10,9},{13,14},{14,13},{17,18},{18,... | collective-permute-start | bytes 6291464 | tf_op jit(solution)/shard_map/ppermute | solution.py:609
  (118 other events, 1094.7 us)
Sparse Core Ops, SparseCore 0:
  37.6 148.9 all-gather.2

commit v5 on v4

--- a/solution.py
+++ b/solution.py
@@ -371,7 +371,7 @@
     add_to(sums_ref, column_sums(z, xhat))
 
 
-def turn(m_part, m_other, h, y, norm, rows=256):
+def turn(m_part, m_other, h, y, norm, rows=512):
     tokens, model = y.shape
     row = pl.BlockSpec((rows, model), lambda i: (i, 0))
     return call(

time: 569 us -> 569 us (level)
  transfers between devices with their start and end apart: 60 -> 60, of which waited for: 14 -> 15; matrix products, arithmetic and copies ran while one was open for 22% -> 22% of each run, Pallas kernels for 38% -> 38%
where the time goes in v5:
time: 569 us; the launch traced here: 559 us
  Pallas kernels  245 us (43%)
  starting transfers between devices  80.8 us (14%)
  other arithmetic  65.8 us (12%)
  local copies, waits for them, and re-layouts  58.9 us (10%)
  waiting for transfers between devices  54.3 us (10%)
  matrix products  38 us (7%)
  between operations  16.2 us (3%)
    pallas_call x17, Pallas kernels, call(): pl.pallas_call(body, grid_spec=pltpu.PrefetchScalarGridSpec(num_scalar_pr...  245 us
    ppermute x54, starting transfers between devices, exchange(): return lax.ppermute(x, everyone, [(i, i ^ mask) for i in range(4 * chips)])  52.1 us
    ppermute x54, waiting for transfers between devices, exchange(): return lax.ppermute(x, everyone, [(i, i ^ mask) for i in range(4 * chips)])  47.9 us
    dot_general x7, matrix products, dot(): return lax.dot_general(x, y, dims, preferred_element_type=F32)  38 us
    ppermute x4, starting transfers between devices, swap_begin(): return lax.ppermute(x, ('core', 'ctx'), [(1, 2), (2, 1)])  23.1 us
    unnamed x180, local copies, waits for them, and re-layouts  15 us
    convert_element_type x14, other arithmetic, add(): self.value = v.astype(self.wire) if self.order else v  13.7 us
    squeeze x18, local copies, waits for them, and re-layouts, pick(): return lax.dynamic_index_in_dim(x, index, dim, keepdims=False)  12.4 us
  transfers between devices with their start and end apart: 60, of which 15 were waited for; matrix products, arithmetic and copies ran while one was open for 22% of the time, Pallas kernels for 38%

profile of v5, /device:TPU:1, one launch (start us, length us, event | category | flops | bytes accessed | tf_op | source)
XLA Modules:
  0.0 559.3 jit_solution(13971189859340682481)
XLA Ops:
  55.3 9.0 %collective-permute-done.9 = bf16[2,32,1280]{2,1,0:T(8,128)(2,1)S(1)} collective-permute-done((bf16[2,32,1280]{2,1,0:T(8,128)(2,1)S(1)}, bf16[2,32,1280]{2,1,0:T(8,128)(2,1)S(1)}, u32[]{:S(2)}, u32[]{:S(2)}) %collective-permute-start.9) | collective-permute-done | bytes 163872 | tf_op jit(solution)/shard_map/ppermute | solution.py:603
  75.5 9.4 %collective-permute-done.14 = bf16[2,2,2,32,1280]{4,3,2,1,0:T(8,128)(2,1)S(1)} collective-permute-done((bf16[2,2,2,32,1280]{4,3,2,1,0:T(8,128)(2,1)S(1)}, bf16[2,2,2,32,1280]{4,3,2,1,0:T(8,128)(2,1)S(1)}, u32[]{:S(2)}, u32[]{:S(2)}) %collective-permute-start.14) | collective-permute-done | bytes 655392 | tf_op jit(solution)/shard_map/ppermute | solution.py:603
  84.9 5.9 %collective-permute-done.13 = bf16[2,2,2,72,768]{4,3,1,0,2:T(8,128)(2,1)S(1)} collective-permute-done((bf16[2,2,2,72,768]{4,3,1,0,2:T(8,128)(2,1)S(1)}, bf16[2,2,2,72,768]{4,3,1,0,2:T(8,128)(2,1)S(1)}, u32[]{:S(2)}, u32[]{:S(2)}) %collective-permute-start.13) | collective-permute-done | bytes 884768 | tf_op jit(solution)/shard_map/ppermute | solution.py:603
  95.2 13.1 %shard_map.341 = (bf16[2048,1024]{1,0:T(8,128)(2,1)}, bf16[2048,256]{1,0:T(8,128)(2,1)}, bf16[2048,256]{1,0:T(8,128)(2,1)}, bf16[2048,256]{1,0:T(8,128)(2,1)}) custom-call(s32[4]{0:T(128)} %broadcast_select_fusion.11.inverse, bf16[1024,1024]{1,0:T(8,128)(2,1)} %copy-done, bf16[1024,1024]{1,0:T(8,128)(2,1)} %collective-permute-done.12.other_ref, ...), custom_call_target="tpu_custom_call" | custom-call | tf_op jit(solution)/shard_map/pallas_call | solution.py:37
  108.3 12.9 %collective-permute-start.16 = (bf16[1024,1024]{1,0:T(8,128)(2,1)S(1)}, bf16[1024,1024]{1,0:T(8,128)(2,1)}, u32[]{:S(2)}, u32[]{:S(2)}) collective-permute-start(bf16[1024,1024]{1,0:T(8,128)(2,1)S(1)} %copy-done.21), channel_id=1, source_target_pairs={{1,2},{2,1},{5,6},{6,5},{9,10},{10,9},{13,14},{14,13},{17,18},{18,... | collective-permute-start | bytes 6291464 | tf_op jit(solution)/shard_map/ppermute | solution.py:609
  121.1 19.2 %shard_map.342 = (bf16[1024,256]{1,0:T(8,128)(2,1)}, bf16[1024,256]{1,0:T(8,128)(2,1)}, f32[32,2048]{1,0:T(8,128)}) custom-call(s32[4]{0:T(128)} %broadcast_select_fusion.10.place, bf16[2048,256]{1,0:T(8,128)(2,1)} %get-tuple-element.269.q_ref, bf16[2048,256]{1,0:T(8,128)(2,1)} %get-tuple-element.270.k_ref, bf16[2048,256]{1,0:T(8,128)(2,1)} %get-tuple-element.271.v_ref), custom_call_target="tpu_custom_call" | custom-call | tf_op jit(solution)/shard_map/pallas_call | solution.py:37
  144.4 8.0 %shard_map.343 = (bf16[2048,256]{1,0:T(8,128)(2,1)}, bf16[2048,256]{1,0:T(8,128)(2,1)}, bf16[2048,256]{1,0:T(8,128)(2,1)}) custom-call(bf16[2048,1024]{1,0:T(8,128)(2,1)} %get-tuple-element.280.a_ref, bf16[1024,768]{1,0:T(8,128)(2,1)} %bitcast.273, f32[2048,128]{1,0:T(8,128)} %pad_maximum_fusion.3.cos_ref, f32[2048,128]{1,0:T(8,128)} %pad_maximum_fusion.4.sin_ref), custom_call_target="tpu_custom_call" | custom-call | tf_op jit(solution)/shard_map/pallas_call | solution.py:37
  152.4 19.5 %shard_map.344 = (bf16[1024,256]{1,0:T(8,128)(2,1)}, bf16[1024,256]{1,0:T(8,128)(2,1)}, f32[32,2048]{1,0:T(8,128)}) custom-call(s32[4]{0:T(128)} %broadcast_select_fusion.10.place, bf16[2048,256]{1,0:T(8,128)(2,1)} %get-tuple-element.282.q_ref, bf16[2048,256]{1,0:T(8,128)(2,1)} %get-tuple-element.283.k_ref, bf16[2048,256]{1,0:T(8,128)(2,1)} %get-tuple-element.284.v_ref), custom_call_target="tpu_custom_call" | custom-call | tf_op jit(solution)/shard_map/pallas_call | solution.py:37
  177.7 9.3 %shard_map.345 = (f32[1024,1024]{1,0:T(8,128)}, f32[1024,1024]{1,0:T(8,128)}, bf16[1024,1024]{1,0:T(8,128)(2,1)}) custom-call(bf16[1024,256]{1,0:T(8,128)(2,1)} %get-tuple-element.279.m0_ref.own_ref, bf16[1024,256]{1,0:T(8,128)(2,1)} %get-tuple-element.288.m1_ref.own_ref, bf16[1024,256]{1,0:T(8,128)(2,1)} %collective-permute-done.17.o0_ref, ...), custom_call_target="tpu_custom_call" | custom-call | tf_op jit(solution)/shard_map/pallas_call | solution.py:37
  191.5 18.4 %shard_map.347 = (bf16[1024,2048]{1,0:T(8,128)(2,1)}, bf16[1024,2048]{1,0:T(8,128)(2,1)}, bf16[1024,1024]{1,0:T(8,128)(2,1)}) custom-call(bf16[1024,1024]{1,0:T(8,128)(2,1)} %collective-permute-done.20.c_ref, bf16[16,4,64,1024]{3,2,1,0:T(8,128)(2,1)} %bitcast.265, bf16[16,2,128,1024]{3,2,1,0:T(8,128)(2,1)} %bitcast.266), custom_call_target="tpu_custom_call" | custom-call | tf_op jit(solution)/shard_map/pallas_call | solution.py:37
  213.5 18.4 %shard_map.346 = (bf16[1024,2048]{1,0:T(8,128)(2,1)}, bf16[1024,2048]{1,0:T(8,128)(2,1)}, f32[1024,1024]{1,0:T(8,128)}) custom-call(bf16[1024,1024]{1,0:T(8,128)(2,1)} %get-tuple-element.291.c_ref, bf16[16,4,64,1024]{3,2,1,0:T(8,128)(2,1)} %bitcast.267, bf16[16,2,128,1024]{3,2,1,0:T(8,128)(2,1)} %bitcast.268), custom_call_target="tpu_custom_call" | custom-call | tf_op jit(solution)/shard_map/pallas_call | solution.py:37
  233.3 7.9 %shard_map.348 = (bf16[1024,1024]{1,0:T(8,128)(2,1)}, bf16[1024,1024]{1,0:T(8,128)(2,1)}, f32[2,1024]{1,0:T(2,128)}) custom-call(f32[1024,1024]{1,0:T(8,128)} %get-tuple-element.293.m_ref, bf16[1024,1024]{1,0:T(8,128)(2,1)} %copy-done.38, f32[1024,1024]{1,0:T(8,128)} %get-tuple-element.295.h_ref, bf16[1024,1024]{1,0:T(8,128)(2,1)} %broadcast_select_fusion.2.y_ref, ...), custom_call_target="tpu_custom_call" | custom-call | tf_op jit(solution)/shard_map/pallas_call | solution.py:37
  241.3 17.1 %shard_map.350 = (bf16[1024,2048]{1,0:T(8,128)(2,1)}, f32[1024,1024]{1,0:T(8,128)}) custom-call(bf16[1024,1024]{1,0:T(8,128)(2,1)} %get-tuple-element.298.dm_ref, bf16[1024,2048]{1,0:T(8,128)(2,1)} %get-tuple-element.302.s_ref, bf16[16,4,64,1024]{3,2,1,0:T(8,128)(2,1)} %bitcast.269, bf16[16,2,128,1024]{3,2,1,0:T(8,128)(2,1)} %bitcast.270), custom_call_target="tpu_custom_call" | custom-call | tf_op jit(solution)/shard_map/pallas_call | solution.py:37
  260.6 12.1 %fusion.19 = bf16[2048,1024]{1,0:T(8,128)(2,1)S(1)} fusion(bf16[1024,1024]{1,0:T(8,128)(2,1)} %collective-permute-done.22.dm_ref, bf16[1024,1024]{1,0:T(8,128)(2,1)S(1)} %copy-done.39, bf16[1024,2048]{1,0:T(8,128)(2,1)} %get-tuple-element.306, bf16[1024,2048]{1,0:T(8,128)(2,1)} %get-tuple-element.305), kind=kOutput, calls=%fused_computation.19 | convolution fusion | flops 8617197568 | bytes 16777216 | tf_op jit(solution)/shard_map/dot_general | solution.py:33
  275.4 15.5 %shard_map.349 = (bf16[1024,2048]{1,0:T(8,128)(2,1)}, bf16[1024,1024]{1,0:T(8,128)(2,1)}) custom-call(bf16[1024,1024]{1,0:T(8,128)(2,1)} %collective-permute-done.22.dm_ref, bf16[1024,2048]{1,0:T(8,128)(2,1)} %get-tuple-element.299.s_ref, bf16[16,4,64,1024]{3,2,1,0:T(8,128)(2,1)} %bitcast.271, bf16[16,2,128,1024]{3,2,1,0:T(8,128)(2,1)} %bitcast.272), custom_call_target="tpu_custom_call" | custom-call | tf_op jit(solution)/shard_map/pallas_call | solution.py:37
  292.5 12.3 %fusion.14 = bf16[1024,2048]{1,0:T(8,128)(2,1)S(1)} fusion(bf16[1024,2048]{1,0:T(8,128)(2,1)} %get-tuple-element.312, bf16[1024,2048]{1,0:T(8,128)(2,1)} %get-tuple-element.311, bf16[1024,1024]{1,0:T(8,128)(2,1)} %collective-permute-done.20.c_ref, bf16[1024,1024]{1,0:T(8,128)(2,1)S(1)} %copy-done.25), kind=kOutput, calls=%fused_computation.18 | convolution fusion | flops 8617197568 | bytes 16777216 | tf_op jit(solution)/shard_map/dot_general | solution.py:33
  308.8 13.1 %shard_map.351 = (f32[1024,1024]{1,0:T(8,128)}, bf16[1024,1024]{1,0:T(8,128)(2,1)}, f32[2,1024]{1,0:T(2,128)}, f32[2,1024]{1,0:T(2,128)}) custom-call(f32[1024,1024]{1,0:T(8,128)} %get-tuple-element.314.dc_ref, bf16[1024,1024]{1,0:T(8,128)(2,1)} %collective-permute-done.26.r_ref, f32[1024,1024]{1,0:T(8,128)} %get-tuple-element.295.h_ref, ...), custom_call_target="tpu_custom_call" | custom-call | tf_op jit(solution)/shard_map/pallas_call | solution.py:37
  340.5 16.5 %shard_map.352 = (bf16[2048,128]{1,0:T(8,128)(2,1)}, bf16[2048,128]{1,0:T(8,128)(2,1)}, bf16[2048,128]{1,0:T(8,128)(2,1)}) custom-call(s32[4]{0:T(128)} %broadcast_select_fusion.10.place, bf16[2048,256]{1,0:T(8,128)(2,1)} %get-tuple-element.269.q_ref, bf16[2048,256]{1,0:T(8,128)(2,1)} %get-tuple-element.270.k_ref, ...), custom_call_target="tpu_custom_call" | custom-call | tf_op jit(solution)/shard_map/pallas_call | solution.py:37
  361.1 16.6 %shard_map.353 = (bf16[2048,128]{1,0:T(8,128)(2,1)}, bf16[2048,128]{1,0:T(8,128)(2,1)}, bf16[2048,128]{1,0:T(8,128)(2,1)}) custom-call(s32[4]{0:T(128)} %broadcast_select_fusion.10.place, bf16[2048,256]{1,0:T(8,128)(2,1)} %get-tuple-element.269.q_ref, bf16[2048,256]{1,0:T(8,128)(2,1)} %get-tuple-element.270.k_ref, ...), custom_call_target="tpu_custom_call" | custom-call | tf_op jit(solution)/shard_map/pallas_call | solution.py:37
  395.9 16.8 %shard_map.354 = (bf16[2048,128]{1,0:T(8,128)(2,1)}, bf16[2048,128]{1,0:T(8,128)(2,1)}, bf16[2048,128]{1,0:T(8,128)(2,1)}) custom-call(s32[4]{0:T(128)} %broadcast_select_fusion.10.place, bf16[2048,256]{1,0:T(8,128)(2,1)} %get-tuple-element.282.q_ref, bf16[2048,256]{1,0:T(8,128)(2,1)} %get-tuple-element.283.k_ref, ...), custom_call_target="tpu_custom_call" | custom-call | tf_op jit(solution)/shard_map/pallas_call | solution.py:37
  421.0 16.5 %shard_map.355 = (bf16[2048,128]{1,0:T(8,128)(2,1)}, bf16[2048,128]{1,0:T(8,128)(2,1)}, bf16[2048,128]{1,0:T(8,128)(2,1)}) custom-call(s32[4]{0:T(128)} %broadcast_select_fusion.10.place, bf16[2048,256]{1,0:T(8,128)(2,1)} %get-tuple-element.282.q_ref, bf16[2048,256]{1,0:T(8,128)(2,1)} %get-tuple-element.283.k_ref, ...), custom_call_target="tpu_custom_call" | custom-call | tf_op jit(solution)/shard_map/pallas_call | solution.py:37
  437.7 6.4 %collective-permute-done.42 = bf16[2,2,2,32,1280]{4,3,2,1,0:T(8,128)(2,1)} collective-permute-done((bf16[2,2,2,32,1280]{4,3,2,1,0:T(8,128)(2,1)}, bf16[2,2,2,32,1280]{4,3,2,1,0:T(8,128)(2,1)}, u32[]{:S(2)}, u32[]{:S(2)}) %collective-permute-start.42) | collective-permute-done | bytes 655392 | tf_op jit(solution)/shard_map/ppermute | solution.py:603
  457.4 7.7 %shard_map.356 = bf16[1024,1024]{1,0:T(8,128)(2,1)} custom-call(s32[4]{0:T(128)} %broadcast_select_fusion.11.inverse, bf16[2048,768]{1,0:T(8,128)(2,1)} %copy-done.2, bf16[2048,768]{1,0:T(8,128)(2,1)} %copy-done.3, bf16[1024,768]{1,0:T(8,128)(2,1)} %bitcast.279, bf16[1024,768]{1,0:T(8,128)(2,1)} %bitcast.274), custom_call_target="tpu_custom_call" | custom-call | tf_op jit(solution)/shard_map/pallas_call | solution.py:37
  480.0 11.6 %shard_map.357 = (bf16[1024,1024]{1,0:T(8,128)(2,1)}, f32[2,1024]{1,0:T(2,128)}) custom-call(s32[4]{0:T(128)} %broadcast_select_fusion.11.inverse, bf16[2048,768]{1,0:T(8,128)(2,1)} %copy-done.2, bf16[2048,768]{1,0:T(8,128)(2,1)} %copy-done.3, bf16[1024,768]{1,0:T(8,128)(2,1)} %bitcast.280, bf16[1024,768]{1,0:T(8,128)(2,1)} %bitcast.275, ...), custom_call_target="tpu_custom_call" | custom-call | tf_op jit(solution)/shard_map/pallas_call | solution.py:37
  (450 shorter events, 229.8 us)
Async XLA Ops:
  7.2 184.3 %all-gather.3.cloned.1.call-start = ((), (), s32[]{:S(2)}) async-start(), calls=%async_computation.1 | async-start | bytes 8912896 | tf_op jit(solution)/shard_map/all_gather | solution.py:731
  7.3 28.6 %collective-permute-start.6 = (bf16[1024,1024]{1,0:T(8,128)(2,1)}, bf16[1024,1024]{1,0:T(8,128)(2,1)S(1)}, u32[]{:S(2)}, u32[]{:S(2)}) collective-permute-start(bf16[1024,1024]{1,0:T(8,128)(2,1)} %param.22), channel_id=1, source_target_pairs={{1,2},{2,1},{5,6},{6,5},{9,10},{10,9},{13,14},{14,13},{17,18},{18,... | collective-permute-start | bytes 6291464 | tf_op jit(solution)/shard_map/ppermute | solution.py:609
  39.4 24.9 %collective-permute-start.12 = (bf16[1024,1024]{1,0:T(8,128)(2,1)S(1)}, bf16[1024,1024]{1,0:T(8,128)(2,1)}, u32[]{:S(2)}, u32[]{:S(2)}) collective-permute-start(bf16[1024,1024]{1,0:T(8,128)(2,1)S(1)} %broadcast_select_fusion.3.own_ref.x_ref), channel_id=1, source_target_pairs={{0,2},{1,3},{2,0},{3,1},{4,6},{5,7},{6,4},{7,5},{8,10},{9,11},{10,... | collective-permute-start | bytes 6291464 | tf_op jit(solution)/shard_map/ppermute | solution.py:603
  64.7 26.1 %collective-permute-start.13 = (bf16[2,2,2,72,768]{4,3,1,0,2:T(8,128)(2,1)S(1)}, bf16[2,2,2,72,768]{4,3,1,0,2:T(8,128)(2,1)S(1)}, u32[]{:S(2)}, u32[]{:S(2)}) collective-permute-start(bf16[2,2,2,72,768]{4,3,1,0,2:T(8,128)(2,1)S(1)} %pad_maximum_fusion.6), channel_id=1, source_target_pairs={{0,4},{1,5},{2,6},{3,7},{4,0},{5,1},{6,2},{7,3},{8,12},{9,13},{10,... | collective-permute-start | bytes 2654216 | tf_op jit(solution)/shard_map/ppermute | solution.py:603
  91.5 48.9 %collective-permute-start.15 = (bf16[2,2,2,2,32,1280]{5,4,2,1,0,3:T(8,128)(2,1)S(1)}, bf16[2,2,2,2,32,1280]{5,4,2,1,0,3:T(8,128)(2,1)S(1)}, u32[]{:S(2)}, u32[]{:S(2)}) collective-permute-start(bf16[2,2,2,2,32,1280]{5,4,2,1,0,3:T(8,128)(2,1)S(1)} %pad_maximum_fusion.2), channel_id=1, source_target_pairs={{0,4},{1,5},{2,6},{3,7},{4,0},{5,1},{6,2},{7,3},{8,12},{9,13},{10,... | collective-permute-start | bytes 3932168 | tf_op jit(solution)/shard_map/ppermute | solution.py:603
  108.3 66.8 %collective-permute-start.16 = (bf16[1024,1024]{1,0:T(8,128)(2,1)S(1)}, bf16[1024,1024]{1,0:T(8,128)(2,1)}, u32[]{:S(2)}, u32[]{:S(2)}) collective-permute-start(bf16[1024,1024]{1,0:T(8,128)(2,1)S(1)} %copy-done.21), channel_id=1, source_target_pairs={{1,2},{2,1},{5,6},{6,5},{9,10},{10,9},{13,14},{14,13},{17,18},{18,... | collective-permute-start | bytes 6291464 | tf_op jit(solution)/shard_map/ppermute | solution.py:609
  142.5 35.1 %collective-permute-start.19 = (bf16[512,1024]{1,0:T(8,128)(2,1)S(1)}, bf16[512,1024]{1,0:T(8,128)(2,1)}, u32[]{:S(2)}, u32[]{:S(2)}) collective-permute-start(bf16[512,1024]{1,0:T(8,128)(2,1)S(1)} %bitcast.294), channel_id=1, source_target_pairs={{0,2},{1,3},{2,0},{3,1},{4,6},{5,7},{6,4},{7,5},{8,10},{9,11},{10,... | collective-permute-start | bytes 3145736 | tf_op jit(solution)/shard_map/ppermute | solution.py:603
  144.1 33.6 %collective-permute-start.17 = (bf16[1024,256]{1,0:T(8,128)(2,1)S(1)}, bf16[1024,256]{1,0:T(8,128)(2,1)}, u32[]{:S(2)}, u32[]{:S(2)}) collective-permute-start(bf16[1024,256]{1,0:T(8,128)(2,1)S(1)} %copy-done.28), channel_id=1, source_target_pairs={{0,2},{1,3},{2,0},{3,1},{4,6},{5,7},{6,4},{7,5},{8,10},{9,11},{10,... | collective-permute-start | bytes 1572872 | tf_op jit(solution)/shard_map/ppermute | solution.py:603
  258.4 32.5 %collective-permute-start.23 = (bf16[1024,1024]{1,0:T(8,128)(2,1)}, bf16[1024,1024]{1,0:T(8,128)(2,1)}, u32[]{:S(2)}, u32[]{:S(2)}) collective-permute-start(bf16[1024,1024]{1,0:T(8,128)(2,1)} %get-tuple-element.297), channel_id=1, source_target_pairs={{1,2},{2,1},{5,6},{6,5},{9,10},{10,9},{13,14},{14,13},{17,18},{18,... | collective-permute-start | bytes 6291464 | tf_op jit(solution)/shard_map/ppermute | solution.py:609
  291.2 30.7 %collective-permute-start.24 = (bf16[2,2,2,128,512]{4,3,0,1,2:T(8,128)(2,1)}, bf16[2,2,2,128,512]{4,3,0,1,2:T(8,128)(2,1)S(1)}, u32[]{:S(2)}, u32[]{:S(2)}) collective-permute-start(bf16[2,2,2,128,512]{4,3,0,1,2:T(8,128)(2,1)} %bitcast.304), channel_id=1, source_target_pairs={{0,4},{1,5},{2,6},{3,7},{4,0},{5,1},{6,2},{7,3},{8,12},{9,13},{10,... | collective-permute-start | bytes 3145736 | tf_op jit(solution)/shard_map/ppermute | solution.py:603
  292.0 29.8 %collective-permute-start.25 = (bf16[2,2,2,128,512]{4,3,0,1,2:T(8,128)(2,1)}, bf16[2,2,2,128,512]{4,3,0,1,2:T(8,128)(2,1)}, u32[]{:S(2)}, u32[]{:S(2)}) collective-permute-start(bf16[2,2,2,128,512]{4,3,0,1,2:T(8,128)(2,1)} %bitcast.303), channel_id=1, source_target_pairs={{0,1},{1,0},{2,3},{3,2},{4,5},{5,4},{6,7},{7,6},{8,9},{9,8},{10,11... | collective-permute-start | bytes 3145736 | tf_op jit(solution)/shard_map/ppermute | solution.py:603
  327.4 29.7 %collective-permute-start.27 = (bf16[2,2,128,512]{3,2,0,1:T(8,128)(2,1)}, bf16[2,2,128,512]{3,2,0,1:T(8,128)(2,1)S(1)}, u32[]{:S(2)}, u32[]{:S(2)}) collective-permute-start(bf16[2,2,128,512]{3,2,0,1:T(8,128)(2,1)} %dynamic-slice_bitcast_fusion.4), channel_id=1, source_target_pairs={{0,1},{1,0},{2,3},{3,2},{4,5},{5,4},{6,7},{7,6},{8,9},{9,8},{10,11... | collective-permute-start | bytes 1572872 | tf_op jit(solution)/shard_map/ppermute | solution.py:603
  328.7 28.4 %collective-permute-start.28 = (bf16[2,2,128,512]{3,2,0,1:T(8,128)(2,1)}, bf16[2,2,128,512]{3,2,0,1:T(8,128)(2,1)S(1)}, u32[]{:S(2)}, u32[]{:S(2)}) collective-permute-start(bf16[2,2,128,512]{3,2,0,1:T(8,128)(2,1)} %dynamic-slice_bitcast_fusion.3), channel_id=1, source_target_pairs={{0,4},{1,5},{2,6},{3,7},{4,0},{5,1},{6,2},{7,3},{8,12},{9,13},{10,... | collective-permute-start | bytes 1572872 | tf_op jit(solution)/shard_map/ppermute | solution.py:603
  329.1 48.7 %collective-permute-start.32 = (bf16[2,2,2,64,1024]{4,3,0,1,2:T(8,128)(2,1)}, bf16[2,2,2,64,1024]{4,3,0,1,2:T(8,128)(2,1)}, u32[]{:S(2)}, u32[]{:S(2)}) collective-permute-start(bf16[2,2,2,64,1024]{4,3,0,1,2:T(8,128)(2,1)} %bitcast.302), channel_id=1, source_target_pairs={{0,4},{1,5},{2,6},{3,7},{4,0},{5,1},{6,2},{7,3},{8,12},{9,13},{10,... | collective-permute-start | bytes 3145736 | tf_op jit(solution)/shard_map/ppermute | solution.py:603
  330.1 47.7 %collective-permute-start.33 = (bf16[2,2,2,64,1024]{4,3,2,1,0:T(8,128)(2,1)}, bf16[2,2,2,64,1024]{4,3,2,1,0:T(8,128)(2,1)}, u32[]{:S(2)}, u32[]{:S(2)}) collective-permute-start(bf16[2,2,2,64,1024]{4,3,2,1,0:T(8,128)(2,1)} %dynamic-slice_bitcast_fusion), channel_id=1, source_target_pairs={{0,1},{1,0},{2,3},{3,2},{4,5},{5,4},{6,7},{7,6},{8,9},{9,8},{10,11... | collective-permute-start | bytes 3145736 | tf_op jit(solution)/shard_map/ppermute | solution.py:603
  384.8 27.9 %collective-permute-start.36 = (bf16[2,2,64,1024]{3,2,0,1:T(8,128)(2,1)S(1)}, bf16[2,2,64,1024]{3,2,0,1:T(8,128)(2,1)S(1)}, u32[]{:S(2)}, u32[]{:S(2)}) collective-permute-start(bf16[2,2,64,1024]{3,2,0,1:T(8,128)(2,1)S(1)} %dynamic-slice_bitcast_fusion.2), channel_id=1, source_target_pairs={{0,1},{1,0},{2,3},{3,2},{4,5},{5,4},{6,7},{7,6},{8,9},{9,8},{10,11... | collective-permute-start | bytes 1572872 | tf_op jit(solution)/shard_map/ppermute | solution.py:603
  386.2 26.5 %collective-permute-start.37 = (bf16[2,2,64,1024]{3,2,1,0:T(8,128)(2,1)S(1)}, bf16[2,2,64,1024]{3,2,1,0:T(8,128)(2,1)S(1)}, u32[]{:S(2)}, u32[]{:S(2)}) collective-permute-start(bf16[2,2,64,1024]{3,2,1,0:T(8,128)(2,1)S(1)} %dynamic-slice_bitcast_fusion.1), channel_id=1, source_target_pairs={{0,4},{1,5},{2,6},{3,7},{4,0},{5,1},{6,2},{7,3},{8,12},{9,13},{10,... | collective-permute-start | bytes 1572872 | tf_op jit(solution)/shard_map/ppermute | solution.py:603
  386.6 26.0 %collective-permute-start.34 = (bf16[128,512]{1,0:T(8,128)(2,1)S(1)}, bf16[128,512]{1,0:T(8,128)(2,1)S(1)}, u32[]{:S(2)}, u32[]{:S(2)}) collective-permute-start(bf16[128,512]{1,0:T(8,128)(2,1)S(1)} %dynamic-slice_bitcast_fusion.20), channel_id=1, source_target_pairs={{0,16},{1,17},{2,18},{3,19},{4,20},{5,21},{6,22},{7,23},{8,24},{9,... | collective-permute-start | bytes 393224 | tf_op jit(solution)/shard_map/ppermute | solution.py:603
  416.6 27.5 %collective-permute-start.42 = (bf16[2,2,2,32,1280]{4,3,2,1,0:T(8,128)(2,1)}, bf16[2,2,2,32,1280]{4,3,2,1,0:T(8,128)(2,1)}, u32[]{:S(2)}, u32[]{:S(2)}) collective-permute-start(bf16[2,2,2,32,1280]{4,3,2,1,0:T(8,128)(2,1)} %get-tuple-element.379), channel_id=1, source_target_pairs={{0,5},{1,4},{2,7},{3,6},{4,1},{5,0},{6,3},{7,2},{8,13},{9,12},{10,... | collective-permute-start | bytes 1966088 | tf_op jit(solution)/shard_map/ppermute | solution.py:603
  473.1 28.7 %collective-permute-start.46 = (bf16[2,32,1280]{2,1,0:T(8,128)(2,1)}, bf16[2,32,1280]{2,1,0:T(8,128)(2,1)}, u32[]{:S(2)}, u32[]{:S(2)}) collective-permute-start(bf16[2,32,1280]{2,1,0:T(8,128)(2,1)} %get-tuple-element.402), channel_id=1, source_target_pairs={{0,16},{1,17},{2,18},{3,19},{4,20},{5,21},{6,22},{7,23},{8,24},{9,... | collective-permute-start | bytes 491528 | tf_op jit(solution)/shard_map/ppermute | solution.py:603
  475.5 24.8 %collective-permute-start.45 = (bf16[64,1024]{1,0:T(8,128)(2,1)}, bf16[64,1024]{1,0:T(8,128)(2,1)}, u32[]{:S(2)}, u32[]{:S(2)}) collective-permute-start(bf16[64,1024]{1,0:T(8,128)(2,1)} %dynamic-slice_bitcast_fusion.17), channel_id=1, source_target_pairs={{0,16},{1,17},{2,18},{3,19},{4,20},{5,21},{6,22},{7,23},{8,24},{9,... | collective-permute-start | bytes 393224 | tf_op jit(solution)/shard_map/ppermute | solution.py:603
  478.4 34.3 %collective-permute-start.49 = (bf16[2,2,2,32,768]{4,3,2,1,0:T(8,128)(2,1)}, bf16[2,2,2,32,768]{4,3,2,1,0:T(8,128)(2,1)}, u32[]{:S(2)}, u32[]{:S(2)}) collective-permute-start(bf16[2,2,2,32,768]{4,3,2,1,0:T(8,128)(2,1)} %get-tuple-element.405), channel_id=1, source_target_pairs={{0,1},{1,0},{2,3},{3,2},{4,5},{5,4},{6,7},{7,6},{8,9},{9,8},{10,11... | collective-permute-start | bytes 1179656 | tf_op jit(solution)/shard_map/ppermute | solution.py:603
  478.7 34.0 %collective-permute-start.50 = (bf16[2,2,2,32,768]{4,3,2,1,0:T(8,128)(2,1)}, bf16[2,2,2,32,768]{4,3,2,1,0:T(8,128)(2,1)}, u32[]{:S(2)}, u32[]{:S(2)}) collective-permute-start(bf16[2,2,2,32,768]{4,3,2,1,0:T(8,128)(2,1)} %get-tuple-element.406), channel_id=1, source_target_pairs={{0,4},{1,5},{2,6},{3,7},{4,0},{5,1},{6,2},{7,3},{8,12},{9,13},{10,... | collective-permute-start | bytes 1179656 | tf_op jit(solution)/shard_map/ppermute | solution.py:603
  509.3 38.8 %collective-permute-start.57 = (bf16[1024,1024]{1,0:T(8,128)(2,1)S(1)}, bf16[1024,1024]{1,0:T(8,128)(2,1)}, u32[]{:S(2)}, u32[]{:S(2)}) collective-permute-start(bf16[1024,1024]{1,0:T(8,128)(2,1)S(1)} %copy-done.23), channel_id=1, source_target_pairs={{1,2},{2,1},{5,6},{6,5},{9,10},{10,9},{13,14},{14,13},{17,18},{18,... | collective-permute-start | bytes 6291464 | tf_op jit(solution)/shard_map/ppermute | solution.py:609
  (118 other events, 1098.4 us)
Sparse Core Ops, SparseCore 0:
  37.6 148.8 all-gather.2
